TPU v7x, 128 devices: a whole 4x4x4 slice. The times are simulated.
128 devices in a mesh: ctx: 16 (over y, z_hi, core), head: 8 (over x, z_lo).
Axes of the slice: x: 4, y: 4, z: 4 (z_hi: 2, z_lo: 2; z = z_hi * 2 + z_lo), core: 2. Of those that a mesh axis runs over, the one named last changes fastest.
Arguments:
- queries: bfloat16 [2048, 12288], P('ctx', 'head'), may hold values from -8 to 8
- latents: bfloat16 [2048, 512], P('ctx'), may hold values from -4 to 4
- rope_key: bfloat16 [2048, 64], P('ctx'), may hold values from -8 to 8
- up_key_weight: bfloat16 [512, 8192], P(None, 'head'), may hold values from -0.5 to 0.5
- up_value_weight: bfloat16 [512, 8192], P(None, 'head'), may hold values from -0.25 to 0.25
- out_grad: bfloat16 [2048, 8192], P('ctx', 'head'), may hold values from -6 to 6
- group_order: int32 [32], replicated, may hold values from 0 to 31, as said below
Outputs:
- query_grad: bfloat16 [2048, 12288], P('ctx', 'head')
- latent_grad: float32 [2048, 512], P('ctx')
- rope_grad: float32 [2048, 64], P('ctx')
- up_key_grad: float32 [512, 8192], P('ctx', 'head')
- up_value_grad: float32 [512, 8192], P('ctx', 'head')
Inputs may be any that keep to these rules, and one draw needn't show every extreme that they name: A permutation of the 32 group numbers; storage slot k (rows k * 64 to k * 64 + 63) holds the sequence positions group_order[k] * 64 on, in order.
All inputs are finite; a program needn't handle non-finite values.
Results may differ from a plain program's by a relative error of at most 0.017.
Values may be sent and summed in bfloat16 or wider, within the bound.
No kernel may reach another device: no remote copies, remote signals or barrier semaphores. Data moves between devices by JAX's collectives and lax.ppermute only.
A program may use at most 64 MiB of HBM per device.

v0:
```python
import math

import jax
import jax.numpy as jnp
from jax import lax
from jax.experimental import pallas as pl
from jax.experimental.pallas import tpu as pltpu
from jax.sharding import PartitionSpec as P


D_LATENT = 512
ROPE = 64
NOPE = 128
VDIM = 128
WIDTH = D_LATENT + ROPE
GROUP = 64
NEG_FILL = -1e30
SCALE = (NOPE + ROPE) ** -0.5
SCALE_LOG2 = SCALE * math.log2(math.e)

CTX = 16
HEAD = 8
BF16 = jnp.bfloat16
F32 = jnp.float32


def ctx_xor(position):
    core, y_bits, zhi = position >> 3, (position >> 1) & 3, position & 1
    return (y_bits << 2) | (zhi << 1) | core


def swap_ctx(value, mask):
    return lax.ppermute(value, "ctx", [(i, i ^ mask) for i in range(CTX)])


def swap_head(value, mask):
    return lax.ppermute(value, "head", [(i, i ^ mask) for i in range(HEAD)])


def dot(a, b, dims):
    return lax.dot_general(a, b, (dims, ((), ())), preferred_element_type=F32)


NT = ((1,), (1,))
NN = ((1,), (0,))
TN = ((0,), (0,))

BLOCK = 256
BLOCKS = 8
PAIRS = 4
CHUNK = 128
ROPE_ROWS = 16
PACKED = CHUNK + ROPE_ROWS
LANES = 128


def load_keys(k_refs, keys, ropes, sems):
    copies = []
    for b in range(BLOCKS):
        for c in range(2):
            chunk = 2 * b + c
            rows = slice(chunk * CHUNK, (chunk + 1) * CHUNK)
            top = c * PACKED
            copies.append(pltpu.make_async_copy(k_refs[b].at[top : top + CHUNK], keys.at[rows, :D_LATENT], sems.at[0, chunk]))
            copies.append(pltpu.make_async_copy(k_refs[b].at[top + CHUNK : top + PACKED], ropes.at[chunk], sems.at[1, chunk]))
    for copy in copies:
        copy.start()
    for copy in copies:
        copy.wait()


def rope_rows(packed):
    return jnp.concatenate([packed[:, g * LANES : (g + 1) * LANES] for g in range(ROPE // ROPE_ROWS)], axis=0)


def prep_kernel(own_ref, order_ref, query_ref, up_key_ref, out_grad_ref, up_value_ref, q_ref, gl_ref, bias_ref):
    queries = query_ref[...]
    step = pl.program_id(0)
    for h in range(2):
        first = h * (NOPE + ROPE)
        cols = slice(h * NOPE, (h + 1) * NOPE)
        rows = slice(h * CHUNK, (h + 1) * CHUNK)
        q_ref[0, rows, :D_LATENT] = dot(queries[:, first : first + NOPE], up_key_ref[:, cols], NT).astype(BF16)
        q_ref[0, rows, D_LATENT:] = queries[:, first + NOPE : first + NOPE + ROPE]
        gl_ref[0, rows, :] = dot(out_grad_ref[:, cols], up_value_ref[:, cols], NT).astype(BF16)
    own = own_ref[0]
    lane = lax.broadcasted_iota(jnp.int32, (GROUP, CHUNK), 1)
    row = lax.broadcasted_iota(jnp.int32, (GROUP, CHUNK), 0)
    query_pos = jnp.where(lane < GROUP, order_ref[2 * own] * GROUP, order_ref[2 * own + 1] * GROUP - GROUP) + lane
    for c in range(CTX // PAIRS):
        position = step * (CTX // PAIRS) + c
        core, y_bits, zhi = position >> 3, (position >> 1) & 3, position & 1
        device = own ^ ((y_bits << 2) | (zhi << 1) | core)
        for g in range(2):
            key_pos = order_ref[2 * device + g] * GROUP + row
            first = c * CHUNK + g * GROUP
            bias_ref[first : first + GROUP, :] = jnp.where(key_pos <= query_pos, 0.0, NEG_FILL).astype(F32)


def latent_rows(probs, grads, q_ref, gl_ref):
    query = q_ref[...].reshape(PAIRS * 2 * CHUNK, WIDTH)
    grad_lat = gl_ref[...].reshape(PAIRS * 2 * CHUNK, D_LATENT)
    both = dot(grads, query, NN)
    return both[:, :D_LATENT] + dot(probs, grad_lat, NN), both[:, D_LATENT:]


def store_latents(out_ref, latent, rope):
    for c in range(latent.shape[0] // CHUNK):
        rows = slice(c * CHUNK, (c + 1) * CHUNK)
        top = c * PACKED
        out_ref[top : top + CHUNK, :] = latent[rows].astype(BF16)
        turned = rope[rows].T
        packed = [turned[g * ROPE_ROWS : (g + 1) * ROPE_ROWS] for g in range(ROPE // ROPE_ROWS)]
        out_ref[top + CHUNK : top + PACKED, :] = jnp.concatenate(packed, axis=1).astype(BF16)


def scores_kernel(*refs):
    k_refs = refs[:BLOCKS]
    q_ref, gl_ref, bias_ref = refs[BLOCKS : BLOCKS + 3]
    probs, grads, send_ref = refs[BLOCKS + 3 : BLOCKS + 6]
    keys, ropes, e_ref, g_ref, key_sems = refs[BLOCKS + 6 :]
    step = pl.program_id(0)

    @pl.when(step == 0)
    def _():
        load_keys(k_refs, keys, ropes, key_sems)
        for chunk in range(CTX):
            keys[chunk * CHUNK : (chunk + 1) * CHUNK, D_LATENT:] = rope_rows(ropes[chunk]).T

    @pl.when(step < PAIRS)
    def _():
        q = q_ref[step]
        gl = gl_ref[step]
        run_max, run_sum, run_dot = None, None, None
        maxes = []
        for kb in range(BLOCKS):
            rows = slice(kb * BLOCK, (kb + 1) * BLOCK)
            block = keys[rows, :]
            s = dot(block, q, NT)
            g = dot(block[:, :D_LATENT], gl, NT)
            bias = bias_ref[rows, :]
            s = s * SCALE_LOG2 + jnp.concatenate([bias, bias], axis=1)
            top = jnp.max(s, axis=0, keepdims=True)
            if kb > 0:
                top = jnp.maximum(run_max, top)
            e = jnp.exp2(s - top)
            part = jnp.sum(e, axis=0, keepdims=True)
            part_dot = jnp.sum(e * g, axis=0, keepdims=True)
            if kb > 0:
                shrink = jnp.exp2(run_max - top)
                part = run_sum * shrink + part
                part_dot = run_dot * shrink + part_dot
            run_max, run_sum, run_dot = top, part, part_dot
            maxes.append(top)
            e_ref[rows, :] = e
            g_ref[rows, :] = g
        inverse = 1.0 / run_sum
        delta = run_dot * inverse
        for kb in range(BLOCKS):
            rows = slice(kb * BLOCK, (kb + 1) * BLOCK)
            factor = jnp.exp2(maxes[kb] - run_max) * inverse
            p = e_ref[rows, :] * factor
            probs[step, rows, :] = p.astype(BF16)
            grads[step, rows, :] = (p * (g_ref[rows, :] - delta) * SCALE).astype(BF16)

    @pl.when(step == PAIRS)
    def _():
        rows = slice((BLOCKS // 2) * BLOCK, BLOCKS * BLOCK)
        both = [jnp.concatenate([ref[i, rows, :] for i in range(PAIRS)], axis=1) for ref in (probs, grads)]
        store_latents(send_ref, *latent_rows(*both, q_ref, gl_ref))


def keep_kernel(probs_ref, grads_ref, q_ref, gl_ref, keep_ref):
    rows = slice(0, (BLOCKS // 2) * BLOCK)
    both = [jnp.concatenate([ref[i, rows, :] for i in range(PAIRS)], axis=1) for ref in (probs_ref, grads_ref)]
    store_latents(keep_ref, *latent_rows(*both, q_ref, gl_ref))


def weights_kernel(*refs):
    own_ref = refs[0]
    k_refs = refs[1 : BLOCKS + 1]
    probs_ref, grads_ref, query_ref, out_grad_ref, up_key_ref = refs[BLOCKS + 1 : BLOCKS + 6]
    query_grad_ref, send_ref, keep_ref = refs[BLOCKS + 6 : BLOCKS + 9]
    keys, ropes, kt_ref, w_ref, key_sems = refs[BLOCKS + 9 :]

    @pl.when(pl.program_id(0) == 0)
    def _():
        load_keys(k_refs, keys, ropes, key_sems)
        for chunk in range(CTX):
            cols = slice(chunk * CHUNK, (chunk + 1) * CHUNK)
            kt_ref[:D_LATENT, cols] = keys[cols, :].T
            kt_ref[D_LATENT:, cols] = rope_rows(ropes[chunk])

    step = pl.program_id(0)
    out_t = dot(kt_ref[:D_LATENT, :], probs_ref[step], NN).astype(BF16)
    abs_t = dot(kt_ref[...], grads_ref[step], NN)
    rope_t = abs_t[D_LATENT:, :]
    abs_t = abs_t[:D_LATENT, :].astype(BF16)
    queries = query_ref[...]
    pieces = []
    for h in range(2):
        cols = slice(h * NOPE, (h + 1) * NOPE)
        first = h * (NOPE + ROPE)
        nope = queries[:, first : first + NOPE]
        w_ref[0, :, cols] = dot(abs_t[:, cols], nope, NN).astype(BF16)
        w_ref[1, :, cols] = dot(out_t[:, cols], out_grad_ref[:, cols], NN).astype(BF16)
        pieces.append(dot(abs_t[:, cols], up_key_ref[:, cols], TN))
        pieces.append(rope_t[:, cols].T)
    query_grad_ref[...] = jnp.concatenate(pieces, axis=1).astype(BF16)
    own = own_ref[0]
    share = D_LATENT // CTX
    for position in range(CTX):
        rows = pl.ds(pl.multiple_of((own ^ ctx_xor(position)) * share, share), share)
        out = send_ref if position >= CTX // 2 else keep_ref
        out[position % (CTX // 2), 0] = w_ref[0, rows, :]
        out[position % (CTX // 2), 1] = w_ref[1, rows, :]


def spread_sum(parts):
    total = parts[0].astype(F32)
    for part in parts[1:]:
        total = total + part.astype(F32)
    return total


def in_hbm(*arrays):
    return [pltpu.with_memory_space_constraint(a, pltpu.HBM) for a in arrays]


def in_vmem(*arrays):
    return [pltpu.with_memory_space_constraint(a, pltpu.VMEM) for a in arrays]


def cost(flops, moved):
    return pl.CostEstimate(flops=flops, transcendentals=0, bytes_accessed=moved)


def per_device(queries, latents, rope_key, up_key_weight, up_value_weight, out_grad, group_order):
    tok = queries.shape[0]
    heads = up_key_weight.shape[1] // NOPE
    own = lax.axis_index("ctx").astype(jnp.int32)
    vmem = pl.BlockSpec(memory_space=pltpu.VMEM)
    smem = pl.BlockSpec(memory_space=pltpu.SMEM)
    hbm = pl.BlockSpec(memory_space=pl.ANY)
    total = BLOCKS * BLOCK
    half = (CTX // 2) * PACKED
    pair_cols = 2 * (NOPE + ROPE)
    rope_parts = ROPE // ROPE_ROWS

    turned = rope_key.T
    packed = jnp.concatenate([turned[g * ROPE_ROWS : (g + 1) * ROPE_ROWS] for g in range(rope_parts)], axis=1)
    keys = jnp.concatenate([latents, packed], axis=0)
    got = swap_ctx(keys, 2)
    keys = jnp.concatenate([keys, got], axis=0)
    near = [keys]
    for k in (2, 1, 3):
        near.append(swap_ctx(keys, k << 2))
    near = [near[0], near[2], near[1], near[3]]
    far = []
    for k in range(4):
        far.append(swap_ctx(near[k], 1))
    k_blocks = near + far

    query_all, grad_lat, bias = pl.pallas_call(
        prep_kernel,
        grid=(PAIRS,),
        out_shape=(
            jax.ShapeDtypeStruct((PAIRS, 2 * tok, WIDTH), BF16),
            jax.ShapeDtypeStruct((PAIRS, 2 * tok, D_LATENT), BF16),
            jax.ShapeDtypeStruct((total, tok), F32),
        ),
        in_specs=[
            smem,
            smem,
            pl.BlockSpec((tok, pair_cols), lambda i: (0, i)),
            pl.BlockSpec((D_LATENT, 2 * NOPE), lambda i: (0, i)),
            pl.BlockSpec((tok, 2 * VDIM), lambda i: (0, i)),
            pl.BlockSpec((D_LATENT, 2 * VDIM), lambda i: (0, i)),
        ],
        out_specs=(
            pl.BlockSpec((1, 2 * tok, WIDTH), lambda i: (i, 0, 0)),
            pl.BlockSpec((1, 2 * tok, D_LATENT), lambda i: (i, 0, 0)),
            pl.BlockSpec((total // PAIRS, tok), lambda i: (i, 0)),
        ),
        compiler_params=pltpu.CompilerParams(vmem_limit_bytes=8 << 20),
        cost_estimate=cost(300_000_000, 10_000_000),
        name="prep",
    )(own.reshape(1), group_order, *in_hbm(queries, up_key_weight, out_grad, up_value_weight))

    pair_shape = pltpu.VMEM((PAIRS, total, 2 * tok), BF16)
    latent_shape = jax.ShapeDtypeStruct((half, D_LATENT), BF16)
    probs, grads, latent_send = pl.pallas_call(
        scores_kernel,
        grid=(PAIRS + 1,),
        out_shape=(pair_shape, pair_shape, latent_shape),
        in_specs=[hbm] * BLOCKS + [vmem] * 3,
        out_specs=(vmem, vmem, vmem),
        scratch_shapes=[
            pltpu.VMEM((total, WIDTH), BF16),
            pltpu.VMEM((CTX, ROPE_ROWS, D_LATENT), BF16),
            pltpu.VMEM((total, 2 * tok), F32),
            pltpu.VMEM((total, 2 * tok), F32),
            pltpu.SemaphoreType.DMA((2, CTX)),
        ],
        compiler_params=pltpu.CompilerParams(vmem_limit_bytes=40 << 20),
        cost_estimate=cost(8_000_000_000, 14_000_000),
        name="scores",
    )(*k_blocks, query_all, grad_lat, bias)

    latent_got = swap_ctx(latent_send, 1)

    latent_keep = pl.pallas_call(
        keep_kernel,
        out_shape=latent_shape,
        in_specs=[vmem] * 4,
        out_specs=vmem,
        compiler_params=pltpu.CompilerParams(vmem_limit_bytes=24 << 20),
        cost_estimate=cost(2_300_000_000, 7_000_000),
        name="keep",
    )(*in_vmem(probs, grads), query_all, grad_lat)

    share = D_LATENT // CTX
    weight_shape = jax.ShapeDtypeStruct((CTX // 2, 2, share, heads * NOPE), BF16)
    weight_spec = pl.BlockSpec((CTX // 2, 2, share, 2 * NOPE), lambda i: (0, 0, 0, i))
    query_grad, weight_send, weight_keep = pl.pallas_call(
        weights_kernel,
        grid=(PAIRS,),
        out_shape=(jax.ShapeDtypeStruct(queries.shape, BF16), weight_shape, weight_shape),
        in_specs=[smem]
        + [hbm] * BLOCKS
        + [
            vmem,
            vmem,
            pl.BlockSpec((tok, pair_cols), lambda i: (0, i)),
            pl.BlockSpec((tok, 2 * VDIM), lambda i: (0, i)),
            pl.BlockSpec((D_LATENT, 2 * NOPE), lambda i: (0, i)),
        ],
        out_specs=(pl.BlockSpec((tok, pair_cols), lambda i: (0, i)), weight_spec, weight_spec),
        scratch_shapes=[
            pltpu.VMEM((total, D_LATENT), BF16),
            pltpu.VMEM((CTX, ROPE_ROWS, D_LATENT), BF16),
            pltpu.VMEM((WIDTH, total), BF16),
            pltpu.VMEM((2, D_LATENT, 2 * NOPE), BF16),
            pltpu.SemaphoreType.DMA((2, CTX)),
        ],
        compiler_params=pltpu.CompilerParams(vmem_limit_bytes=24 << 20),
        cost_estimate=cost(5_000_000_000, 14_000_000),
        name="weights",
    )(own.reshape(1), *k_blocks, *in_vmem(probs, grads), *in_hbm(queries, out_grad, up_key_weight))

    step = 2 * PACKED
    pieces = [
        spread_sum([latent_keep[k * step : (k + 1) * step], latent_got[k * step : (k + 1) * step]]).astype(BF16)
        for k in range(4)
    ]
    got = [pieces[0]]
    for k in (2, 1, 3):
        got.append(swap_ctx(pieces[k], k << 2))
    other = spread_sum([g[PACKED:] for g in got]).astype(BF16)
    other = swap_ctx(other, 2)
    mine = spread_sum([g[:PACKED] for g in got] + [other]).astype(BF16)
    other = swap_head(mine, 1)
    mine = spread_sum([mine, other]).astype(BF16)
    other = swap_head(mine, 2)
    mine = spread_sum([mine, other]).astype(BF16)
    other = swap_head(mine, 6)
    latent_grad = spread_sum([mine[:tok], other[:tok]])
    turned = [
        spread_sum([part[tok:, g * LANES : (g + 1) * LANES] for part in (mine, other)]) for g in range(rope_parts)
    ]
    rope_grad = jnp.concatenate(turned, axis=0).T

    weight_got = swap_ctx(weight_send, 1)
    pieces = [
        spread_sum([weight_keep[2 * k : 2 * k + 2], weight_got[2 * k : 2 * k + 2]]).astype(BF16) for k in range(4)
    ]
    got = [pieces[0]]
    for k in (2, 1, 3):
        got.append(swap_ctx(pieces[k], k << 2))
    other = spread_sum([g[1] for g in got]).astype(BF16)
    other = swap_ctx(other, 2)
    up_key_grad, up_value_grad = (spread_sum([g[0, i] for g in got] + [other[i]]) for i in range(2))
    return query_grad, latent_grad, rope_grad, up_key_grad, up_value_grad


def solution(mesh):
    placed = (
        P("ctx", "head"),
        P("ctx", None),
        P("ctx", None),
        P(None, "head"),
        P(None, "head"),
        P("ctx", "head"),
        P(),
    )
    return jax.shard_map(
        per_device,
        mesh=mesh,
        in_specs=placed,
        out_specs=(
            P("ctx", "head"),
            P("ctx", None),
            P("ctx", None),
            P("ctx", "head"),
            P("ctx", "head"),
        ),
        check_vma=False,
    )
```

profile of v0, /device:TPU:0, one launch (start us, length us, event | category | flops | bytes accessed | tf_op | source)
XLA Modules:
  0.0 117.1 jit_solution(12588007747844222571)
XLA Ops:
  0.6 0.7 fusion.1
  1.4 0.9 maximum_maximum_fusion
  2.3 4.1 %collective-permute-start = (bf16[144,512]{1,0:T(8,128)(2,1)S(1)}, bf16[144,512]{1,0:T(8,128)(2,1)S(1)}, u32[]{:S(2)}, u32[]{:S(2)}) collective-permute-start(bf16[144,512]{1,0:T(8,128)(2,1)S(1)} %maximum_maximum_fusion), channel_id=1, source_target_pairs={{0,16},{8,24},{16,0},{24,8},{32,48},{40,56},{48,32},{56,40},{64,80... | collective-permute-start | bytes 442376 | tf_op jit(solution)/shard_map/ppermute | solution.py:33
  6.4 3.8 %collective-permute-done = bf16[144,512]{1,0:T(8,128)(2,1)S(1)} collective-permute-done((bf16[144,512]{1,0:T(8,128)(2,1)S(1)}, bf16[144,512]{1,0:T(8,128)(2,1)S(1)}, u32[]{:S(2)}, u32[]{:S(2)}) %collective-permute-start) | collective-permute-done | bytes 147488 | tf_op jit(solution)/shard_map/ppermute | solution.py:33
  10.2 0.9 pad_maximum_fusion.refs_0_.refs_1_
  11.1 3.1 %collective-permute-start.3 = (bf16[288,512]{1,0:T(8,128)(2,1)S(1)}, bf16[288,512]{1,0:T(8,128)(2,1)S(1)}, u32[]{:S(2)}, u32[]{:S(2)}) collective-permute-start(bf16[288,512]{1,0:T(8,128)(2,1)S(1)} %pad_maximum_fusion.refs_0_.refs_1_), channel_id=1, source_target_pairs={{0,96},{8,104},{16,112},{24,120},{32,64},{40,72},{48,80},{56,88},{... | collective-permute-start | bytes 884744 | tf_op jit(solution)/shard_map/ppermute | solution.py:33
  14.2 0.6 collective-permute-start.2
  14.9 0.5 collective-permute-start.1
  15.3 0.0 collective-permute-start.4
  15.3 11.7 %collective-permute-done.3.refs_3_.refs_4_ = bf16[288,512]{1,0:T(8,128)(2,1)S(1)} collective-permute-done((bf16[288,512]{1,0:T(8,128)(2,1)S(1)}, bf16[288,512]{1,0:T(8,128)(2,1)S(1)}, u32[]{:S(2)}, u32[]{:S(2)}) %collective-permute-start.3) | collective-permute-done | bytes 294944 | tf_op jit(solution)/shard_map/ppermute | solution.py:33
  27.0 0.0 collective-permute-start.7
  27.0 0.5 collective-permute-start.6
  27.5 0.2 collective-permute-done.1.refs_1_.refs_2_
  27.7 0.7 copy-done.2
  28.4 3.3 %prep.1 = (bf16[4,256,576]{2,1,0:T(8,128)(2,1)S(1)}, bf16[4,256,512]{2,1,0:T(8,128)(2,1)S(1)}, f32[2048,128]{1,0:T(8,128)S(1)}) custom-call(s32[1]{0:T(128)} %bitcast.own_ref.refs_0_, s32[32]{0:T(128)S(1)} %copy-done.2, bf16[128,1536]{1,0:T(8,128)(2,1)} %refs_11_.1, bf16[512,1024]{1,0:T(8,128)(2,1)} %refs_13_.1, bf16[128,1024]{1,0:T(8,128)(2,1)} %refs_12_.1, ...), custom_call_target="tpu_custom_call" | custom-call | flops 300000000 | bytes 10000000 | tf_op jit(solution)/shard_map/prep/pallas_call | solution.py:264
  31.6 1.1 copy-done
  32.7 14.0 %scores.1 = (bf16[4,2048,256]{2,1,0:T(8,128)(2,1)S(1)}, bf16[4,2048,256]{2,1,0:T(8,128)(2,1)S(1)}, bf16[1152,512]{1,0:T(8,128)(2,1)S(1)}) custom-call(bf16[288,512]{1,0:T(8,128)(2,1)S(1)} %pad_maximum_fusion.refs_0_.refs_1_, bf16[288,512]{1,0:T(8,128)(2,1)S(1)} %collective-permute-done.1.refs_1_.refs_2_, ...), custom_call_target="tpu_custom_call" | custom-call | flops 8000000000 | bytes 14000000 | tf_op jit(solution)/shard_map/scores/pallas_call | solution.py:292
  46.7 0.6 collective-permute-start.8
  47.3 13.8 %weights.1 = (bf16[128,1536]{1,0:T(8,128)(2,1)}, bf16[8,2,32,1024]{3,2,1,0:T(8,128)(2,1)S(1)}, bf16[8,2,32,1024]{3,2,1,0:T(8,128)(2,1)S(1)}) custom-call(s32[1]{0:T(128)} %bitcast.own_ref.refs_0_, bf16[288,512]{1,0:T(8,128)(2,1)S(1)} %pad_maximum_fusion.refs_0_.refs_1_, bf16[288,512]{1,0:T(8,128)(2,1)S(1)} %collective-permute-done.1.refs_1_.refs_2_, ...), custom_call_target="tpu_custom_call" | custom-call | flops 5000000000 | bytes 14000000 | tf_op jit(solution)/shard_map/weights/pallas_call | solution.py:325
  61.2 0.3 collective-permute-start.16
  61.5 2.9 %keep.1 = bf16[1152,512]{1,0:T(8,128)(2,1)S(1)} custom-call(bf16[4,2048,256]{2,1,0:T(8,128)(2,1)S(1)} %get-tuple-element.17.refs_9_.probs_ref, bf16[4,2048,256]{2,1,0:T(8,128)(2,1)S(1)} %get-tuple-element.18.refs_10_.grads_ref, bf16[4,256,576]{2,1,0:T(8,128)(2,1)S(1)} %copy-done.1, bf16[4,256,512]{2,1,0:T(8,128)(2,1)S(1)} %get-tuple-element.15.refs_9_.gl_ref), custom_call_target="tpu_custom_call" | custom-call | flops 2300000000 | bytes 7000000 | tf_op jit(solution)/shard_map/keep/pallas_call | solution.py:312
  64.4 0.3 add_convert_fusion.3
  64.7 2.9 %collective-permute-start.11 = (bf16[288,512]{1,0:T(8,128)(2,1)S(1)}, bf16[288,512]{1,0:T(8,128)(2,1)S(1)}, u32[]{:S(2)}, u32[]{:S(2)}) collective-permute-start(bf16[288,512]{1,0:T(8,128)(2,1)S(1)} %get-tuple-element.24), channel_id=1, source_target_pairs={{0,96},{8,104},{16,112},{24,120},{32,64},{40,72},{48,80},{56,88},{... | collective-permute-start | bytes 884744 | tf_op jit(solution)/shard_map/ppermute | solution.py:33
  67.6 0.1 collective-permute-start.10
  67.8 1.7 %collective-permute-start.9 = (bf16[288,512]{1,0:T(8,128)(2,1)S(1)}, bf16[288,512]{1,0:T(8,128)(2,1)S(1)}, u32[]{:S(2)}, u32[]{:S(2)}) collective-permute-start(bf16[288,512]{1,0:T(8,128)(2,1)S(1)} %get-tuple-element.26), channel_id=1, source_target_pairs={{0,64},{8,72},{16,80},{24,88},{32,96},{40,104},{48,112},{56,120},{... | collective-permute-start | bytes 884744 | tf_op jit(solution)/shard_map/ppermute | solution.py:33
  69.5 5.9 %collective-permute-done.11 = bf16[288,512]{1,0:T(8,128)(2,1)S(1)} collective-permute-done((bf16[288,512]{1,0:T(8,128)(2,1)S(1)}, bf16[288,512]{1,0:T(8,128)(2,1)S(1)}, u32[]{:S(2)}, u32[]{:S(2)}) %collective-permute-start.11) | collective-permute-done | bytes 294944 | tf_op jit(solution)/shard_map/ppermute | solution.py:33
  75.4 2.1 %collective-permute-done.10 = bf16[288,512]{1,0:T(8,128)(2,1)S(1)} collective-permute-done((bf16[288,512]{1,0:T(8,128)(2,1)S(1)}, bf16[288,512]{1,0:T(8,128)(2,1)S(1)}, u32[]{:S(2)}, u32[]{:S(2)}) %collective-permute-start.10) | collective-permute-done | bytes 294944 | tf_op jit(solution)/shard_map/ppermute | solution.py:33
  77.5 5.4 %collective-permute-done.9 = bf16[288,512]{1,0:T(8,128)(2,1)S(1)} collective-permute-done((bf16[288,512]{1,0:T(8,128)(2,1)S(1)}, bf16[288,512]{1,0:T(8,128)(2,1)S(1)}, u32[]{:S(2)}, u32[]{:S(2)}) %collective-permute-start.9) | collective-permute-done | bytes 294944 | tf_op jit(solution)/shard_map/ppermute | solution.py:33
  82.9 0.1 add_convert_fusion.11
  83.0 3.0 %collective-permute-start.12 = (bf16[144,512]{1,0:T(8,128)(2,1)S(1)}, bf16[144,512]{1,0:T(8,128)(2,1)S(1)}, u32[]{:S(2)}, u32[]{:S(2)}) collective-permute-start(bf16[144,512]{1,0:T(8,128)(2,1)S(1)} %add_convert_fusion.11), channel_id=1, source_target_pairs={{0,16},{8,24},{16,0},{24,8},{32,48},{40,56},{48,32},{56,40},{64,80... | collective-permute-start | bytes 442376 | tf_op jit(solution)/shard_map/ppermute | solution.py:33
  86.0 3.7 %collective-permute-done.12 = bf16[144,512]{1,0:T(8,128)(2,1)S(1)} collective-permute-done((bf16[144,512]{1,0:T(8,128)(2,1)S(1)}, bf16[144,512]{1,0:T(8,128)(2,1)S(1)}, u32[]{:S(2)}, u32[]{:S(2)}) %collective-permute-start.12) | collective-permute-done | bytes 147488 | tf_op jit(solution)/shard_map/ppermute | solution.py:33
  89.7 0.1 add_convert_fusion.10
  89.8 1.1 collective-permute-start.13
  90.9 0.4 add_convert_fusion.7
  91.3 2.9 %collective-permute-start.19 = (bf16[2,2,32,1024]{3,2,1,0:T(8,128)(2,1)S(1)}, bf16[2,2,32,1024]{3,2,1,0:T(8,128)(2,1)S(1)}, u32[]{:S(2)}, u32[]{:S(2)}) collective-permute-start(bf16[2,2,32,1024]{3,2,1,0:T(8,128)(2,1)S(1)} %get-tuple-element.28), channel_id=1, source_target_pairs={{0,96},{8,104},{16,112},{24,120},{32,64},{40,72},{48,80},{56,88},{... | collective-permute-start | bytes 786440 | tf_op jit(solution)/shard_map/ppermute | solution.py:33
  94.3 1.8 %collective-permute-start.17 = (bf16[2,2,32,1024]{3,2,1,0:T(8,128)(2,1)S(1)}, bf16[2,2,32,1024]{3,2,1,0:T(8,128)(2,1)S(1)}, u32[]{:S(2)}, u32[]{:S(2)}) collective-permute-start(bf16[2,2,32,1024]{3,2,1,0:T(8,128)(2,1)S(1)} %get-tuple-element.30), channel_id=1, source_target_pairs={{0,64},{8,72},{16,80},{24,88},{32,96},{40,104},{48,112},{56,120},{... | collective-permute-start | bytes 786440 | tf_op jit(solution)/shard_map/ppermute | solution.py:33
  96.2 1.6 %collective-permute-start.14 = (bf16[144,512]{1,0:T(8,128)(2,1)S(1)}, bf16[144,512]{1,0:T(8,128)(2,1)S(1)}, u32[]{:S(2)}, u32[]{:S(2)}) collective-permute-start(bf16[144,512]{1,0:T(8,128)(2,1)S(1)} %add_convert_fusion.9), channel_id=1, source_target_pairs={{0,2},{1,3},{2,0},{3,1},{4,6},{5,7},{6,4},{7,5},{8,10},{9,11},{10,... | collective-permute-start | bytes 442376 | tf_op jit(solution)/shard_map/ppermute | solution.py:37
  97.7 3.7 %collective-permute-done.19 = bf16[2,2,32,1024]{3,2,1,0:T(8,128)(2,1)S(1)} collective-permute-done((bf16[2,2,32,1024]{3,2,1,0:T(8,128)(2,1)S(1)}, bf16[2,2,32,1024]{3,2,1,0:T(8,128)(2,1)S(1)}, u32[]{:S(2)}, u32[]{:S(2)}) %collective-permute-start.19) | collective-permute-done | bytes 262176 | tf_op jit(solution)/shard_map/ppermute | solution.py:33
  101.4 1.5 %collective-permute-done.18 = bf16[2,2,32,1024]{3,2,1,0:T(8,128)(2,1)S(1)} collective-permute-done((bf16[2,2,32,1024]{3,2,1,0:T(8,128)(2,1)S(1)}, bf16[2,2,32,1024]{3,2,1,0:T(8,128)(2,1)S(1)}, u32[]{:S(2)}, u32[]{:S(2)}) %collective-permute-start.18) | collective-permute-done | bytes 262176 | tf_op jit(solution)/shard_map/ppermute | solution.py:33
  102.9 2.6 %collective-permute-done.17 = bf16[2,2,32,1024]{3,2,1,0:T(8,128)(2,1)S(1)} collective-permute-done((bf16[2,2,32,1024]{3,2,1,0:T(8,128)(2,1)S(1)}, bf16[2,2,32,1024]{3,2,1,0:T(8,128)(2,1)S(1)}, u32[]{:S(2)}, u32[]{:S(2)}) %collective-permute-start.17) | collective-permute-done | bytes 262176 | tf_op jit(solution)/shard_map/ppermute | solution.py:33
  105.5 0.1 fusion
  105.6 3.7 %collective-permute-start.20 = (bf16[2,32,1024]{2,1,0:T(8,128)(2,1)S(1)}, bf16[2,32,1024]{2,1,0:T(8,128)(2,1)S(1)}, u32[]{:S(2)}, u32[]{:S(2)}) collective-permute-start(bf16[2,32,1024]{2,1,0:T(8,128)(2,1)S(1)} %fusion), channel_id=1, source_target_pairs={{0,16},{8,24},{16,0},{24,8},{32,48},{40,56},{48,32},{56,40},{64,80... | collective-permute-start | bytes 393224 | tf_op jit(solution)/shard_map/ppermute | solution.py:33
  109.3 2.8 %collective-permute-start.15 = (bf16[144,512]{1,0:T(8,128)(2,1)S(1)}, bf16[144,512]{1,0:T(8,128)(2,1)S(1)}, u32[]{:S(2)}, u32[]{:S(2)}) collective-permute-start(bf16[144,512]{1,0:T(8,128)(2,1)S(1)} %add_convert_fusion.8), channel_id=1, source_target_pairs={{0,6},{1,7},{2,4},{3,5},{4,2},{5,3},{6,0},{7,1},{8,14},{9,15},{10,... | collective-permute-start | bytes 442376 | tf_op jit(solution)/shard_map/ppermute | solution.py:37
  112.1 0.1 collective-permute-done.20
  112.2 0.8 convert_add_fusion.1
  113.0 2.7 %collective-permute-done.15 = bf16[144,512]{1,0:T(8,128)(2,1)S(1)} collective-permute-done((bf16[144,512]{1,0:T(8,128)(2,1)S(1)}, bf16[144,512]{1,0:T(8,128)(2,1)S(1)}, u32[]{:S(2)}, u32[]{:S(2)}) %collective-permute-start.15) | collective-permute-done | bytes 147488 | tf_op jit(solution)/shard_map/ppermute | solution.py:37
  115.8 0.6 maximum_bitcast_fusion
  116.4 0.7 convert_add_fusion
  (18 shorter events, 0.1 us)
Async XLA Ops:
  2.3 7.9 %collective-permute-start = (bf16[144,512]{1,0:T(8,128)(2,1)S(1)}, bf16[144,512]{1,0:T(8,128)(2,1)S(1)}, u32[]{:S(2)}, u32[]{:S(2)}) collective-permute-start(bf16[144,512]{1,0:T(8,128)(2,1)S(1)} %maximum_maximum_fusion), channel_id=1, source_target_pairs={{0,16},{8,24},{16,0},{24,8},{32,48},{40,56},{48,32},{56,40},{64,80... | collective-permute-start | bytes 442376 | tf_op jit(solution)/shard_map/ppermute | solution.py:33
  11.1 15.8 %collective-permute-start.3 = (bf16[288,512]{1,0:T(8,128)(2,1)S(1)}, bf16[288,512]{1,0:T(8,128)(2,1)S(1)}, u32[]{:S(2)}, u32[]{:S(2)}) collective-permute-start(bf16[288,512]{1,0:T(8,128)(2,1)S(1)} %pad_maximum_fusion.refs_0_.refs_1_), channel_id=1, source_target_pairs={{0,96},{8,104},{16,112},{24,120},{32,64},{40,72},{48,80},{56,88},{... | collective-permute-start | bytes 884744 | tf_op jit(solution)/shard_map/ppermute | solution.py:33
  14.2 12.8 %collective-permute-start.2 = (bf16[288,512]{1,0:T(8,128)(2,1)S(1)}, bf16[288,512]{1,0:T(8,128)(2,1)S(1)}, u32[]{:S(2)}, u32[]{:S(2)}) collective-permute-start(bf16[288,512]{1,0:T(8,128)(2,1)S(1)} %pad_maximum_fusion.refs_0_.refs_1_), channel_id=1, source_target_pairs={{0,64},{8,72},{16,80},{24,88},{32,96},{40,104},{48,112},{56,120},{... | collective-permute-start | bytes 884744 | tf_op jit(solution)/shard_map/ppermute | solution.py:33
  14.9 12.8 %collective-permute-start.1 = (bf16[288,512]{1,0:T(8,128)(2,1)S(1)}, bf16[288,512]{1,0:T(8,128)(2,1)S(1)}, u32[]{:S(2)}, u32[]{:S(2)}) collective-permute-start(bf16[288,512]{1,0:T(8,128)(2,1)S(1)} %pad_maximum_fusion.refs_0_.refs_1_), channel_id=1, source_target_pairs={{0,32},{8,40},{16,48},{24,56},{32,0},{40,8},{48,16},{56,24},{64,96... | collective-permute-start | bytes 884744 | tf_op jit(solution)/shard_map/ppermute | solution.py:33
  15.3 17.4 %collective-permute-start.4 = (bf16[288,512]{1,0:T(8,128)(2,1)S(1)}, bf16[288,512]{1,0:T(8,128)(2,1)S(1)}, u32[]{:S(2)}, u32[]{:S(2)}) collective-permute-start(bf16[288,512]{1,0:T(8,128)(2,1)S(1)} %pad_maximum_fusion.refs_0_.refs_1_), channel_id=1, source_target_pairs={{0,8},{8,0},{16,24},{24,16},{32,40},{40,32},{48,56},{56,48},{64,72... | collective-permute-start | bytes 884744 | tf_op jit(solution)/shard_map/ppermute | solution.py:33
  27.0 5.7 %collective-permute-start.7 = (bf16[288,512]{1,0:T(8,128)(2,1)S(1)}, bf16[288,512]{1,0:T(8,128)(2,1)S(1)}, u32[]{:S(2)}, u32[]{:S(2)}) collective-permute-start(bf16[288,512]{1,0:T(8,128)(2,1)S(1)} %collective-permute-done.3.refs_3_.refs_4_), channel_id=1, source_target_pairs={{0,8},{8,0},{16,24},{24,16},{32,40},{40,32},{48,56},{56,48},{64,72... | collective-permute-start | bytes 884744 | tf_op jit(solution)/shard_map/ppermute | solution.py:33
  27.0 5.7 %collective-permute-start.6 = (bf16[288,512]{1,0:T(8,128)(2,1)S(1)}, bf16[288,512]{1,0:T(8,128)(2,1)S(1)}, u32[]{:S(2)}, u32[]{:S(2)}) collective-permute-start(bf16[288,512]{1,0:T(8,128)(2,1)S(1)} %collective-permute-done.2.refs_2_.refs_3_), channel_id=1, source_target_pairs={{0,8},{8,0},{16,24},{24,16},{32,40},{40,32},{48,56},{56,48},{64,72... | collective-permute-start | bytes 884744 | tf_op jit(solution)/shard_map/ppermute | solution.py:33
  27.7 5.0 %collective-permute-start.5 = (bf16[288,512]{1,0:T(8,128)(2,1)S(1)}, bf16[288,512]{1,0:T(8,128)(2,1)S(1)}, u32[]{:S(2)}, u32[]{:S(2)}) collective-permute-start(bf16[288,512]{1,0:T(8,128)(2,1)S(1)} %collective-permute-done.1.refs_1_.refs_2_), channel_id=1, source_target_pairs={{0,8},{8,0},{16,24},{24,16},{32,40},{40,32},{48,56},{56,48},{64,72... | collective-permute-start | bytes 884744 | tf_op jit(solution)/shard_map/ppermute | solution.py:33
  27.7 0.7 copy-start.2
  31.6 1.1 copy-start
  46.7 17.6 %collective-permute-start.8 = (bf16[1152,512]{1,0:T(8,128)(2,1)S(1)}, bf16[1152,512]{1,0:T(8,128)(2,1)S(1)}, u32[]{:S(2)}, u32[]{:S(2)}) collective-permute-start(bf16[1152,512]{1,0:T(8,128)(2,1)S(1)} %get-tuple-element.20), channel_id=1, source_target_pairs={{0,8},{8,0},{16,24},{24,16},{32,40},{40,32},{48,56},{56,48},{64,72... | collective-permute-start | bytes 3538952 | tf_op jit(solution)/shard_map/ppermute | solution.py:33
  47.3 14.1 %copy-start.1 = (bf16[4,256,576]{2,1,0:T(8,128)(2,1)S(1)}, bf16[4,256,576]{2,1,0:T(8,128)(2,1)}, u32[]{:S(2)}) copy-start(bf16[4,256,576]{2,1,0:T(8,128)(2,1)} %copy-done) | copy-start | bytes 3538948
  61.2 29.7 %collective-permute-start.16 = (bf16[8,2,32,1024]{3,2,1,0:T(8,128)(2,1)S(1)}, bf16[8,2,32,1024]{3,2,1,0:T(8,128)(2,1)S(1)}, u32[]{:S(2)}, u32[]{:S(2)}) collective-permute-start(bf16[8,2,32,1024]{3,2,1,0:T(8,128)(2,1)S(1)} %get-tuple-element.22), channel_id=1, source_target_pairs={{0,8},{8,0},{16,24},{24,16},{32,40},{40,32},{48,56},{56,48},{64,72... | collective-permute-start | bytes 3145736 | tf_op jit(solution)/shard_map/ppermute | solution.py:33
  64.7 10.7 %collective-permute-start.11 = (bf16[288,512]{1,0:T(8,128)(2,1)S(1)}, bf16[288,512]{1,0:T(8,128)(2,1)S(1)}, u32[]{:S(2)}, u32[]{:S(2)}) collective-permute-start(bf16[288,512]{1,0:T(8,128)(2,1)S(1)} %get-tuple-element.24), channel_id=1, source_target_pairs={{0,96},{8,104},{16,112},{24,120},{32,64},{40,72},{48,80},{56,88},{... | collective-permute-start | bytes 884744 | tf_op jit(solution)/shard_map/ppermute | solution.py:33
  67.6 9.9 %collective-permute-start.10 = (bf16[288,512]{1,0:T(8,128)(2,1)S(1)}, bf16[288,512]{1,0:T(8,128)(2,1)S(1)}, u32[]{:S(2)}, u32[]{:S(2)}) collective-permute-start(bf16[288,512]{1,0:T(8,128)(2,1)S(1)} %get-tuple-element.25), channel_id=1, source_target_pairs={{0,32},{8,40},{16,48},{24,56},{32,0},{40,8},{48,16},{56,24},{64,96... | collective-permute-start | bytes 884744 | tf_op jit(solution)/shard_map/ppermute | solution.py:33
  67.8 15.1 %collective-permute-start.9 = (bf16[288,512]{1,0:T(8,128)(2,1)S(1)}, bf16[288,512]{1,0:T(8,128)(2,1)S(1)}, u32[]{:S(2)}, u32[]{:S(2)}) collective-permute-start(bf16[288,512]{1,0:T(8,128)(2,1)S(1)} %get-tuple-element.26), channel_id=1, source_target_pairs={{0,64},{8,72},{16,80},{24,88},{32,96},{40,104},{48,112},{56,120},{... | collective-permute-start | bytes 884744 | tf_op jit(solution)/shard_map/ppermute | solution.py:33
  83.0 6.7 %collective-permute-start.12 = (bf16[144,512]{1,0:T(8,128)(2,1)S(1)}, bf16[144,512]{1,0:T(8,128)(2,1)S(1)}, u32[]{:S(2)}, u32[]{:S(2)}) collective-permute-start(bf16[144,512]{1,0:T(8,128)(2,1)S(1)} %add_convert_fusion.11), channel_id=1, source_target_pairs={{0,16},{8,24},{16,0},{24,8},{32,48},{40,56},{48,32},{56,40},{64,80... | collective-permute-start | bytes 442376 | tf_op jit(solution)/shard_map/ppermute | solution.py:33
  89.8 6.3 %collective-permute-start.13 = (bf16[144,512]{1,0:T(8,128)(2,1)S(1)}, bf16[144,512]{1,0:T(8,128)(2,1)S(1)}, u32[]{:S(2)}, u32[]{:S(2)}) collective-permute-start(bf16[144,512]{1,0:T(8,128)(2,1)S(1)} %add_convert_fusion.10), channel_id=1, source_target_pairs={{0,1},{1,0},{2,3},{3,2},{4,5},{5,4},{6,7},{7,6},{8,9},{9,8},{10,11... | collective-permute-start | bytes 442376 | tf_op jit(solution)/shard_map/ppermute | solution.py:37
  91.3 10.1 %collective-permute-start.19 = (bf16[2,2,32,1024]{3,2,1,0:T(8,128)(2,1)S(1)}, bf16[2,2,32,1024]{3,2,1,0:T(8,128)(2,1)S(1)}, u32[]{:S(2)}, u32[]{:S(2)}) collective-permute-start(bf16[2,2,32,1024]{3,2,1,0:T(8,128)(2,1)S(1)} %get-tuple-element.28), channel_id=1, source_target_pairs={{0,96},{8,104},{16,112},{24,120},{32,64},{40,72},{48,80},{56,88},{... | collective-permute-start | bytes 786440 | tf_op jit(solution)/shard_map/ppermute | solution.py:33
  94.3 8.6 %collective-permute-start.18 = (bf16[2,2,32,1024]{3,2,1,0:T(8,128)(2,1)S(1)}, bf16[2,2,32,1024]{3,2,1,0:T(8,128)(2,1)S(1)}, u32[]{:S(2)}, u32[]{:S(2)}) collective-permute-start(bf16[2,2,32,1024]{3,2,1,0:T(8,128)(2,1)S(1)} %get-tuple-element.29), channel_id=1, source_target_pairs={{0,32},{8,40},{16,48},{24,56},{32,0},{40,8},{48,16},{56,24},{64,96... | collective-permute-start | bytes 786440 | tf_op jit(solution)/shard_map/ppermute | solution.py:33
  94.3 11.3 %collective-permute-start.17 = (bf16[2,2,32,1024]{3,2,1,0:T(8,128)(2,1)S(1)}, bf16[2,2,32,1024]{3,2,1,0:T(8,128)(2,1)S(1)}, u32[]{:S(2)}, u32[]{:S(2)}) collective-permute-start(bf16[2,2,32,1024]{3,2,1,0:T(8,128)(2,1)S(1)} %get-tuple-element.30), channel_id=1, source_target_pairs={{0,64},{8,72},{16,80},{24,88},{32,96},{40,104},{48,112},{56,120},{... | collective-permute-start | bytes 786440 | tf_op jit(solution)/shard_map/ppermute | solution.py:33
  96.2 13.1 %collective-permute-start.14 = (bf16[144,512]{1,0:T(8,128)(2,1)S(1)}, bf16[144,512]{1,0:T(8,128)(2,1)S(1)}, u32[]{:S(2)}, u32[]{:S(2)}) collective-permute-start(bf16[144,512]{1,0:T(8,128)(2,1)S(1)} %add_convert_fusion.9), channel_id=1, source_target_pairs={{0,2},{1,3},{2,0},{3,1},{4,6},{5,7},{6,4},{7,5},{8,10},{9,11},{10,... | collective-permute-start | bytes 442376 | tf_op jit(solution)/shard_map/ppermute | solution.py:37
  105.6 6.6 %collective-permute-start.20 = (bf16[2,32,1024]{2,1,0:T(8,128)(2,1)S(1)}, bf16[2,32,1024]{2,1,0:T(8,128)(2,1)S(1)}, u32[]{:S(2)}, u32[]{:S(2)}) collective-permute-start(bf16[2,32,1024]{2,1,0:T(8,128)(2,1)S(1)} %fusion), channel_id=1, source_target_pairs={{0,16},{8,24},{16,0},{24,8},{32,48},{40,56},{48,32},{56,40},{64,80... | collective-permute-start | bytes 393224 | tf_op jit(solution)/shard_map/ppermute | solution.py:33
  109.3 6.4 %collective-permute-start.15 = (bf16[144,512]{1,0:T(8,128)(2,1)S(1)}, bf16[144,512]{1,0:T(8,128)(2,1)S(1)}, u32[]{:S(2)}, u32[]{:S(2)}) collective-permute-start(bf16[144,512]{1,0:T(8,128)(2,1)S(1)} %add_convert_fusion.8), channel_id=1, source_target_pairs={{0,6},{1,7},{2,4},{3,5},{4,2},{5,3},{6,0},{7,1},{8,14},{9,15},{10,... | collective-permute-start | bytes 442376 | tf_op jit(solution)/shard_map/ppermute | solution.py:37
where the time goes:
time: 117 us
  waiting for transfers between devices  43.4 us (37%)
  Pallas kernels  34 us (29%)
  starting transfers between devices  31.4 us (27%)
  other arithmetic  5.09 us (4%)
  local copies, waits for them, and re-layouts  2.48 us (2%)
    ppermute x18, waiting for transfers between devices, swap_ctx(): return lax.ppermute(value, 'ctx', [(i, i ^ mask) for i in range(CTX)])  40.7 us
    ppermute x18, starting transfers between devices, swap_ctx(): return lax.ppermute(value, 'ctx', [(i, i ^ mask) for i in range(CTX)])  25.9 us
    pallas_call x1, Pallas kernels, per_device(): pl.pallas_call(scores_kernel, grid=(PAIRS + 1,), out_shape=(pair_shape, p...  14 us
    pallas_call x1, Pallas kernels, per_device(): pl.pallas_call(weights_kernel, grid=(PAIRS,), out_shape=(jax.ShapeDtypeSt...  13.8 us
    ppermute x3, starting transfers between devices, swap_head(): return lax.ppermute(value, 'head', [(i, i ^ mask) for i in range(HEAD)])  5.48 us
    pallas_call x1, Pallas kernels, per_device(): pl.pallas_call(prep_kernel, grid=(PAIRS,), out_shape=(jax.ShapeDtypeStruc...  3.26 us
    pallas_call x1, Pallas kernels, per_device(): pl.pallas_call(keep_kernel, out_shape=latent_shape, in_specs=[vmem] * 4,...  2.88 us
    ppermute x3, waiting for transfers between devices, swap_head(): return lax.ppermute(value, 'head', [(i, i ^ mask) for i in range(HEAD)])  2.75 us
  transfers between devices with their start and end apart: 21, of which 12 were waited for; matrix products, arithmetic and copies ran while one was open for 2% of the time, Pallas kernels for 17%

commit v1 on v0

--- a/solution.py
+++ b/solution.py
@@ -24,7 +24,12 @@
 F32 = jnp.float32
 
 
-def ctx_xor(position):
+def key_xor(position):
+    core, zhi, y_bits = position >> 3, (position >> 2) & 1, position & 3
+    return (y_bits << 2) | (zhi << 1) | core
+
+
+def row_xor(position):
     core, y_bits, zhi = position >> 3, (position >> 1) & 3, position & 1
     return (y_bits << 2) | (zhi << 1) | core
 
@@ -52,21 +57,13 @@
 ROPE_ROWS = 16
 PACKED = CHUNK + ROPE_ROWS
 LANES = 128
-
-
-def load_keys(k_refs, keys, ropes, sems):
-    copies = []
-    for b in range(BLOCKS):
-        for c in range(2):
-            chunk = 2 * b + c
-            rows = slice(chunk * CHUNK, (chunk + 1) * CHUNK)
-            top = c * PACKED
-            copies.append(pltpu.make_async_copy(k_refs[b].at[top : top + CHUNK], keys.at[rows, :D_LATENT], sems.at[0, chunk]))
-            copies.append(pltpu.make_async_copy(k_refs[b].at[top + CHUNK : top + PACKED], ropes.at[chunk], sems.at[1, chunk]))
-    for copy in copies:
-        copy.start()
-    for copy in copies:
-        copy.wait()
+TILE = 64
+EARLY = (0, 1, 4, 5)
+LATE = (2, 3, 6, 7)
+
+
+def key_ropes(k_ref):
+    return rope_rows(k_ref[CHUNK:, :])
 
 
 def rope_rows(packed):
@@ -89,8 +86,7 @@
     query_pos = jnp.where(lane < GROUP, order_ref[2 * own] * GROUP, order_ref[2 * own + 1] * GROUP - GROUP) + lane
     for c in range(CTX // PAIRS):
         position = step * (CTX // PAIRS) + c
-        core, y_bits, zhi = position >> 3, (position >> 1) & 3, position & 1
-        device = own ^ ((y_bits << 2) | (zhi << 1) | core)
+        device = own ^ key_xor(position)
         for g in range(2):
             key_pos = order_ref[2 * device + g] * GROUP + row
             first = c * CHUNK + g * GROUP
@@ -100,7 +96,7 @@
 def latent_rows(probs, grads, q_ref, gl_ref):
     query = q_ref[...].reshape(PAIRS * 2 * CHUNK, WIDTH)
     grad_lat = gl_ref[...].reshape(PAIRS * 2 * CHUNK, D_LATENT)
-    both = dot(grads, query, NN)
+    both = dot(grads, query, NN) * SCALE
     return both[:, :D_LATENT] + dot(probs, grad_lat, NN), both[:, D_LATENT:]
 
 
@@ -114,54 +110,86 @@
         out_ref[top + CHUNK : top + PACKED, :] = jnp.concatenate(packed, axis=1).astype(BF16)
 
 
-def scores_kernel(*refs):
-    k_refs = refs[:BLOCKS]
-    q_ref, gl_ref, bias_ref = refs[BLOCKS : BLOCKS + 3]
-    probs, grads, send_ref = refs[BLOCKS + 3 : BLOCKS + 6]
-    keys, ropes, e_ref, g_ref, key_sems = refs[BLOCKS + 6 :]
+def load_keys(k_refs, keys):
+    for i, k_ref in enumerate(k_refs):
+        rows = slice(i * CHUNK, (i + 1) * CHUNK)
+        keys[rows, :D_LATENT] = k_ref[:CHUNK, :]
+        keys[rows, D_LATENT:] = key_ropes(k_ref).T
+
+
+def score_blocks(blocks, step, keys, q_ref, gl_ref, bias_ref, e_ref, g_ref, state):
+    q = q_ref[step]
+    gl = gl_ref[step]
+    tops = []
+    for i, kb in enumerate(blocks):
+        rows = slice(i * BLOCK, (i + 1) * BLOCK)
+        block = keys[rows, :]
+        s = dot(block, q, NT)
+        g = dot(block[:, :D_LATENT], gl, NT)
+        bias = bias_ref[kb * BLOCK : (kb + 1) * BLOCK, :]
+        s = s * SCALE_LOG2 + jnp.concatenate([bias, bias], axis=1)
+        top = jnp.max(s, axis=0, keepdims=True)
+        if state is not None:
+            top = jnp.maximum(state[0], top)
+        e = jnp.exp2(s - top)
+        total = jnp.sum(e, axis=0, keepdims=True)
+        weighted = jnp.sum(e * g, axis=0, keepdims=True)
+        if state is not None:
+            shrink = jnp.exp2(state[0] - top)
+            total = state[1] * shrink + total
+            weighted = state[2] * shrink + weighted
+        state = (top, total, weighted)
+        tops.append(top)
+        e_ref[rows, :] = e.astype(BF16)
+        g_ref[rows, :] = g
+    return state, tops
+
+
+def early_kernel(*refs):
+    count = 2 * len(EARLY)
+    k_refs = refs[:count]
+    q_ref, gl_ref, bias_ref, e_ref, g_ref, state_ref, keys = refs[count:]
     step = pl.program_id(0)
 
     @pl.when(step == 0)
     def _():
-        load_keys(k_refs, keys, ropes, key_sems)
-        for chunk in range(CTX):
-            keys[chunk * CHUNK : (chunk + 1) * CHUNK, D_LATENT:] = rope_rows(ropes[chunk]).T
+        load_keys(k_refs, keys)
+
+    state, tops = score_blocks(
+        EARLY, step, keys, q_ref, gl_ref, bias_ref, e_ref.at[step], g_ref.at[step], None
+    )
+    for i, value in enumerate(state + tuple(tops)):
+        state_ref[step, i : i + 1, :] = value
+
+
+def scores_kernel(*refs):
+    count = 2 * len(LATE)
+    k_refs = refs[:count]
+    q_ref, gl_ref, bias_ref, early_e, early_g, early_state, probs, grads, send_ref, keys, e_ref, g_ref = refs[count:]
+    step = pl.program_id(0)
+
+    @pl.when(step == 0)
+    def _():
+        load_keys(k_refs, keys)
 
     @pl.when(step < PAIRS)
     def _():
-        q = q_ref[step]
-        gl = gl_ref[step]
-        run_max, run_sum, run_dot = None, None, None
-        maxes = []
-        for kb in range(BLOCKS):
-            rows = slice(kb * BLOCK, (kb + 1) * BLOCK)
-            block = keys[rows, :]
-            s = dot(block, q, NT)
-            g = dot(block[:, :D_LATENT], gl, NT)
-            bias = bias_ref[rows, :]
-            s = s * SCALE_LOG2 + jnp.concatenate([bias, bias], axis=1)
-            top = jnp.max(s, axis=0, keepdims=True)
-            if kb > 0:
-                top = jnp.maximum(run_max, top)
-            e = jnp.exp2(s - top)
-            part = jnp.sum(e, axis=0, keepdims=True)
-            part_dot = jnp.sum(e * g, axis=0, keepdims=True)
-            if kb > 0:
-                shrink = jnp.exp2(run_max - top)
-                part = run_sum * shrink + part
-                part_dot = run_dot * shrink + part_dot
-            run_max, run_sum, run_dot = top, part, part_dot
-            maxes.append(top)
-            e_ref[rows, :] = e
-            g_ref[rows, :] = g
-        inverse = 1.0 / run_sum
-        delta = run_dot * inverse
-        for kb in range(BLOCKS):
-            rows = slice(kb * BLOCK, (kb + 1) * BLOCK)
-            factor = jnp.exp2(maxes[kb] - run_max) * inverse
-            p = e_ref[rows, :] * factor
-            probs[step, rows, :] = p.astype(BF16)
-            grads[step, rows, :] = (p * (g_ref[rows, :] - delta) * SCALE).astype(BF16)
+        before = [early_state[step, i : i + 1, :] for i in range(3 + len(EARLY))]
+        state, late_tops = score_blocks(
+            LATE, step, keys, q_ref, gl_ref, bias_ref, e_ref, g_ref, tuple(before[:3])
+        )
+        inverse = 1.0 / state[1]
+        delta = state[2] * inverse
+        parts = [(EARLY, before[3:], early_e.at[step], early_g.at[step]), (LATE, late_tops, e_ref, g_ref)]
+        for blocks, tops, e_part, g_part in parts:
+            for i, kb in enumerate(blocks):
+                factor = jnp.broadcast_to(jnp.exp2(tops[i] - state[0]) * inverse, (TILE, 2 * CHUNK)).astype(BF16)
+                for tile in range(BLOCK // TILE):
+                    rows = slice(i * BLOCK + tile * TILE, i * BLOCK + (tile + 1) * TILE)
+                    to = slice(kb * BLOCK + tile * TILE, kb * BLOCK + (tile + 1) * TILE)
+                    p = e_part[rows, :] * factor
+                    probs[step, to, :] = p
+                    grads[step, to, :] = p * (g_part[rows, :] - delta).astype(BF16)
 
     @pl.when(step == PAIRS)
     def _():
@@ -178,22 +206,20 @@
 
 def weights_kernel(*refs):
     own_ref = refs[0]
-    k_refs = refs[1 : BLOCKS + 1]
-    probs_ref, grads_ref, query_ref, out_grad_ref, up_key_ref = refs[BLOCKS + 1 : BLOCKS + 6]
-    query_grad_ref, send_ref, keep_ref = refs[BLOCKS + 6 : BLOCKS + 9]
-    keys, ropes, kt_ref, w_ref, key_sems = refs[BLOCKS + 9 :]
-
-    @pl.when(pl.program_id(0) == 0)
+    k_refs = refs[1 : CTX + 1]
+    probs_ref, grads_ref, query_ref, out_grad_ref, up_key_ref = refs[CTX + 1 : CTX + 6]
+    query_grad_ref, send_ref, keep_ref, kt_ref, w_ref = refs[CTX + 6 :]
+    step = pl.program_id(0)
+
+    @pl.when(step == 0)
     def _():
-        load_keys(k_refs, keys, ropes, key_sems)
-        for chunk in range(CTX):
-            cols = slice(chunk * CHUNK, (chunk + 1) * CHUNK)
-            kt_ref[:D_LATENT, cols] = keys[cols, :].T
-            kt_ref[D_LATENT:, cols] = rope_rows(ropes[chunk])
-
-    step = pl.program_id(0)
+        for i, k_ref in enumerate(k_refs):
+            cols = slice(i * CHUNK, (i + 1) * CHUNK)
+            kt_ref[:D_LATENT, cols] = k_ref[:CHUNK, :].T
+            kt_ref[D_LATENT:, cols] = key_ropes(k_ref)
+
     out_t = dot(kt_ref[:D_LATENT, :], probs_ref[step], NN).astype(BF16)
-    abs_t = dot(kt_ref[...], grads_ref[step], NN)
+    abs_t = dot(kt_ref[...], grads_ref[step], NN) * SCALE
     rope_t = abs_t[D_LATENT:, :]
     abs_t = abs_t[:D_LATENT, :].astype(BF16)
     queries = query_ref[...]
@@ -210,10 +236,11 @@
     own = own_ref[0]
     share = D_LATENT // CTX
     for position in range(CTX):
-        rows = pl.ds(pl.multiple_of((own ^ ctx_xor(position)) * share, share), share)
+        rows = pl.ds(pl.multiple_of((own ^ row_xor(position)) * share, share), share)
         out = send_ref if position >= CTX // 2 else keep_ref
-        out[position % (CTX // 2), 0] = w_ref[0, rows, :]
-        out[position % (CTX // 2), 1] = w_ref[1, rows, :]
+        lanes = pl.ds(pl.multiple_of(step * 2 * NOPE, 2 * NOPE), 2 * NOPE)
+        out[position % (CTX // 2), 0, :, lanes] = w_ref[0, rows, :]
+        out[position % (CTX // 2), 1, :, lanes] = w_ref[1, rows, :]
 
 
 def spread_sum(parts):
@@ -241,7 +268,6 @@
     own = lax.axis_index("ctx").astype(jnp.int32)
     vmem = pl.BlockSpec(memory_space=pltpu.VMEM)
     smem = pl.BlockSpec(memory_space=pltpu.SMEM)
-    hbm = pl.BlockSpec(memory_space=pl.ANY)
     total = BLOCKS * BLOCK
     half = (CTX // 2) * PACKED
     pair_cols = 2 * (NOPE + ROPE)
@@ -250,16 +276,15 @@
     turned = rope_key.T
     packed = jnp.concatenate([turned[g * ROPE_ROWS : (g + 1) * ROPE_ROWS] for g in range(rope_parts)], axis=1)
     keys = jnp.concatenate([latents, packed], axis=0)
-    got = swap_ctx(keys, 2)
-    keys = jnp.concatenate([keys, got], axis=0)
-    near = [keys]
-    for k in (2, 1, 3):
-        near.append(swap_ctx(keys, k << 2))
-    near = [near[0], near[2], near[1], near[3]]
-    far = []
-    for k in range(4):
-        far.append(swap_ctx(near[k], 1))
-    k_blocks = near + far
+    other = swap_ctx(keys, 2)
+    k_chunks = [None] * CTX
+    for z, chunk in enumerate((keys, other)):
+        near = [chunk]
+        for k in (1, 2, 3):
+            near.append(swap_ctx(chunk, k << 2))
+        for k in range(4):
+            k_chunks[4 * z + k] = near[k]
+            k_chunks[8 + 4 * z + k] = swap_ctx(near[k], 1)
 
     query_all, grad_lat, bias = pl.pallas_call(
         prep_kernel,
@@ -288,24 +313,41 @@
     )(own.reshape(1), group_order, *in_hbm(queries, up_key_weight, out_grad, up_value_weight))
 
     pair_shape = pltpu.VMEM((PAIRS, total, 2 * tok), BF16)
-    latent_shape = jax.ShapeDtypeStruct((half, D_LATENT), BF16)
+    latent_shape = pltpu.VMEM((half, D_LATENT), BF16)
+    early_chunks = [k_chunks[2 * kb + c] for kb in EARLY for c in range(2)]
+    late_chunks = [k_chunks[2 * kb + c] for kb in LATE for c in range(2)]
+    early = len(EARLY) * BLOCK
+    late = len(LATE) * BLOCK
+    early_parts = pl.pallas_call(
+        early_kernel,
+        grid=(PAIRS,),
+        out_shape=(
+            pltpu.VMEM((PAIRS, early, 2 * tok), BF16),
+            pltpu.VMEM((PAIRS, early, 2 * tok), F32),
+            pltpu.VMEM((PAIRS, 8, 2 * tok), F32),
+        ),
+        in_specs=[vmem] * (len(early_chunks) + 3),
+        out_specs=(vmem,) * 3,
+        scratch_shapes=[pltpu.VMEM((early, WIDTH), BF16)],
+        compiler_params=pltpu.CompilerParams(vmem_limit_bytes=16 << 20),
+        cost_estimate=cost(3_000_000_000, 10_000_000),
+        name="early",
+    )(*in_vmem(*early_chunks, query_all, grad_lat, bias))
     probs, grads, latent_send = pl.pallas_call(
         scores_kernel,
         grid=(PAIRS + 1,),
         out_shape=(pair_shape, pair_shape, latent_shape),
-        in_specs=[hbm] * BLOCKS + [vmem] * 3,
-        out_specs=(vmem, vmem, vmem),
+        in_specs=[vmem] * (len(late_chunks) + 6),
+        out_specs=(vmem,) * 3,
         scratch_shapes=[
-            pltpu.VMEM((total, WIDTH), BF16),
-            pltpu.VMEM((CTX, ROPE_ROWS, D_LATENT), BF16),
-            pltpu.VMEM((total, 2 * tok), F32),
-            pltpu.VMEM((total, 2 * tok), F32),
-            pltpu.SemaphoreType.DMA((2, CTX)),
+            pltpu.VMEM((late, WIDTH), BF16),
+            pltpu.VMEM((late, 2 * tok), BF16),
+            pltpu.VMEM((late, 2 * tok), F32),
         ],
-        compiler_params=pltpu.CompilerParams(vmem_limit_bytes=40 << 20),
-        cost_estimate=cost(8_000_000_000, 14_000_000),
+        compiler_params=pltpu.CompilerParams(vmem_limit_bytes=24 << 20),
+        cost_estimate=cost(6_000_000_000, 14_000_000),
         name="scores",
-    )(*k_blocks, query_all, grad_lat, bias)
+    )(*in_vmem(*late_chunks, query_all, grad_lat, bias, *early_parts))
 
     latent_got = swap_ctx(latent_send, 1)
 
@@ -317,42 +359,39 @@
         compiler_params=pltpu.CompilerParams(vmem_limit_bytes=24 << 20),
         cost_estimate=cost(2_300_000_000, 7_000_000),
         name="keep",
-    )(*in_vmem(probs, grads), query_all, grad_lat)
+    )(*in_vmem(probs, grads, query_all, grad_lat))
 
     share = D_LATENT // CTX
-    weight_shape = jax.ShapeDtypeStruct((CTX // 2, 2, share, heads * NOPE), BF16)
-    weight_spec = pl.BlockSpec((CTX // 2, 2, share, 2 * NOPE), lambda i: (0, 0, 0, i))
+    weight_shape = pltpu.VMEM((CTX // 2, 2, share, heads * NOPE), BF16)
     query_grad, weight_send, weight_keep = pl.pallas_call(
         weights_kernel,
         grid=(PAIRS,),
         out_shape=(jax.ShapeDtypeStruct(queries.shape, BF16), weight_shape, weight_shape),
         in_specs=[smem]
-        + [hbm] * BLOCKS
+        + [vmem] * (CTX + 2)
         + [
-            vmem,
-            vmem,
             pl.BlockSpec((tok, pair_cols), lambda i: (0, i)),
             pl.BlockSpec((tok, 2 * VDIM), lambda i: (0, i)),
             pl.BlockSpec((D_LATENT, 2 * NOPE), lambda i: (0, i)),
         ],
-        out_specs=(pl.BlockSpec((tok, pair_cols), lambda i: (0, i)), weight_spec, weight_spec),
+        out_specs=(pl.BlockSpec((tok, pair_cols), lambda i: (0, i)), vmem, vmem),
         scratch_shapes=[
-            pltpu.VMEM((total, D_LATENT), BF16),
-            pltpu.VMEM((CTX, ROPE_ROWS, D_LATENT), BF16),
             pltpu.VMEM((WIDTH, total), BF16),
             pltpu.VMEM((2, D_LATENT, 2 * NOPE), BF16),
-            pltpu.SemaphoreType.DMA((2, CTX)),
         ],
         compiler_params=pltpu.CompilerParams(vmem_limit_bytes=24 << 20),
         cost_estimate=cost(5_000_000_000, 14_000_000),
         name="weights",
-    )(own.reshape(1), *k_blocks, *in_vmem(probs, grads), *in_hbm(queries, out_grad, up_key_weight))
-
-    step = 2 * PACKED
+    )(own.reshape(1), *in_vmem(*k_chunks, probs, grads), *in_hbm(queries, out_grad, up_key_weight))
+
     pieces = [
-        spread_sum([latent_keep[k * step : (k + 1) * step], latent_got[k * step : (k + 1) * step]]).astype(BF16)
+        [
+            spread_sum([part[(4 * z + k) * PACKED : (4 * z + k + 1) * PACKED] for part in (latent_keep, latent_got)])
+            for z in range(2)
+        ]
         for k in range(4)
     ]
+    pieces = [jnp.concatenate(p, axis=0).astype(BF16) for p in pieces]
     got = [pieces[0]]
     for k in (2, 1, 3):
         got.append(swap_ctx(pieces[k], k << 2))

time: 117 us -> 105 us (0.90)
  Pallas kernels: 34 us -> 28.3 us
  waiting for transfers between devices: 43.4 us -> 39.4 us
    pallas_call x1, Pallas kernels: 14 us -> 8.1 us  [per_device(): pl.pallas_call(scores_kernel, grid=(PAIRS + 1,), out_shape=(pair_shape, p...]
    pallas_call x0 -> x1, Pallas kernels: none -> 4.25 us  [per_device(): pl.pallas_call(early_kernel, grid=(PAIRS,), out_shape=(pltpu.VMEM((PAIRS,...]
    pallas_call x1, Pallas kernels: 13.8 us -> 9.8 us  [per_device(): pl.pallas_call(weights_kernel, grid=(PAIRS,), out_shape=(jax.ShapeDtypeSt...]
    ppermute x3, waiting for transfers between devices: 2.75 us -> 0.38 us  [swap_head(): return lax.ppermute(value, 'head', [(i, i ^ mask) for i in range(HEAD)])]
    ppermute x18 -> x25, waiting for transfers between devices: 40.7 us -> 39 us  [swap_ctx(): return lax.ppermute(value, 'ctx', [(i, i ^ mask) for i in range(CTX)])]
    ppermute x18 -> x25, starting transfers between devices: 25.9 us -> 25.6 us  [swap_ctx(): return lax.ppermute(value, 'ctx', [(i, i ^ mask) for i in range(CTX)])]
  transfers between devices with their start and end apart: 21 -> 28, of which waited for: 12 -> 13; matrix products, arithmetic and copies ran while one was open for 2% -> 2% of each run, Pallas kernels for 17% -> 19%
where the time goes in v1:
time: 105 us
  waiting for transfers between devices  39.4 us (38%)
  starting transfers between devices  31.1 us (30%)
  Pallas kernels  28.3 us (27%)
  other arithmetic  4.14 us (4%)
  local copies, waits for them, and re-layouts  1.4 us (1%)
    ppermute x25, waiting for transfers between devices, swap_ctx(): return lax.ppermute(value, 'ctx', [(i, i ^ mask) for i in range(CTX)])  39 us
    ppermute x25, starting transfers between devices, swap_ctx(): return lax.ppermute(value, 'ctx', [(i, i ^ mask) for i in range(CTX)])  25.6 us
    pallas_call x1, Pallas kernels, per_device(): pl.pallas_call(weights_kernel, grid=(PAIRS,), out_shape=(jax.ShapeDtypeSt...  9.8 us
    pallas_call x1, Pallas kernels, per_device(): pl.pallas_call(scores_kernel, grid=(PAIRS + 1,), out_shape=(pair_shape, p...  8.1 us
    ppermute x3, starting transfers between devices, swap_head(): return lax.ppermute(value, 'head', [(i, i ^ mask) for i in range(HEAD)])  5.53 us
    pallas_call x1, Pallas kernels, per_device(): pl.pallas_call(early_kernel, grid=(PAIRS,), out_shape=(pltpu.VMEM((PAIRS,...  4.25 us
    pallas_call x1, Pallas kernels, per_device(): pl.pallas_call(prep_kernel, grid=(PAIRS,), out_shape=(jax.ShapeDtypeStruc...  3.26 us
    pallas_call x1, Pallas kernels, per_device(): pl.pallas_call(keep_kernel, out_shape=latent_shape, in_specs=[vmem] * 4,...  2.87 us
  transfers between devices with their start and end apart: 28, of which 13 were waited for; matrix products, arithmetic and copies ran while one was open for 2% of the time, Pallas kernels for 19%

profile of v1, /device:TPU:0, one launch (start us, length us, event | category | flops | bytes accessed | tf_op | source)
XLA Modules:
  0.0 105.1 jit_solution(15562825234573338411)
XLA Ops:
  0.6 0.7 fusion.1
  1.4 0.9 maximum_maximum_fusion.refs_0_.refs_1_
  2.3 4.1 %collective-permute-start.3 = (bf16[144,512]{1,0:T(8,128)(2,1)S(1)}, bf16[144,512]{1,0:T(8,128)(2,1)S(1)}, u32[]{:S(2)}, u32[]{:S(2)}) collective-permute-start(bf16[144,512]{1,0:T(8,128)(2,1)S(1)} %maximum_maximum_fusion.refs_0_.refs_1_), channel_id=1, source_target_pairs={{0,16},{8,24},{16,0},{24,8},{32,48},{40,56},{48,32},{56,40},{64,80... | collective-permute-start | bytes 442376 | tf_op jit(solution)/shard_map/ppermute | solution.py:38
  6.4 3.0 %collective-permute-start.2 = (bf16[144,512]{1,0:T(8,128)(2,1)S(1)}, bf16[144,512]{1,0:T(8,128)(2,1)S(1)}, u32[]{:S(2)}, u32[]{:S(2)}) collective-permute-start(bf16[144,512]{1,0:T(8,128)(2,1)S(1)} %maximum_maximum_fusion.refs_0_.refs_1_), channel_id=1, source_target_pairs={{0,96},{8,104},{16,112},{24,120},{32,64},{40,72},{48,80},{56,88},{... | collective-permute-start | bytes 442376 | tf_op jit(solution)/shard_map/ppermute | solution.py:38
  9.4 0.6 collective-permute-start.1
  10.0 0.5 collective-permute-start
  10.5 3.0 %collective-permute-start.6 = (bf16[144,512]{1,0:T(8,128)(2,1)S(1)}, bf16[144,512]{1,0:T(8,128)(2,1)S(1)}, u32[]{:S(2)}, u32[]{:S(2)}) collective-permute-start(bf16[144,512]{1,0:T(8,128)(2,1)S(1)} %collective-permute-done.3.refs_0_.refs_5_), channel_id=1, source_target_pairs={{0,96},{8,104},{16,112},{24,120},{32,64},{40,72},{48,80},{56,88},{... | collective-permute-start | bytes 442376 | tf_op jit(solution)/shard_map/ppermute | solution.py:38
  13.5 0.6 collective-permute-start.5
  14.1 2.8 %collective-permute-done.2.refs_3_.refs_4_ = bf16[144,512]{1,0:T(8,128)(2,1)S(1)} collective-permute-done((bf16[144,512]{1,0:T(8,128)(2,1)S(1)}, bf16[144,512]{1,0:T(8,128)(2,1)S(1)}, u32[]{:S(2)}, u32[]{:S(2)}) %collective-permute-start.2) | collective-permute-done | bytes 147488 | tf_op jit(solution)/shard_map/ppermute | solution.py:38
  16.9 0.5 collective-permute-start.4
  17.4 0.2 collective-permute-done.1.refs_2_.refs_3_
  17.6 0.7 collective-permute-done.refs_1_.refs_2_
  18.4 4.4 %collective-permute-done.6.refs_3_.refs_8_ = bf16[144,512]{1,0:T(8,128)(2,1)S(1)} collective-permute-done((bf16[144,512]{1,0:T(8,128)(2,1)S(1)}, bf16[144,512]{1,0:T(8,128)(2,1)S(1)}, u32[]{:S(2)}, u32[]{:S(2)}) %collective-permute-start.6) | collective-permute-done | bytes 147488 | tf_op jit(solution)/shard_map/ppermute | solution.py:38
  22.7 0.7 copy-done
  23.4 3.3 %prep.1 = (bf16[4,256,576]{2,1,0:T(8,128)(2,1)S(1)}, bf16[4,256,512]{2,1,0:T(8,128)(2,1)S(1)}, f32[2048,128]{1,0:T(8,128)S(1)}) custom-call(s32[1]{0:T(128)} %bitcast.own_ref.refs_0_, s32[32]{0:T(128)S(1)} %copy-done, bf16[128,1536]{1,0:T(8,128)(2,1)} %refs_19_.1, bf16[512,1024]{1,0:T(8,128)(2,1)} %refs_21_.1, bf16[128,1024]{1,0:T(8,128)(2,1)} %refs_20_.1, ...), custom_call_target="tpu_custom_call" | custom-call | flops 300000000 | bytes 10000000 | tf_op jit(solution)/shard_map/prep/pallas_call | solution.py:289
  26.7 0.6 collective-permute-start.11
  27.3 0.1 collective-permute-start.14
  27.4 0.4 collective-permute-start.13
  27.9 4.3 %early.1 = (bf16[4,1024,256]{2,1,0:T(8,128)(2,1)S(1)}, f32[4,1024,256]{2,1,0:T(8,128)S(1)}, f32[4,8,256]{2,1,0:T(8,128)S(1)}) custom-call(bf16[144,512]{1,0:T(8,128)(2,1)S(1)} %maximum_maximum_fusion.refs_0_.refs_1_, bf16[144,512]{1,0:T(8,128)(2,1)S(1)} %collective-permute-done.refs_1_.refs_2_, bf16[144,512]{1,0:T(8,128)(2,1)S(1)} %collective-permute-done.1.refs_2_.refs_3_, ...), custom_call_target="tpu_custom_call" | custom-call | flops 3000000000 | bytes 10000000 | tf_op jit(solution)/shard_map/early/pallas_call | solution.py:321
  32.2 8.1 %scores.1 = (bf16[4,2048,256]{2,1,0:T(8,128)(2,1)S(1)}, bf16[4,2048,256]{2,1,0:T(8,128)(2,1)S(1)}, bf16[1152,512]{1,0:T(8,128)(2,1)S(1)}) custom-call(bf16[144,512]{1,0:T(8,128)(2,1)S(1)} %collective-permute-done.3.refs_0_.refs_5_, bf16[144,512]{1,0:T(8,128)(2,1)S(1)} %collective-permute-done.4.refs_1_.refs_6_, ...), custom_call_target="tpu_custom_call" | custom-call | flops 6000000000 | bytes 14000000 | tf_op jit(solution)/shard_map/scores/pallas_call | solution.py:336
  40.3 0.5 collective-permute-start.15
  40.8 9.8 %weights.1 = (bf16[128,1536]{1,0:T(8,128)(2,1)}, bf16[8,2,32,1024]{3,2,1,0:T(8,128)(2,1)S(1)}, bf16[8,2,32,1024]{3,2,1,0:T(8,128)(2,1)S(1)}) custom-call(s32[1]{0:T(128)} %bitcast.own_ref.refs_0_, bf16[144,512]{1,0:T(8,128)(2,1)S(1)} %maximum_maximum_fusion.refs_0_.refs_1_, bf16[144,512]{1,0:T(8,128)(2,1)S(1)} %collective-permute-done.refs_1_.refs_2_, ...), custom_call_target="tpu_custom_call" | custom-call | flops 5000000000 | bytes 14000000 | tf_op jit(solution)/shard_map/weights/pallas_call | solution.py:366
  50.7 2.9 %keep.1 = bf16[1152,512]{1,0:T(8,128)(2,1)S(1)} custom-call(bf16[4,2048,256]{2,1,0:T(8,128)(2,1)S(1)} %get-tuple-element.23.refs_17_.probs_ref, bf16[4,2048,256]{2,1,0:T(8,128)(2,1)S(1)} %get-tuple-element.24.refs_18_.grads_ref, bf16[4,256,576]{2,1,0:T(8,128)(2,1)S(1)} %get-tuple-element.17.refs_8_.q_ref, ...), custom_call_target="tpu_custom_call" | custom-call | flops 2300000000 | bytes 7000000 | tf_op jit(solution)/shard_map/keep/pallas_call | solution.py:354
  53.6 0.3 add_convert_fusion.14
  53.9 0.5 collective-permute-start.17
  54.4 3.2 %collective-permute-start.18 = (bf16[288,512]{1,0:T(8,128)(2,1)S(1)}, bf16[288,512]{1,0:T(8,128)(2,1)S(1)}, u32[]{:S(2)}, u32[]{:S(2)}) collective-permute-start(bf16[288,512]{1,0:T(8,128)(2,1)S(1)} %pad_maximum_fusion.2), channel_id=1, source_target_pairs={{0,96},{8,104},{16,112},{24,120},{32,64},{40,72},{48,80},{56,88},{... | collective-permute-start | bytes 884744 | tf_op jit(solution)/shard_map/ppermute | solution.py:38
  57.7 1.5 %collective-permute-start.16 = (bf16[288,512]{1,0:T(8,128)(2,1)S(1)}, bf16[288,512]{1,0:T(8,128)(2,1)S(1)}, u32[]{:S(2)}, u32[]{:S(2)}) collective-permute-start(bf16[288,512]{1,0:T(8,128)(2,1)S(1)} %pad_maximum_fusion), channel_id=1, source_target_pairs={{0,64},{8,72},{16,80},{24,88},{32,96},{40,104},{48,112},{56,120},{... | collective-permute-start | bytes 884744 | tf_op jit(solution)/shard_map/ppermute | solution.py:38
  59.2 4.6 %collective-permute-done.17 = bf16[288,512]{1,0:T(8,128)(2,1)S(1)} collective-permute-done((bf16[288,512]{1,0:T(8,128)(2,1)S(1)}, bf16[288,512]{1,0:T(8,128)(2,1)S(1)}, u32[]{:S(2)}, u32[]{:S(2)}) %collective-permute-start.17) | collective-permute-done | bytes 294944 | tf_op jit(solution)/shard_map/ppermute | solution.py:38
  63.8 7.0 %collective-permute-done.18 = bf16[288,512]{1,0:T(8,128)(2,1)S(1)} collective-permute-done((bf16[288,512]{1,0:T(8,128)(2,1)S(1)}, bf16[288,512]{1,0:T(8,128)(2,1)S(1)}, u32[]{:S(2)}, u32[]{:S(2)}) %collective-permute-start.18) | collective-permute-done | bytes 294944 | tf_op jit(solution)/shard_map/ppermute | solution.py:38
  70.8 1.8 %collective-permute-done.16 = bf16[288,512]{1,0:T(8,128)(2,1)S(1)} collective-permute-done((bf16[288,512]{1,0:T(8,128)(2,1)S(1)}, bf16[288,512]{1,0:T(8,128)(2,1)S(1)}, u32[]{:S(2)}, u32[]{:S(2)}) %collective-permute-start.16) | collective-permute-done | bytes 294944 | tf_op jit(solution)/shard_map/ppermute | solution.py:38
  72.7 0.2 collective-permute-start.19
  72.9 6.7 %collective-permute-done.19 = bf16[144,512]{1,0:T(8,128)(2,1)S(1)} collective-permute-done((bf16[144,512]{1,0:T(8,128)(2,1)S(1)}, bf16[144,512]{1,0:T(8,128)(2,1)S(1)}, u32[]{:S(2)}, u32[]{:S(2)}) %collective-permute-start.19) | collective-permute-done | bytes 147488 | tf_op jit(solution)/shard_map/ppermute | solution.py:38
  79.6 0.1 add_convert_fusion.6
  79.7 1.1 %collective-permute-start.20 = (bf16[144,512]{1,0:T(8,128)(2,1)S(1)}, bf16[144,512]{1,0:T(8,128)(2,1)S(1)}, u32[]{:S(2)}, u32[]{:S(2)}) collective-permute-start(bf16[144,512]{1,0:T(8,128)(2,1)S(1)} %add_convert_fusion.6), channel_id=1, source_target_pairs={{0,1},{1,0},{2,3},{3,2},{4,5},{5,4},{6,7},{7,6},{8,9},{9,8},{10,11... | collective-permute-start | bytes 442376 | tf_op jit(solution)/shard_map/ppermute | solution.py:42
  80.8 0.4 add_convert_fusion.3
  81.2 2.0 %collective-permute-start.26 = (bf16[2,2,32,1024]{3,2,1,0:T(8,128)(2,1)S(1)}, bf16[2,2,32,1024]{3,2,1,0:T(8,128)(2,1)S(1)}, u32[]{:S(2)}, u32[]{:S(2)}) collective-permute-start(bf16[2,2,32,1024]{3,2,1,0:T(8,128)(2,1)S(1)} %get-tuple-element.36), channel_id=1, source_target_pairs={{0,96},{8,104},{16,112},{24,120},{32,64},{40,72},{48,80},{56,88},{... | collective-permute-start | bytes 786440 | tf_op jit(solution)/shard_map/ppermute | solution.py:38
  83.2 2.8 %collective-permute-start.24 = (bf16[2,2,32,1024]{3,2,1,0:T(8,128)(2,1)S(1)}, bf16[2,2,32,1024]{3,2,1,0:T(8,128)(2,1)S(1)}, u32[]{:S(2)}, u32[]{:S(2)}) collective-permute-start(bf16[2,2,32,1024]{3,2,1,0:T(8,128)(2,1)S(1)} %get-tuple-element.38), channel_id=1, source_target_pairs={{0,64},{8,72},{16,80},{24,88},{32,96},{40,104},{48,112},{56,120},{... | collective-permute-start | bytes 786440 | tf_op jit(solution)/shard_map/ppermute | solution.py:38
  86.1 1.6 %collective-permute-start.21 = (bf16[144,512]{1,0:T(8,128)(2,1)S(1)}, bf16[144,512]{1,0:T(8,128)(2,1)S(1)}, u32[]{:S(2)}, u32[]{:S(2)}) collective-permute-start(bf16[144,512]{1,0:T(8,128)(2,1)S(1)} %add_convert_fusion.5), channel_id=1, source_target_pairs={{0,2},{1,3},{2,0},{3,1},{4,6},{5,7},{6,4},{7,5},{8,10},{9,11},{10,... | collective-permute-start | bytes 442376 | tf_op jit(solution)/shard_map/ppermute | solution.py:42
  87.6 3.2 %collective-permute-done.26 = bf16[2,2,32,1024]{3,2,1,0:T(8,128)(2,1)S(1)} collective-permute-done((bf16[2,2,32,1024]{3,2,1,0:T(8,128)(2,1)S(1)}, bf16[2,2,32,1024]{3,2,1,0:T(8,128)(2,1)S(1)}, u32[]{:S(2)}, u32[]{:S(2)}) %collective-permute-start.26) | collective-permute-done | bytes 262176 | tf_op jit(solution)/shard_map/ppermute | solution.py:38
  90.8 1.6 %collective-permute-done.25 = bf16[2,2,32,1024]{3,2,1,0:T(8,128)(2,1)S(1)} collective-permute-done((bf16[2,2,32,1024]{3,2,1,0:T(8,128)(2,1)S(1)}, bf16[2,2,32,1024]{3,2,1,0:T(8,128)(2,1)S(1)}, u32[]{:S(2)}, u32[]{:S(2)}) %collective-permute-start.25) | collective-permute-done | bytes 262176 | tf_op jit(solution)/shard_map/ppermute | solution.py:38
  92.4 3.6 %collective-permute-done.24 = bf16[2,2,32,1024]{3,2,1,0:T(8,128)(2,1)S(1)} collective-permute-done((bf16[2,2,32,1024]{3,2,1,0:T(8,128)(2,1)S(1)}, bf16[2,2,32,1024]{3,2,1,0:T(8,128)(2,1)S(1)}, u32[]{:S(2)}, u32[]{:S(2)}) %collective-permute-start.24) | collective-permute-done | bytes 262176 | tf_op jit(solution)/shard_map/ppermute | solution.py:38
  96.0 1.2 %collective-permute-start.27 = (bf16[2,32,1024]{2,1,0:T(8,128)(2,1)S(1)}, bf16[2,32,1024]{2,1,0:T(8,128)(2,1)S(1)}, u32[]{:S(2)}, u32[]{:S(2)}) collective-permute-start(bf16[2,32,1024]{2,1,0:T(8,128)(2,1)S(1)} %fusion), channel_id=1, source_target_pairs={{0,16},{8,24},{16,0},{24,8},{32,48},{40,56},{48,32},{56,40},{64,80... | collective-permute-start | bytes 393224 | tf_op jit(solution)/shard_map/ppermute | solution.py:38
  97.3 2.9 %collective-permute-start.22 = (bf16[144,512]{1,0:T(8,128)(2,1)S(1)}, bf16[144,512]{1,0:T(8,128)(2,1)S(1)}, u32[]{:S(2)}, u32[]{:S(2)}) collective-permute-start(bf16[144,512]{1,0:T(8,128)(2,1)S(1)} %add_convert_fusion.4), channel_id=1, source_target_pairs={{0,6},{1,7},{2,4},{3,5},{4,2},{5,3},{6,0},{7,1},{8,14},{9,15},{10,... | collective-permute-start | bytes 442376 | tf_op jit(solution)/shard_map/ppermute | solution.py:42
  100.2 2.4 %collective-permute-done.27 = bf16[2,32,1024]{2,1,0:T(8,128)(2,1)S(1)} collective-permute-done((bf16[2,32,1024]{2,1,0:T(8,128)(2,1)S(1)}, bf16[2,32,1024]{2,1,0:T(8,128)(2,1)S(1)}, u32[]{:S(2)}, u32[]{:S(2)}) %collective-permute-start.27) | collective-permute-done | bytes 131104 | tf_op jit(solution)/shard_map/ppermute | solution.py:38
  102.6 0.8 convert_add_fusion.1
  103.4 0.4 collective-permute-done.22
  103.8 0.6 maximum_bitcast_fusion
  104.4 0.7 convert_add_fusion
  (31 shorter events, 0.6 us)
Async XLA Ops:
  2.3 8.2 %collective-permute-start.3 = (bf16[144,512]{1,0:T(8,128)(2,1)S(1)}, bf16[144,512]{1,0:T(8,128)(2,1)S(1)}, u32[]{:S(2)}, u32[]{:S(2)}) collective-permute-start(bf16[144,512]{1,0:T(8,128)(2,1)S(1)} %maximum_maximum_fusion.refs_0_.refs_1_), channel_id=1, source_target_pairs={{0,16},{8,24},{16,0},{24,8},{32,48},{40,56},{48,32},{56,40},{64,80... | collective-permute-start | bytes 442376 | tf_op jit(solution)/shard_map/ppermute | solution.py:38
  6.4 7.1 %collective-permute-start.7 = (bf16[144,512]{1,0:T(8,128)(2,1)S(1)}, bf16[144,512]{1,0:T(8,128)(2,1)S(1)}, u32[]{:S(2)}, u32[]{:S(2)}) collective-permute-start(bf16[144,512]{1,0:T(8,128)(2,1)S(1)} %maximum_maximum_fusion.refs_0_.refs_1_), channel_id=1, source_target_pairs={{0,8},{8,0},{16,24},{24,16},{32,40},{40,32},{48,56},{56,48},{64,72... | collective-permute-start | bytes 442376 | tf_op jit(solution)/shard_map/ppermute | solution.py:38
  6.4 10.6 %collective-permute-start.2 = (bf16[144,512]{1,0:T(8,128)(2,1)S(1)}, bf16[144,512]{1,0:T(8,128)(2,1)S(1)}, u32[]{:S(2)}, u32[]{:S(2)}) collective-permute-start(bf16[144,512]{1,0:T(8,128)(2,1)S(1)} %maximum_maximum_fusion.refs_0_.refs_1_), channel_id=1, source_target_pairs={{0,96},{8,104},{16,112},{24,120},{32,64},{40,72},{48,80},{56,88},{... | collective-permute-start | bytes 442376 | tf_op jit(solution)/shard_map/ppermute | solution.py:38
  9.4 8.3 %collective-permute-start.1 = (bf16[144,512]{1,0:T(8,128)(2,1)S(1)}, bf16[144,512]{1,0:T(8,128)(2,1)S(1)}, u32[]{:S(2)}, u32[]{:S(2)}) collective-permute-start(bf16[144,512]{1,0:T(8,128)(2,1)S(1)} %maximum_maximum_fusion.refs_0_.refs_1_), channel_id=1, source_target_pairs={{0,64},{8,72},{16,80},{24,88},{32,96},{40,104},{48,112},{56,120},{... | collective-permute-start | bytes 442376 | tf_op jit(solution)/shard_map/ppermute | solution.py:38
  10.0 8.4 %collective-permute-start = (bf16[144,512]{1,0:T(8,128)(2,1)S(1)}, bf16[144,512]{1,0:T(8,128)(2,1)S(1)}, u32[]{:S(2)}, u32[]{:S(2)}) collective-permute-start(bf16[144,512]{1,0:T(8,128)(2,1)S(1)} %maximum_maximum_fusion.refs_0_.refs_1_), channel_id=1, source_target_pairs={{0,32},{8,40},{16,48},{24,56},{32,0},{40,8},{48,16},{56,24},{64,96... | collective-permute-start | bytes 442376 | tf_op jit(solution)/shard_map/ppermute | solution.py:38
  10.5 12.3 %collective-permute-start.6 = (bf16[144,512]{1,0:T(8,128)(2,1)S(1)}, bf16[144,512]{1,0:T(8,128)(2,1)S(1)}, u32[]{:S(2)}, u32[]{:S(2)}) collective-permute-start(bf16[144,512]{1,0:T(8,128)(2,1)S(1)} %collective-permute-done.3.refs_0_.refs_5_), channel_id=1, source_target_pairs={{0,96},{8,104},{16,112},{24,120},{32,64},{40,72},{48,80},{56,88},{... | collective-permute-start | bytes 442376 | tf_op jit(solution)/shard_map/ppermute | solution.py:38
  13.5 13.2 %collective-permute-start.5 = (bf16[144,512]{1,0:T(8,128)(2,1)S(1)}, bf16[144,512]{1,0:T(8,128)(2,1)S(1)}, u32[]{:S(2)}, u32[]{:S(2)}) collective-permute-start(bf16[144,512]{1,0:T(8,128)(2,1)S(1)} %collective-permute-done.3.refs_0_.refs_5_), channel_id=1, source_target_pairs={{0,64},{8,72},{16,80},{24,88},{32,96},{40,104},{48,112},{56,120},{... | collective-permute-start | bytes 442376 | tf_op jit(solution)/shard_map/ppermute | solution.py:38
  16.9 10.3 %collective-permute-start.4 = (bf16[144,512]{1,0:T(8,128)(2,1)S(1)}, bf16[144,512]{1,0:T(8,128)(2,1)S(1)}, u32[]{:S(2)}, u32[]{:S(2)}) collective-permute-start(bf16[144,512]{1,0:T(8,128)(2,1)S(1)} %collective-permute-done.3.refs_0_.refs_5_), channel_id=1, source_target_pairs={{0,32},{8,40},{16,48},{24,56},{32,0},{40,8},{48,16},{56,24},{64,96... | collective-permute-start | bytes 442376 | tf_op jit(solution)/shard_map/ppermute | solution.py:38
  17.6 9.7 %collective-permute-start.10 = (bf16[144,512]{1,0:T(8,128)(2,1)S(1)}, bf16[144,512]{1,0:T(8,128)(2,1)S(1)}, u32[]{:S(2)}, u32[]{:S(2)}) collective-permute-start(bf16[144,512]{1,0:T(8,128)(2,1)S(1)} %collective-permute-done.2.refs_3_.refs_4_), channel_id=1, source_target_pairs={{0,8},{8,0},{16,24},{24,16},{32,40},{40,32},{48,56},{56,48},{64,72... | collective-permute-start | bytes 442376 | tf_op jit(solution)/shard_map/ppermute | solution.py:38
  18.4 9.4 %collective-permute-start.9 = (bf16[144,512]{1,0:T(8,128)(2,1)S(1)}, bf16[144,512]{1,0:T(8,128)(2,1)S(1)}, u32[]{:S(2)}, u32[]{:S(2)}) collective-permute-start(bf16[144,512]{1,0:T(8,128)(2,1)S(1)} %collective-permute-done.1.refs_2_.refs_3_), channel_id=1, source_target_pairs={{0,8},{8,0},{16,24},{24,16},{32,40},{40,32},{48,56},{56,48},{64,72... | collective-permute-start | bytes 442376 | tf_op jit(solution)/shard_map/ppermute | solution.py:38
  22.7 5.2 %collective-permute-start.8 = (bf16[144,512]{1,0:T(8,128)(2,1)S(1)}, bf16[144,512]{1,0:T(8,128)(2,1)S(1)}, u32[]{:S(2)}, u32[]{:S(2)}) collective-permute-start(bf16[144,512]{1,0:T(8,128)(2,1)S(1)} %collective-permute-done.refs_1_.refs_2_), channel_id=1, source_target_pairs={{0,8},{8,0},{16,24},{24,16},{32,40},{40,32},{48,56},{56,48},{64,72... | collective-permute-start | bytes 442376 | tf_op jit(solution)/shard_map/ppermute | solution.py:38
  22.7 0.7 copy-start
  26.7 5.5 %collective-permute-start.11 = (bf16[144,512]{1,0:T(8,128)(2,1)S(1)}, bf16[144,512]{1,0:T(8,128)(2,1)S(1)}, u32[]{:S(2)}, u32[]{:S(2)}) collective-permute-start(bf16[144,512]{1,0:T(8,128)(2,1)S(1)} %collective-permute-done.3.refs_0_.refs_5_), channel_id=1, source_target_pairs={{0,8},{8,0},{16,24},{24,16},{32,40},{40,32},{48,56},{56,48},{64,72... | collective-permute-start | bytes 442376 | tf_op jit(solution)/shard_map/ppermute | solution.py:38
  27.3 4.9 %collective-permute-start.14 = (bf16[144,512]{1,0:T(8,128)(2,1)S(1)}, bf16[144,512]{1,0:T(8,128)(2,1)S(1)}, u32[]{:S(2)}, u32[]{:S(2)}) collective-permute-start(bf16[144,512]{1,0:T(8,128)(2,1)S(1)} %collective-permute-done.6.refs_3_.refs_8_), channel_id=1, source_target_pairs={{0,8},{8,0},{16,24},{24,16},{32,40},{40,32},{48,56},{56,48},{64,72... | collective-permute-start | bytes 442376 | tf_op jit(solution)/shard_map/ppermute | solution.py:38
  27.4 4.8 %collective-permute-start.13 = (bf16[144,512]{1,0:T(8,128)(2,1)S(1)}, bf16[144,512]{1,0:T(8,128)(2,1)S(1)}, u32[]{:S(2)}, u32[]{:S(2)}) collective-permute-start(bf16[144,512]{1,0:T(8,128)(2,1)S(1)} %collective-permute-done.5.refs_2_.refs_7_), channel_id=1, source_target_pairs={{0,8},{8,0},{16,24},{24,16},{32,40},{40,32},{48,56},{56,48},{64,72... | collective-permute-start | bytes 442376 | tf_op jit(solution)/shard_map/ppermute | solution.py:38
  27.8 4.4 %collective-permute-start.12 = (bf16[144,512]{1,0:T(8,128)(2,1)S(1)}, bf16[144,512]{1,0:T(8,128)(2,1)S(1)}, u32[]{:S(2)}, u32[]{:S(2)}) collective-permute-start(bf16[144,512]{1,0:T(8,128)(2,1)S(1)} %collective-permute-done.4.refs_1_.refs_6_), channel_id=1, source_target_pairs={{0,8},{8,0},{16,24},{24,16},{32,40},{40,32},{48,56},{56,48},{64,72... | collective-permute-start | bytes 442376 | tf_op jit(solution)/shard_map/ppermute | solution.py:38
  40.3 13.3 %collective-permute-start.15 = (bf16[1152,512]{1,0:T(8,128)(2,1)S(1)}, bf16[1152,512]{1,0:T(8,128)(2,1)S(1)}, u32[]{:S(2)}, u32[]{:S(2)}) collective-permute-start(bf16[1152,512]{1,0:T(8,128)(2,1)S(1)} %get-tuple-element.26), channel_id=1, source_target_pairs={{0,8},{8,0},{16,24},{24,16},{32,40},{40,32},{48,56},{56,48},{64,72... | collective-permute-start | bytes 3538952 | tf_op jit(solution)/shard_map/ppermute | solution.py:38
  50.6 30.2 %collective-permute-start.23 = (bf16[8,2,32,1024]{3,2,1,0:T(8,128)(2,1)S(1)}, bf16[8,2,32,1024]{3,2,1,0:T(8,128)(2,1)S(1)}, u32[]{:S(2)}, u32[]{:S(2)}) collective-permute-start(bf16[8,2,32,1024]{3,2,1,0:T(8,128)(2,1)S(1)} %get-tuple-element.28), channel_id=1, source_target_pairs={{0,8},{8,0},{16,24},{24,16},{32,40},{40,32},{48,56},{56,48},{64,72... | collective-permute-start | bytes 3145736 | tf_op jit(solution)/shard_map/ppermute | solution.py:38
  53.9 10.0 %collective-permute-start.17 = (bf16[288,512]{1,0:T(8,128)(2,1)S(1)}, bf16[288,512]{1,0:T(8,128)(2,1)S(1)}, u32[]{:S(2)}, u32[]{:S(2)}) collective-permute-start(bf16[288,512]{1,0:T(8,128)(2,1)S(1)} %pad_maximum_fusion.1), channel_id=1, source_target_pairs={{0,32},{8,40},{16,48},{24,56},{32,0},{40,8},{48,16},{56,24},{64,96... | collective-permute-start | bytes 884744 | tf_op jit(solution)/shard_map/ppermute | solution.py:38
  54.4 16.4 %collective-permute-start.18 = (bf16[288,512]{1,0:T(8,128)(2,1)S(1)}, bf16[288,512]{1,0:T(8,128)(2,1)S(1)}, u32[]{:S(2)}, u32[]{:S(2)}) collective-permute-start(bf16[288,512]{1,0:T(8,128)(2,1)S(1)} %pad_maximum_fusion.2), channel_id=1, source_target_pairs={{0,96},{8,104},{16,112},{24,120},{32,64},{40,72},{48,80},{56,88},{... | collective-permute-start | bytes 884744 | tf_op jit(solution)/shard_map/ppermute | solution.py:38
  57.7 14.9 %collective-permute-start.16 = (bf16[288,512]{1,0:T(8,128)(2,1)S(1)}, bf16[288,512]{1,0:T(8,128)(2,1)S(1)}, u32[]{:S(2)}, u32[]{:S(2)}) collective-permute-start(bf16[288,512]{1,0:T(8,128)(2,1)S(1)} %pad_maximum_fusion), channel_id=1, source_target_pairs={{0,64},{8,72},{16,80},{24,88},{32,96},{40,104},{48,112},{56,120},{... | collective-permute-start | bytes 884744 | tf_op jit(solution)/shard_map/ppermute | solution.py:38
  72.7 6.9 %collective-permute-start.19 = (bf16[144,512]{1,0:T(8,128)(2,1)S(1)}, bf16[144,512]{1,0:T(8,128)(2,1)S(1)}, u32[]{:S(2)}, u32[]{:S(2)}) collective-permute-start(bf16[144,512]{1,0:T(8,128)(2,1)S(1)} %add_convert_fusion.7), channel_id=1, source_target_pairs={{0,16},{8,24},{16,0},{24,8},{32,48},{40,56},{48,32},{56,40},{64,80... | collective-permute-start | bytes 442376 | tf_op jit(solution)/shard_map/ppermute | solution.py:38
  79.7 6.3 %collective-permute-start.20 = (bf16[144,512]{1,0:T(8,128)(2,1)S(1)}, bf16[144,512]{1,0:T(8,128)(2,1)S(1)}, u32[]{:S(2)}, u32[]{:S(2)}) collective-permute-start(bf16[144,512]{1,0:T(8,128)(2,1)S(1)} %add_convert_fusion.6), channel_id=1, source_target_pairs={{0,1},{1,0},{2,3},{3,2},{4,5},{5,4},{6,7},{7,6},{8,9},{9,8},{10,11... | collective-permute-start | bytes 442376 | tf_op jit(solution)/shard_map/ppermute | solution.py:42
  81.2 9.6 %collective-permute-start.26 = (bf16[2,2,32,1024]{3,2,1,0:T(8,128)(2,1)S(1)}, bf16[2,2,32,1024]{3,2,1,0:T(8,128)(2,1)S(1)}, u32[]{:S(2)}, u32[]{:S(2)}) collective-permute-start(bf16[2,2,32,1024]{3,2,1,0:T(8,128)(2,1)S(1)} %get-tuple-element.36), channel_id=1, source_target_pairs={{0,96},{8,104},{16,112},{24,120},{32,64},{40,72},{48,80},{56,88},{... | collective-permute-start | bytes 786440 | tf_op jit(solution)/shard_map/ppermute | solution.py:38
  83.2 9.2 %collective-permute-start.25 = (bf16[2,2,32,1024]{3,2,1,0:T(8,128)(2,1)S(1)}, bf16[2,2,32,1024]{3,2,1,0:T(8,128)(2,1)S(1)}, u32[]{:S(2)}, u32[]{:S(2)}) collective-permute-start(bf16[2,2,32,1024]{3,2,1,0:T(8,128)(2,1)S(1)} %get-tuple-element.37), channel_id=1, source_target_pairs={{0,32},{8,40},{16,48},{24,56},{32,0},{40,8},{48,16},{56,24},{64,96... | collective-permute-start | bytes 786440 | tf_op jit(solution)/shard_map/ppermute | solution.py:38
  83.2 12.7 %collective-permute-start.24 = (bf16[2,2,32,1024]{3,2,1,0:T(8,128)(2,1)S(1)}, bf16[2,2,32,1024]{3,2,1,0:T(8,128)(2,1)S(1)}, u32[]{:S(2)}, u32[]{:S(2)}) collective-permute-start(bf16[2,2,32,1024]{3,2,1,0:T(8,128)(2,1)S(1)} %get-tuple-element.38), channel_id=1, source_target_pairs={{0,64},{8,72},{16,80},{24,88},{32,96},{40,104},{48,112},{56,120},{... | collective-permute-start | bytes 786440 | tf_op jit(solution)/shard_map/ppermute | solution.py:38
  86.1 11.2 %collective-permute-start.21 = (bf16[144,512]{1,0:T(8,128)(2,1)S(1)}, bf16[144,512]{1,0:T(8,128)(2,1)S(1)}, u32[]{:S(2)}, u32[]{:S(2)}) collective-permute-start(bf16[144,512]{1,0:T(8,128)(2,1)S(1)} %add_convert_fusion.5), channel_id=1, source_target_pairs={{0,2},{1,3},{2,0},{3,1},{4,6},{5,7},{6,4},{7,5},{8,10},{9,11},{10,... | collective-permute-start | bytes 442376 | tf_op jit(solution)/shard_map/ppermute | solution.py:42
  96.0 6.6 %collective-permute-start.27 = (bf16[2,32,1024]{2,1,0:T(8,128)(2,1)S(1)}, bf16[2,32,1024]{2,1,0:T(8,128)(2,1)S(1)}, u32[]{:S(2)}, u32[]{:S(2)}) collective-permute-start(bf16[2,32,1024]{2,1,0:T(8,128)(2,1)S(1)} %fusion), channel_id=1, source_target_pairs={{0,16},{8,24},{16,0},{24,8},{32,48},{40,56},{48,32},{56,40},{64,80... | collective-permute-start | bytes 393224 | tf_op jit(solution)/shard_map/ppermute | solution.py:38
  97.3 6.4 %collective-permute-start.22 = (bf16[144,512]{1,0:T(8,128)(2,1)S(1)}, bf16[144,512]{1,0:T(8,128)(2,1)S(1)}, u32[]{:S(2)}, u32[]{:S(2)}) collective-permute-start(bf16[144,512]{1,0:T(8,128)(2,1)S(1)} %add_convert_fusion.4), channel_id=1, source_target_pairs={{0,6},{1,7},{2,4},{3,5},{4,2},{5,3},{6,0},{7,1},{8,14},{9,15},{10,... | collective-permute-start | bytes 442376 | tf_op jit(solution)/shard_map/ppermute | solution.py:42

commit v2 on v1

--- a/solution.py
+++ b/solution.py
@@ -42,6 +42,11 @@
     return lax.ppermute(value, "head", [(i, i ^ mask) for i in range(HEAD)])
 
 
+def swap_both(value, ctx_mask, head_mask):
+    mask = ctx_mask * HEAD + head_mask
+    return lax.ppermute(value, ("ctx", "head"), [(i, i ^ mask) for i in range(CTX * HEAD)])
+
+
 def dot(a, b, dims):
     return lax.dot_general(a, b, (dims, ((), ())), preferred_element_type=F32)
 
@@ -57,6 +62,7 @@
 ROPE_ROWS = 16
 PACKED = CHUNK + ROPE_ROWS
 LANES = 128
+PAIR_COLS = 2 * (NOPE + ROPE)
 TILE = 64
 EARLY = (0, 1, 4, 5)
 LATE = (2, 3, 6, 7)
@@ -68,6 +74,12 @@
 
 def rope_rows(packed):
     return jnp.concatenate([packed[:, g * LANES : (g + 1) * LANES] for g in range(ROPE // ROPE_ROWS)], axis=0)
+
+
+def pack_kernel(latents_ref, turned_ref, out_ref):
+    out_ref[:CHUNK, :] = latents_ref[...]
+    for g in range(ROPE // ROPE_ROWS):
+        out_ref[CHUNK:, g * LANES : (g + 1) * LANES] = turned_ref[g * ROPE_ROWS : (g + 1) * ROPE_ROWS, :]
 
 
 def prep_kernel(own_ref, order_ref, query_ref, up_key_ref, out_grad_ref, up_value_ref, q_ref, gl_ref, bias_ref):
@@ -222,15 +234,18 @@
     abs_t = dot(kt_ref[...], grads_ref[step], NN) * SCALE
     rope_t = abs_t[D_LATENT:, :]
     abs_t = abs_t[:D_LATENT, :].astype(BF16)
-    queries = query_ref[...]
+    queries = query_ref[:, pl.ds(pl.multiple_of(step * PAIR_COLS, PAIR_COLS), PAIR_COLS)]
+    lanes = pl.ds(pl.multiple_of(step * 2 * NOPE, 2 * NOPE), 2 * NOPE)
+    grad_out = out_grad_ref[:, lanes]
+    up_key = up_key_ref[:, lanes]
     pieces = []
     for h in range(2):
         cols = slice(h * NOPE, (h + 1) * NOPE)
         first = h * (NOPE + ROPE)
         nope = queries[:, first : first + NOPE]
         w_ref[0, :, cols] = dot(abs_t[:, cols], nope, NN).astype(BF16)
-        w_ref[1, :, cols] = dot(out_t[:, cols], out_grad_ref[:, cols], NN).astype(BF16)
-        pieces.append(dot(abs_t[:, cols], up_key_ref[:, cols], TN))
+        w_ref[1, :, cols] = dot(out_t[:, cols], grad_out[:, cols], NN).astype(BF16)
+        pieces.append(dot(abs_t[:, cols], up_key[:, cols], TN))
         pieces.append(rope_t[:, cols].T)
     query_grad_ref[...] = jnp.concatenate(pieces, axis=1).astype(BF16)
     own = own_ref[0]
@@ -238,7 +253,6 @@
     for position in range(CTX):
         rows = pl.ds(pl.multiple_of((own ^ row_xor(position)) * share, share), share)
         out = send_ref if position >= CTX // 2 else keep_ref
-        lanes = pl.ds(pl.multiple_of(step * 2 * NOPE, 2 * NOPE), 2 * NOPE)
         out[position % (CTX // 2), 0, :, lanes] = w_ref[0, rows, :]
         out[position % (CTX // 2), 1, :, lanes] = w_ref[1, rows, :]
 
@@ -273,9 +287,14 @@
     pair_cols = 2 * (NOPE + ROPE)
     rope_parts = ROPE // ROPE_ROWS
 
-    turned = rope_key.T
-    packed = jnp.concatenate([turned[g * ROPE_ROWS : (g + 1) * ROPE_ROWS] for g in range(rope_parts)], axis=1)
-    keys = jnp.concatenate([latents, packed], axis=0)
+    keys = pl.pallas_call(
+        pack_kernel,
+        out_shape=pltpu.VMEM((PACKED, D_LATENT), BF16),
+        in_specs=[vmem] * 2,
+        out_specs=vmem,
+        compiler_params=pltpu.CompilerParams(vmem_limit_bytes=4 << 20),
+        name="pack",
+    )(*in_hbm(latents, rope_key.T))
     other = swap_ctx(keys, 2)
     k_chunks = [None] * CTX
     for z, chunk in enumerate((keys, other)):
@@ -310,7 +329,7 @@
         compiler_params=pltpu.CompilerParams(vmem_limit_bytes=8 << 20),
         cost_estimate=cost(300_000_000, 10_000_000),
         name="prep",
-    )(own.reshape(1), group_order, *in_hbm(queries, up_key_weight, out_grad, up_value_weight))
+    )(own.reshape(1), *in_hbm(group_order, queries, up_key_weight, out_grad, up_value_weight))
 
     pair_shape = pltpu.VMEM((PAIRS, total, 2 * tok), BF16)
     latent_shape = pltpu.VMEM((half, D_LATENT), BF16)
@@ -370,9 +389,9 @@
         in_specs=[smem]
         + [vmem] * (CTX + 2)
         + [
-            pl.BlockSpec((tok, pair_cols), lambda i: (0, i)),
-            pl.BlockSpec((tok, 2 * VDIM), lambda i: (0, i)),
-            pl.BlockSpec((D_LATENT, 2 * NOPE), lambda i: (0, i)),
+            vmem,
+            vmem,
+            vmem,
         ],
         out_specs=(pl.BlockSpec((tok, pair_cols), lambda i: (0, i)), vmem, vmem),
         scratch_shapes=[
@@ -382,7 +401,7 @@
         compiler_params=pltpu.CompilerParams(vmem_limit_bytes=24 << 20),
         cost_estimate=cost(5_000_000_000, 14_000_000),
         name="weights",
-    )(own.reshape(1), *in_vmem(*k_chunks, probs, grads), *in_hbm(queries, out_grad, up_key_weight))
+    )(own.reshape(1), *in_vmem(*k_chunks, probs, grads, queries, out_grad, up_key_weight))
 
     pieces = [
         [
@@ -396,10 +415,12 @@
     for k in (2, 1, 3):
         got.append(swap_ctx(pieces[k], k << 2))
     other = spread_sum([g[PACKED:] for g in got]).astype(BF16)
-    other = swap_ctx(other, 2)
-    mine = spread_sum([g[:PACKED] for g in got] + [other]).astype(BF16)
-    other = swap_head(mine, 1)
-    mine = spread_sum([mine, other]).astype(BF16)
+    mine = spread_sum([g[:PACKED] for g in got]).astype(BF16)
+    first = swap_ctx(other, 2)
+    second = swap_both(other, 2, 1)
+    third = swap_head(mine, 1)
+    mine = spread_sum([mine, first, second, third])
+    mine = mine.astype(BF16)
     other = swap_head(mine, 2)
     mine = spread_sum([mine, other]).astype(BF16)
     other = swap_head(mine, 6)

time: 105 us -> 99.3 us (0.946)
  waiting for transfers between devices: 39.4 us -> 34.1 us
  starting transfers between devices: 31.1 us -> 33.1 us
  local copies, waits for them, and re-layouts: 1.4 us -> 0.02 us
    ppermute x25, waiting for transfers between devices: 39 us -> 30.3 us  [swap_ctx(): return lax.ppermute(value, 'ctx', [(i, i ^ mask) for i in range(CTX)])]
    ppermute x0 -> x1, waiting for transfers between devices: none -> 3.18 us  [swap_both(): lax.ppermute(value, ('ctx', 'head'), [(i, i ^ mask) for i in range(CTX *...]
    ppermute x25, starting transfers between devices: 25.6 us -> 26.9 us  [swap_ctx(): return lax.ppermute(value, 'ctx', [(i, i ^ mask) for i in range(CTX)])]
  transfers between devices with their start and end apart: 28 -> 29, of which waited for: 13 -> 12; matrix products, arithmetic and copies ran while one was open for 2% -> 2% of each run, Pallas kernels for 19% -> 19%
where the time goes in v2:
time: 99.3 us; the launch traced here: 99.2 us
  waiting for transfers between devices  34.1 us (34%)
  starting transfers between devices  33.1 us (33%)
  Pallas kernels  27.9 us (28%)
  other arithmetic  3.23 us (3%)
    ppermute x25, waiting for transfers between devices, swap_ctx(): return lax.ppermute(value, 'ctx', [(i, i ^ mask) for i in range(CTX)])  30.3 us
    ppermute x25, starting transfers between devices, swap_ctx(): return lax.ppermute(value, 'ctx', [(i, i ^ mask) for i in range(CTX)])  26.9 us
    pallas_call x1, Pallas kernels, per_device(): pl.pallas_call(weights_kernel, grid=(PAIRS,), out_shape=(jax.ShapeDtypeSt...  8.77 us
    pallas_call x1, Pallas kernels, per_device(): pl.pallas_call(scores_kernel, grid=(PAIRS + 1,), out_shape=(pair_shape, p...  7.94 us
    ppermute x3, starting transfers between devices, swap_head(): return lax.ppermute(value, 'head', [(i, i ^ mask) for i in range(HEAD)])  5.42 us
    pallas_call x1, Pallas kernels, per_device(): pl.pallas_call(early_kernel, grid=(PAIRS,), out_shape=(pltpu.VMEM((PAIRS,...  4.12 us
    pallas_call x1, Pallas kernels, per_device(): pl.pallas_call(prep_kernel, grid=(PAIRS,), out_shape=(jax.ShapeDtypeStruc...  3.26 us
    ppermute x1, waiting for transfers between devices, swap_both(): lax.ppermute(value, ('ctx', 'head'), [(i, i ^ mask) for i in range(CTX *...  3.18 us
  transfers between devices with their start and end apart: 29, of which 12 were waited for; matrix products, arithmetic and copies ran while one was open for 2% of the time, Pallas kernels for 19%

profile of v2, /device:TPU:0, one launch (start us, length us, event | category | flops | bytes accessed | tf_op | source)
XLA Modules:
  0.0 99.2 jit_solution(16000368997606211931)
XLA Ops:
  0.6 0.9 pack.1.refs_0_.refs_1_
  1.6 4.1 %collective-permute-start.3 = (bf16[144,512]{1,0:T(8,128)(2,1)S(1)}, bf16[144,512]{1,0:T(8,128)(2,1)S(1)}, u32[]{:S(2)}, u32[]{:S(2)}) collective-permute-start(bf16[144,512]{1,0:T(8,128)(2,1)S(1)} %pack.1.refs_0_.refs_1_), channel_id=1, source_target_pairs={{0,16},{8,24},{16,0},{24,8},{32,48},{40,56},{48,32},{56,40},{64,80... | collective-permute-start | bytes 442376 | tf_op jit(solution)/shard_map/ppermute | solution.py:38
  5.6 3.0 %collective-permute-start.2 = (bf16[144,512]{1,0:T(8,128)(2,1)S(1)}, bf16[144,512]{1,0:T(8,128)(2,1)S(1)}, u32[]{:S(2)}, u32[]{:S(2)}) collective-permute-start(bf16[144,512]{1,0:T(8,128)(2,1)S(1)} %pack.1.refs_0_.refs_1_), channel_id=1, source_target_pairs={{0,96},{8,104},{16,112},{24,120},{32,64},{40,72},{48,80},{56,88},{... | collective-permute-start | bytes 442376 | tf_op jit(solution)/shard_map/ppermute | solution.py:38
  8.6 0.6 collective-permute-start.1
  9.3 0.5 collective-permute-start
  9.7 3.0 %collective-permute-start.6 = (bf16[144,512]{1,0:T(8,128)(2,1)S(1)}, bf16[144,512]{1,0:T(8,128)(2,1)S(1)}, u32[]{:S(2)}, u32[]{:S(2)}) collective-permute-start(bf16[144,512]{1,0:T(8,128)(2,1)S(1)} %collective-permute-done.3.refs_0_.refs_5_), channel_id=1, source_target_pairs={{0,96},{8,104},{16,112},{24,120},{32,64},{40,72},{48,80},{56,88},{... | collective-permute-start | bytes 442376 | tf_op jit(solution)/shard_map/ppermute | solution.py:38
  12.7 0.6 collective-permute-start.5
  13.4 2.8 %collective-permute-done.2.refs_3_.refs_4_ = bf16[144,512]{1,0:T(8,128)(2,1)S(1)} collective-permute-done((bf16[144,512]{1,0:T(8,128)(2,1)S(1)}, bf16[144,512]{1,0:T(8,128)(2,1)S(1)}, u32[]{:S(2)}, u32[]{:S(2)}) %collective-permute-start.2) | collective-permute-done | bytes 147488 | tf_op jit(solution)/shard_map/ppermute | solution.py:38
  16.2 0.5 collective-permute-start.4
  16.7 0.2 collective-permute-done.1.refs_2_.refs_3_
  16.9 0.7 collective-permute-done.refs_1_.refs_2_
  17.6 4.4 %collective-permute-done.6.refs_3_.refs_8_ = bf16[144,512]{1,0:T(8,128)(2,1)S(1)} collective-permute-done((bf16[144,512]{1,0:T(8,128)(2,1)S(1)}, bf16[144,512]{1,0:T(8,128)(2,1)S(1)}, u32[]{:S(2)}, u32[]{:S(2)}) %collective-permute-start.6) | collective-permute-done | bytes 147488 | tf_op jit(solution)/shard_map/ppermute | solution.py:38
  22.0 3.3 %prep.1 = (bf16[4,256,576]{2,1,0:T(8,128)(2,1)S(1)}, bf16[4,256,512]{2,1,0:T(8,128)(2,1)S(1)}, f32[2048,128]{1,0:T(8,128)S(1)}) custom-call(s32[1]{0:T(128)} %bitcast.own_ref.refs_0_, s32[32]{0:T(128)} %order_ref.1, bf16[128,1536]{1,0:T(8,128)(2,1)} %refs_19_.1, bf16[512,1024]{1,0:T(8,128)(2,1)} %refs_21_.1, bf16[128,1024]{1,0:T(8,128)(2,1)} %refs_20_.1, ...), custom_call_target="tpu_custom_call" | custom-call | flops 300000000 | bytes 10000000 | tf_op jit(solution)/shard_map/prep/pallas_call | solution.py:308
  25.3 0.6 collective-permute-start.11
  25.9 0.1 collective-permute-start.14
  26.0 0.4 collective-permute-start.13
  26.4 0.1 collective-permute-start.12
  26.5 4.1 %early.1 = (bf16[4,1024,256]{2,1,0:T(8,128)(2,1)S(1)}, f32[4,1024,256]{2,1,0:T(8,128)S(1)}, f32[4,8,256]{2,1,0:T(8,128)S(1)}) custom-call(bf16[144,512]{1,0:T(8,128)(2,1)S(1)} %pack.1.refs_0_.refs_1_, bf16[144,512]{1,0:T(8,128)(2,1)S(1)} %collective-permute-done.refs_1_.refs_2_, bf16[144,512]{1,0:T(8,128)(2,1)S(1)} %collective-permute-done.1.refs_2_.refs_3_, ...), custom_call_target="tpu_custom_call" | custom-call | flops 3000000000 | bytes 10000000 | tf_op jit(solution)/shard_map/early/pallas_call | solution.py:340
  30.7 7.9 %scores.1 = (bf16[4,2048,256]{2,1,0:T(8,128)(2,1)S(1)}, bf16[4,2048,256]{2,1,0:T(8,128)(2,1)S(1)}, bf16[1152,512]{1,0:T(8,128)(2,1)S(1)}) custom-call(bf16[144,512]{1,0:T(8,128)(2,1)S(1)} %collective-permute-done.3.refs_0_.refs_5_, bf16[144,512]{1,0:T(8,128)(2,1)S(1)} %collective-permute-done.4.refs_1_.refs_6_, ...), custom_call_target="tpu_custom_call" | custom-call | flops 6000000000 | bytes 14000000 | tf_op jit(solution)/shard_map/scores/pallas_call | solution.py:355
  38.6 0.5 collective-permute-start.15
  39.1 8.8 %weights.1 = (bf16[128,1536]{1,0:T(8,128)(2,1)}, bf16[8,2,32,1024]{3,2,1,0:T(8,128)(2,1)S(1)}, bf16[8,2,32,1024]{3,2,1,0:T(8,128)(2,1)S(1)}) custom-call(s32[1]{0:T(128)} %bitcast.own_ref.refs_0_, bf16[144,512]{1,0:T(8,128)(2,1)S(1)} %pack.1.refs_0_.refs_1_, bf16[144,512]{1,0:T(8,128)(2,1)S(1)} %collective-permute-done.refs_1_.refs_2_, ...), custom_call_target="tpu_custom_call" | custom-call | flops 5000000000 | bytes 14000000 | tf_op jit(solution)/shard_map/weights/pallas_call | solution.py:385
  47.9 0.1 collective-permute-start.24
  48.0 2.9 %keep.1 = bf16[1152,512]{1,0:T(8,128)(2,1)S(1)} custom-call(bf16[4,2048,256]{2,1,0:T(8,128)(2,1)S(1)} %get-tuple-element.23.refs_17_.probs_ref, bf16[4,2048,256]{2,1,0:T(8,128)(2,1)S(1)} %get-tuple-element.24.refs_18_.grads_ref, bf16[4,256,576]{2,1,0:T(8,128)(2,1)S(1)} %get-tuple-element.17.refs_8_.q_ref, ...), custom_call_target="tpu_custom_call" | custom-call | flops 2300000000 | bytes 7000000 | tf_op jit(solution)/shard_map/keep/pallas_call | solution.py:373
  50.9 0.3 add_convert_fusion.14
  51.2 0.5 collective-permute-start.17
  51.8 3.2 %collective-permute-start.18 = (bf16[288,512]{1,0:T(8,128)(2,1)S(1)}, bf16[288,512]{1,0:T(8,128)(2,1)S(1)}, u32[]{:S(2)}, u32[]{:S(2)}) collective-permute-start(bf16[288,512]{1,0:T(8,128)(2,1)S(1)} %pad_maximum_fusion.2), channel_id=1, source_target_pairs={{0,96},{8,104},{16,112},{24,120},{32,64},{40,72},{48,80},{56,88},{... | collective-permute-start | bytes 884744 | tf_op jit(solution)/shard_map/ppermute | solution.py:38
  55.0 1.5 %collective-permute-start.16 = (bf16[288,512]{1,0:T(8,128)(2,1)S(1)}, bf16[288,512]{1,0:T(8,128)(2,1)S(1)}, u32[]{:S(2)}, u32[]{:S(2)}) collective-permute-start(bf16[288,512]{1,0:T(8,128)(2,1)S(1)} %pad_maximum_fusion), channel_id=1, source_target_pairs={{0,64},{8,72},{16,80},{24,88},{32,96},{40,104},{48,112},{56,120},{... | collective-permute-start | bytes 884744 | tf_op jit(solution)/shard_map/ppermute | solution.py:38
  56.6 4.6 %collective-permute-done.17 = bf16[288,512]{1,0:T(8,128)(2,1)S(1)} collective-permute-done((bf16[288,512]{1,0:T(8,128)(2,1)S(1)}, bf16[288,512]{1,0:T(8,128)(2,1)S(1)}, u32[]{:S(2)}, u32[]{:S(2)}) %collective-permute-start.17) | collective-permute-done | bytes 294944 | tf_op jit(solution)/shard_map/ppermute | solution.py:38
  61.2 7.0 %collective-permute-done.18 = bf16[288,512]{1,0:T(8,128)(2,1)S(1)} collective-permute-done((bf16[288,512]{1,0:T(8,128)(2,1)S(1)}, bf16[288,512]{1,0:T(8,128)(2,1)S(1)}, u32[]{:S(2)}, u32[]{:S(2)}) %collective-permute-start.18) | collective-permute-done | bytes 294944 | tf_op jit(solution)/shard_map/ppermute | solution.py:38
  68.2 1.8 %collective-permute-done.16 = bf16[288,512]{1,0:T(8,128)(2,1)S(1)} collective-permute-done((bf16[288,512]{1,0:T(8,128)(2,1)S(1)}, bf16[288,512]{1,0:T(8,128)(2,1)S(1)}, u32[]{:S(2)}, u32[]{:S(2)}) %collective-permute-start.16) | collective-permute-done | bytes 294944 | tf_op jit(solution)/shard_map/ppermute | solution.py:38
  70.0 0.2 add_convert_fusion.6
  70.2 0.8 collective-permute-start.20
  70.9 2.4 %collective-permute-start.19 = (bf16[144,512]{1,0:T(8,128)(2,1)S(1)}, bf16[144,512]{1,0:T(8,128)(2,1)S(1)}, u32[]{:S(2)}, u32[]{:S(2)}) collective-permute-start(bf16[144,512]{1,0:T(8,128)(2,1)S(1)} %get-tuple-element.29), channel_id=1, source_target_pairs={{0,16},{8,24},{16,0},{24,8},{32,48},{40,56},{48,32},{56,40},{64,80... | collective-permute-start | bytes 442376 | tf_op jit(solution)/shard_map/ppermute | solution.py:38
  73.3 1.0 %collective-permute-start.21 = (bf16[144,512]{1,0:T(8,128)(2,1)S(1)}, bf16[144,512]{1,0:T(8,128)(2,1)S(1)}, u32[]{:S(2)}, u32[]{:S(2)}) collective-permute-start(bf16[144,512]{1,0:T(8,128)(2,1)S(1)} %get-tuple-element.30), channel_id=1, source_target_pairs={{0,1},{1,0},{2,3},{3,2},{4,5},{5,4},{6,7},{7,6},{8,9},{9,8},{10,11... | collective-permute-start | bytes 442376 | tf_op jit(solution)/shard_map/ppermute | solution.py:42
  74.3 0.4 add_convert_fusion.3
  74.7 2.0 %collective-permute-start.27 = (bf16[2,2,32,1024]{3,2,1,0:T(8,128)(2,1)S(1)}, bf16[2,2,32,1024]{3,2,1,0:T(8,128)(2,1)S(1)}, u32[]{:S(2)}, u32[]{:S(2)}) collective-permute-start(bf16[2,2,32,1024]{3,2,1,0:T(8,128)(2,1)S(1)} %get-tuple-element.38), channel_id=1, source_target_pairs={{0,96},{8,104},{16,112},{24,120},{32,64},{40,72},{48,80},{56,88},{... | collective-permute-start | bytes 786440 | tf_op jit(solution)/shard_map/ppermute | solution.py:38
  76.7 3.2 %collective-permute-done.20 = bf16[144,512]{1,0:T(8,128)(2,1)S(1)} collective-permute-done((bf16[144,512]{1,0:T(8,128)(2,1)S(1)}, bf16[144,512]{1,0:T(8,128)(2,1)S(1)}, u32[]{:S(2)}, u32[]{:S(2)}) %collective-permute-start.20) | collective-permute-done | bytes 147488 | tf_op jit(solution)/shard_map/ppermute | solution.py:47
  79.9 1.6 %collective-permute-start.25 = (bf16[2,2,32,1024]{3,2,1,0:T(8,128)(2,1)S(1)}, bf16[2,2,32,1024]{3,2,1,0:T(8,128)(2,1)S(1)}, u32[]{:S(2)}, u32[]{:S(2)}) collective-permute-start(bf16[2,2,32,1024]{3,2,1,0:T(8,128)(2,1)S(1)} %get-tuple-element.40), channel_id=1, source_target_pairs={{0,64},{8,72},{16,80},{24,88},{32,96},{40,104},{48,112},{56,120},{... | collective-permute-start | bytes 786440 | tf_op jit(solution)/shard_map/ppermute | solution.py:38
  81.6 1.6 %collective-permute-start.22 = (bf16[144,512]{1,0:T(8,128)(2,1)S(1)}, bf16[144,512]{1,0:T(8,128)(2,1)S(1)}, u32[]{:S(2)}, u32[]{:S(2)}) collective-permute-start(bf16[144,512]{1,0:T(8,128)(2,1)S(1)} %add_convert_fusion.5), channel_id=1, source_target_pairs={{0,2},{1,3},{2,0},{3,1},{4,6},{5,7},{6,4},{7,5},{8,10},{9,11},{10,... | collective-permute-start | bytes 442376 | tf_op jit(solution)/shard_map/ppermute | solution.py:42
  83.1 1.1 %collective-permute-done.26 = bf16[2,2,32,1024]{3,2,1,0:T(8,128)(2,1)S(1)} collective-permute-done((bf16[2,2,32,1024]{3,2,1,0:T(8,128)(2,1)S(1)}, bf16[2,2,32,1024]{3,2,1,0:T(8,128)(2,1)S(1)}, u32[]{:S(2)}, u32[]{:S(2)}) %collective-permute-start.26) | collective-permute-done | bytes 262176 | tf_op jit(solution)/shard_map/ppermute | solution.py:38
  84.3 5.5 %collective-permute-done.25 = bf16[2,2,32,1024]{3,2,1,0:T(8,128)(2,1)S(1)} collective-permute-done((bf16[2,2,32,1024]{3,2,1,0:T(8,128)(2,1)S(1)}, bf16[2,2,32,1024]{3,2,1,0:T(8,128)(2,1)S(1)}, u32[]{:S(2)}, u32[]{:S(2)}) %collective-permute-start.25) | collective-permute-done | bytes 262176 | tf_op jit(solution)/shard_map/ppermute | solution.py:38
  89.8 1.5 %collective-permute-start.28 = (bf16[2,32,1024]{2,1,0:T(8,128)(2,1)S(1)}, bf16[2,32,1024]{2,1,0:T(8,128)(2,1)S(1)}, u32[]{:S(2)}, u32[]{:S(2)}) collective-permute-start(bf16[2,32,1024]{2,1,0:T(8,128)(2,1)S(1)} %fusion), channel_id=1, source_target_pairs={{0,16},{8,24},{16,0},{24,8},{32,48},{40,56},{48,32},{56,40},{64,80... | collective-permute-start | bytes 393224 | tf_op jit(solution)/shard_map/ppermute | solution.py:38
  91.4 2.8 %collective-permute-start.23 = (bf16[144,512]{1,0:T(8,128)(2,1)S(1)}, bf16[144,512]{1,0:T(8,128)(2,1)S(1)}, u32[]{:S(2)}, u32[]{:S(2)}) collective-permute-start(bf16[144,512]{1,0:T(8,128)(2,1)S(1)} %add_convert_fusion.4), channel_id=1, source_target_pairs={{0,6},{1,7},{2,4},{3,5},{4,2},{5,3},{6,0},{7,1},{8,14},{9,15},{10,... | collective-permute-start | bytes 442376 | tf_op jit(solution)/shard_map/ppermute | solution.py:42
  94.2 2.2 %collective-permute-done.28 = bf16[2,32,1024]{2,1,0:T(8,128)(2,1)S(1)} collective-permute-done((bf16[2,32,1024]{2,1,0:T(8,128)(2,1)S(1)}, bf16[2,32,1024]{2,1,0:T(8,128)(2,1)S(1)}, u32[]{:S(2)}, u32[]{:S(2)}) %collective-permute-start.28) | collective-permute-done | bytes 131104 | tf_op jit(solution)/shard_map/ppermute | solution.py:38
  96.4 0.8 convert_add_fusion.1
  97.1 0.6 collective-permute-done.23
  97.8 0.6 maximum_bitcast_fusion
  98.4 0.7 convert_add_fusion
  (35 shorter events, 0.3 us)
Async XLA Ops:
  1.6 8.2 %collective-permute-start.3 = (bf16[144,512]{1,0:T(8,128)(2,1)S(1)}, bf16[144,512]{1,0:T(8,128)(2,1)S(1)}, u32[]{:S(2)}, u32[]{:S(2)}) collective-permute-start(bf16[144,512]{1,0:T(8,128)(2,1)S(1)} %pack.1.refs_0_.refs_1_), channel_id=1, source_target_pairs={{0,16},{8,24},{16,0},{24,8},{32,48},{40,56},{48,32},{56,40},{64,80... | collective-permute-start | bytes 442376 | tf_op jit(solution)/shard_map/ppermute | solution.py:38
  5.6 7.1 %collective-permute-start.7 = (bf16[144,512]{1,0:T(8,128)(2,1)S(1)}, bf16[144,512]{1,0:T(8,128)(2,1)S(1)}, u32[]{:S(2)}, u32[]{:S(2)}) collective-permute-start(bf16[144,512]{1,0:T(8,128)(2,1)S(1)} %pack.1.refs_0_.refs_1_), channel_id=1, source_target_pairs={{0,8},{8,0},{16,24},{24,16},{32,40},{40,32},{48,56},{56,48},{64,72... | collective-permute-start | bytes 442376 | tf_op jit(solution)/shard_map/ppermute | solution.py:38
  5.6 10.6 %collective-permute-start.2 = (bf16[144,512]{1,0:T(8,128)(2,1)S(1)}, bf16[144,512]{1,0:T(8,128)(2,1)S(1)}, u32[]{:S(2)}, u32[]{:S(2)}) collective-permute-start(bf16[144,512]{1,0:T(8,128)(2,1)S(1)} %pack.1.refs_0_.refs_1_), channel_id=1, source_target_pairs={{0,96},{8,104},{16,112},{24,120},{32,64},{40,72},{48,80},{56,88},{... | collective-permute-start | bytes 442376 | tf_op jit(solution)/shard_map/ppermute | solution.py:38
  8.6 8.3 %collective-permute-start.1 = (bf16[144,512]{1,0:T(8,128)(2,1)S(1)}, bf16[144,512]{1,0:T(8,128)(2,1)S(1)}, u32[]{:S(2)}, u32[]{:S(2)}) collective-permute-start(bf16[144,512]{1,0:T(8,128)(2,1)S(1)} %pack.1.refs_0_.refs_1_), channel_id=1, source_target_pairs={{0,64},{8,72},{16,80},{24,88},{32,96},{40,104},{48,112},{56,120},{... | collective-permute-start | bytes 442376 | tf_op jit(solution)/shard_map/ppermute | solution.py:38
  9.3 8.4 %collective-permute-start = (bf16[144,512]{1,0:T(8,128)(2,1)S(1)}, bf16[144,512]{1,0:T(8,128)(2,1)S(1)}, u32[]{:S(2)}, u32[]{:S(2)}) collective-permute-start(bf16[144,512]{1,0:T(8,128)(2,1)S(1)} %pack.1.refs_0_.refs_1_), channel_id=1, source_target_pairs={{0,32},{8,40},{16,48},{24,56},{32,0},{40,8},{48,16},{56,24},{64,96... | collective-permute-start | bytes 442376 | tf_op jit(solution)/shard_map/ppermute | solution.py:38
  9.7 12.3 %collective-permute-start.6 = (bf16[144,512]{1,0:T(8,128)(2,1)S(1)}, bf16[144,512]{1,0:T(8,128)(2,1)S(1)}, u32[]{:S(2)}, u32[]{:S(2)}) collective-permute-start(bf16[144,512]{1,0:T(8,128)(2,1)S(1)} %collective-permute-done.3.refs_0_.refs_5_), channel_id=1, source_target_pairs={{0,96},{8,104},{16,112},{24,120},{32,64},{40,72},{48,80},{56,88},{... | collective-permute-start | bytes 442376 | tf_op jit(solution)/shard_map/ppermute | solution.py:38
  12.7 12.5 %collective-permute-start.5 = (bf16[144,512]{1,0:T(8,128)(2,1)S(1)}, bf16[144,512]{1,0:T(8,128)(2,1)S(1)}, u32[]{:S(2)}, u32[]{:S(2)}) collective-permute-start(bf16[144,512]{1,0:T(8,128)(2,1)S(1)} %collective-permute-done.3.refs_0_.refs_5_), channel_id=1, source_target_pairs={{0,64},{8,72},{16,80},{24,88},{32,96},{40,104},{48,112},{56,120},{... | collective-permute-start | bytes 442376 | tf_op jit(solution)/shard_map/ppermute | solution.py:38
  16.2 9.7 %collective-permute-start.4 = (bf16[144,512]{1,0:T(8,128)(2,1)S(1)}, bf16[144,512]{1,0:T(8,128)(2,1)S(1)}, u32[]{:S(2)}, u32[]{:S(2)}) collective-permute-start(bf16[144,512]{1,0:T(8,128)(2,1)S(1)} %collective-permute-done.3.refs_0_.refs_5_), channel_id=1, source_target_pairs={{0,32},{8,40},{16,48},{24,56},{32,0},{40,8},{48,16},{56,24},{64,96... | collective-permute-start | bytes 442376 | tf_op jit(solution)/shard_map/ppermute | solution.py:38
  16.9 9.1 %collective-permute-start.10 = (bf16[144,512]{1,0:T(8,128)(2,1)S(1)}, bf16[144,512]{1,0:T(8,128)(2,1)S(1)}, u32[]{:S(2)}, u32[]{:S(2)}) collective-permute-start(bf16[144,512]{1,0:T(8,128)(2,1)S(1)} %collective-permute-done.2.refs_3_.refs_4_), channel_id=1, source_target_pairs={{0,8},{8,0},{16,24},{24,16},{32,40},{40,32},{48,56},{56,48},{64,72... | collective-permute-start | bytes 442376 | tf_op jit(solution)/shard_map/ppermute | solution.py:38
  17.6 8.8 %collective-permute-start.9 = (bf16[144,512]{1,0:T(8,128)(2,1)S(1)}, bf16[144,512]{1,0:T(8,128)(2,1)S(1)}, u32[]{:S(2)}, u32[]{:S(2)}) collective-permute-start(bf16[144,512]{1,0:T(8,128)(2,1)S(1)} %collective-permute-done.1.refs_2_.refs_3_), channel_id=1, source_target_pairs={{0,8},{8,0},{16,24},{24,16},{32,40},{40,32},{48,56},{56,48},{64,72... | collective-permute-start | bytes 442376 | tf_op jit(solution)/shard_map/ppermute | solution.py:38
  22.0 4.5 %collective-permute-start.8 = (bf16[144,512]{1,0:T(8,128)(2,1)S(1)}, bf16[144,512]{1,0:T(8,128)(2,1)S(1)}, u32[]{:S(2)}, u32[]{:S(2)}) collective-permute-start(bf16[144,512]{1,0:T(8,128)(2,1)S(1)} %collective-permute-done.refs_1_.refs_2_), channel_id=1, source_target_pairs={{0,8},{8,0},{16,24},{24,16},{32,40},{40,32},{48,56},{56,48},{64,72... | collective-permute-start | bytes 442376 | tf_op jit(solution)/shard_map/ppermute | solution.py:38
  25.3 5.3 %collective-permute-start.11 = (bf16[144,512]{1,0:T(8,128)(2,1)S(1)}, bf16[144,512]{1,0:T(8,128)(2,1)S(1)}, u32[]{:S(2)}, u32[]{:S(2)}) collective-permute-start(bf16[144,512]{1,0:T(8,128)(2,1)S(1)} %collective-permute-done.3.refs_0_.refs_5_), channel_id=1, source_target_pairs={{0,8},{8,0},{16,24},{24,16},{32,40},{40,32},{48,56},{56,48},{64,72... | collective-permute-start | bytes 442376 | tf_op jit(solution)/shard_map/ppermute | solution.py:38
  25.9 4.8 %collective-permute-start.14 = (bf16[144,512]{1,0:T(8,128)(2,1)S(1)}, bf16[144,512]{1,0:T(8,128)(2,1)S(1)}, u32[]{:S(2)}, u32[]{:S(2)}) collective-permute-start(bf16[144,512]{1,0:T(8,128)(2,1)S(1)} %collective-permute-done.6.refs_3_.refs_8_), channel_id=1, source_target_pairs={{0,8},{8,0},{16,24},{24,16},{32,40},{40,32},{48,56},{56,48},{64,72... | collective-permute-start | bytes 442376 | tf_op jit(solution)/shard_map/ppermute | solution.py:38
  26.0 4.7 %collective-permute-start.13 = (bf16[144,512]{1,0:T(8,128)(2,1)S(1)}, bf16[144,512]{1,0:T(8,128)(2,1)S(1)}, u32[]{:S(2)}, u32[]{:S(2)}) collective-permute-start(bf16[144,512]{1,0:T(8,128)(2,1)S(1)} %collective-permute-done.5.refs_2_.refs_7_), channel_id=1, source_target_pairs={{0,8},{8,0},{16,24},{24,16},{32,40},{40,32},{48,56},{56,48},{64,72... | collective-permute-start | bytes 442376 | tf_op jit(solution)/shard_map/ppermute | solution.py:38
  26.4 4.3 %collective-permute-start.12 = (bf16[144,512]{1,0:T(8,128)(2,1)S(1)}, bf16[144,512]{1,0:T(8,128)(2,1)S(1)}, u32[]{:S(2)}, u32[]{:S(2)}) collective-permute-start(bf16[144,512]{1,0:T(8,128)(2,1)S(1)} %collective-permute-done.4.refs_1_.refs_6_), channel_id=1, source_target_pairs={{0,8},{8,0},{16,24},{24,16},{32,40},{40,32},{48,56},{56,48},{64,72... | collective-permute-start | bytes 442376 | tf_op jit(solution)/shard_map/ppermute | solution.py:38
  30.7 8.5 %copy-start = (bf16[512,1024]{1,0:T(8,128)(2,1)S(1)}, bf16[512,1024]{1,0:T(8,128)(2,1)}, u32[]{:S(2)}) copy-start(bf16[512,1024]{1,0:T(8,128)(2,1)} %refs_21_.1) | copy-start | bytes 3145732
  30.7 8.5 %copy-start.1 = (bf16[128,1536]{1,0:T(8,128)(2,1)S(1)}, bf16[128,1536]{1,0:T(8,128)(2,1)}, u32[]{:S(2)}) copy-start(bf16[128,1536]{1,0:T(8,128)(2,1)} %refs_19_.1) | copy-start | bytes 1179652
  30.7 8.5 %copy-start.2 = (bf16[128,1024]{1,0:T(8,128)(2,1)S(1)}, bf16[128,1024]{1,0:T(8,128)(2,1)}, u32[]{:S(2)}) copy-start(bf16[128,1024]{1,0:T(8,128)(2,1)} %refs_20_.1) | copy-start | bytes 786436
  38.6 12.3 %collective-permute-start.15 = (bf16[1152,512]{1,0:T(8,128)(2,1)S(1)}, bf16[1152,512]{1,0:T(8,128)(2,1)S(1)}, u32[]{:S(2)}, u32[]{:S(2)}) collective-permute-start(bf16[1152,512]{1,0:T(8,128)(2,1)S(1)} %get-tuple-element.26), channel_id=1, source_target_pairs={{0,8},{8,0},{16,24},{24,16},{32,40},{40,32},{48,56},{56,48},{64,72... | collective-permute-start | bytes 3538952 | tf_op jit(solution)/shard_map/ppermute | solution.py:38
  47.9 26.4 %collective-permute-start.24 = (bf16[8,2,32,1024]{3,2,1,0:T(8,128)(2,1)S(1)}, bf16[8,2,32,1024]{3,2,1,0:T(8,128)(2,1)S(1)}, u32[]{:S(2)}, u32[]{:S(2)}) collective-permute-start(bf16[8,2,32,1024]{3,2,1,0:T(8,128)(2,1)S(1)} %get-tuple-element.28), channel_id=1, source_target_pairs={{0,8},{8,0},{16,24},{24,16},{32,40},{40,32},{48,56},{56,48},{64,72... | collective-permute-start | bytes 3145736 | tf_op jit(solution)/shard_map/ppermute | solution.py:38
  51.2 10.0 %collective-permute-start.17 = (bf16[288,512]{1,0:T(8,128)(2,1)S(1)}, bf16[288,512]{1,0:T(8,128)(2,1)S(1)}, u32[]{:S(2)}, u32[]{:S(2)}) collective-permute-start(bf16[288,512]{1,0:T(8,128)(2,1)S(1)} %pad_maximum_fusion.1), channel_id=1, source_target_pairs={{0,32},{8,40},{16,48},{24,56},{32,0},{40,8},{48,16},{56,24},{64,96... | collective-permute-start | bytes 884744 | tf_op jit(solution)/shard_map/ppermute | solution.py:38
  51.8 16.4 %collective-permute-start.18 = (bf16[288,512]{1,0:T(8,128)(2,1)S(1)}, bf16[288,512]{1,0:T(8,128)(2,1)S(1)}, u32[]{:S(2)}, u32[]{:S(2)}) collective-permute-start(bf16[288,512]{1,0:T(8,128)(2,1)S(1)} %pad_maximum_fusion.2), channel_id=1, source_target_pairs={{0,96},{8,104},{16,112},{24,120},{32,64},{40,72},{48,80},{56,88},{... | collective-permute-start | bytes 884744 | tf_op jit(solution)/shard_map/ppermute | solution.py:38
  55.0 14.9 %collective-permute-start.16 = (bf16[288,512]{1,0:T(8,128)(2,1)S(1)}, bf16[288,512]{1,0:T(8,128)(2,1)S(1)}, u32[]{:S(2)}, u32[]{:S(2)}) collective-permute-start(bf16[288,512]{1,0:T(8,128)(2,1)S(1)} %pad_maximum_fusion), channel_id=1, source_target_pairs={{0,64},{8,72},{16,80},{24,88},{32,96},{40,104},{48,112},{56,120},{... | collective-permute-start | bytes 884744 | tf_op jit(solution)/shard_map/ppermute | solution.py:38
  70.2 9.7 %collective-permute-start.20 = (bf16[144,512]{1,0:T(8,128)(2,1)S(1)}, bf16[144,512]{1,0:T(8,128)(2,1)S(1)}, u32[]{:S(2)}, u32[]{:S(2)}) collective-permute-start(bf16[144,512]{1,0:T(8,128)(2,1)S(1)} %get-tuple-element.29), channel_id=1, source_target_pairs={{0,17},{1,16},{2,19},{3,18},{4,21},{5,20},{6,23},{7,22},{8,25},{9,... | collective-permute-start | bytes 442376 | tf_op jit(solution)/shard_map/ppermute | solution.py:47
  70.9 10.5 %collective-permute-start.19 = (bf16[144,512]{1,0:T(8,128)(2,1)S(1)}, bf16[144,512]{1,0:T(8,128)(2,1)S(1)}, u32[]{:S(2)}, u32[]{:S(2)}) collective-permute-start(bf16[144,512]{1,0:T(8,128)(2,1)S(1)} %get-tuple-element.29), channel_id=1, source_target_pairs={{0,16},{8,24},{16,0},{24,8},{32,48},{40,56},{48,32},{56,40},{64,80... | collective-permute-start | bytes 442376 | tf_op jit(solution)/shard_map/ppermute | solution.py:38
  73.3 8.2 %collective-permute-start.21 = (bf16[144,512]{1,0:T(8,128)(2,1)S(1)}, bf16[144,512]{1,0:T(8,128)(2,1)S(1)}, u32[]{:S(2)}, u32[]{:S(2)}) collective-permute-start(bf16[144,512]{1,0:T(8,128)(2,1)S(1)} %get-tuple-element.30), channel_id=1, source_target_pairs={{0,1},{1,0},{2,3},{3,2},{4,5},{5,4},{6,7},{7,6},{8,9},{9,8},{10,11... | collective-permute-start | bytes 442376 | tf_op jit(solution)/shard_map/ppermute | solution.py:42
  74.7 8.4 %collective-permute-start.27 = (bf16[2,2,32,1024]{3,2,1,0:T(8,128)(2,1)S(1)}, bf16[2,2,32,1024]{3,2,1,0:T(8,128)(2,1)S(1)}, u32[]{:S(2)}, u32[]{:S(2)}) collective-permute-start(bf16[2,2,32,1024]{3,2,1,0:T(8,128)(2,1)S(1)} %get-tuple-element.38), channel_id=1, source_target_pairs={{0,96},{8,104},{16,112},{24,120},{32,64},{40,72},{48,80},{56,88},{... | collective-permute-start | bytes 786440 | tf_op jit(solution)/shard_map/ppermute | solution.py:38
  76.7 7.5 %collective-permute-start.26 = (bf16[2,2,32,1024]{3,2,1,0:T(8,128)(2,1)S(1)}, bf16[2,2,32,1024]{3,2,1,0:T(8,128)(2,1)S(1)}, u32[]{:S(2)}, u32[]{:S(2)}) collective-permute-start(bf16[2,2,32,1024]{3,2,1,0:T(8,128)(2,1)S(1)} %get-tuple-element.39), channel_id=1, source_target_pairs={{0,32},{8,40},{16,48},{24,56},{32,0},{40,8},{48,16},{56,24},{64,96... | collective-permute-start | bytes 786440 | tf_op jit(solution)/shard_map/ppermute | solution.py:38
  79.9 9.8 %collective-permute-start.25 = (bf16[2,2,32,1024]{3,2,1,0:T(8,128)(2,1)S(1)}, bf16[2,2,32,1024]{3,2,1,0:T(8,128)(2,1)S(1)}, u32[]{:S(2)}, u32[]{:S(2)}) collective-permute-start(bf16[2,2,32,1024]{3,2,1,0:T(8,128)(2,1)S(1)} %get-tuple-element.40), channel_id=1, source_target_pairs={{0,64},{8,72},{16,80},{24,88},{32,96},{40,104},{48,112},{56,120},{... | collective-permute-start | bytes 786440 | tf_op jit(solution)/shard_map/ppermute | solution.py:38
  81.6 9.8 %collective-permute-start.22 = (bf16[144,512]{1,0:T(8,128)(2,1)S(1)}, bf16[144,512]{1,0:T(8,128)(2,1)S(1)}, u32[]{:S(2)}, u32[]{:S(2)}) collective-permute-start(bf16[144,512]{1,0:T(8,128)(2,1)S(1)} %add_convert_fusion.5), channel_id=1, source_target_pairs={{0,2},{1,3},{2,0},{3,1},{4,6},{5,7},{6,4},{7,5},{8,10},{9,11},{10,... | collective-permute-start | bytes 442376 | tf_op jit(solution)/shard_map/ppermute | solution.py:42
  89.8 6.6 %collective-permute-start.28 = (bf16[2,32,1024]{2,1,0:T(8,128)(2,1)S(1)}, bf16[2,32,1024]{2,1,0:T(8,128)(2,1)S(1)}, u32[]{:S(2)}, u32[]{:S(2)}) collective-permute-start(bf16[2,32,1024]{2,1,0:T(8,128)(2,1)S(1)} %fusion), channel_id=1, source_target_pairs={{0,16},{8,24},{16,0},{24,8},{32,48},{40,56},{48,32},{56,40},{64,80... | collective-permute-start | bytes 393224 | tf_op jit(solution)/shard_map/ppermute | solution.py:38
  91.4 6.4 %collective-permute-start.23 = (bf16[144,512]{1,0:T(8,128)(2,1)S(1)}, bf16[144,512]{1,0:T(8,128)(2,1)S(1)}, u32[]{:S(2)}, u32[]{:S(2)}) collective-permute-start(bf16[144,512]{1,0:T(8,128)(2,1)S(1)} %add_convert_fusion.4), channel_id=1, source_target_pairs={{0,6},{1,7},{2,4},{3,5},{4,2},{5,3},{6,0},{7,1},{8,14},{9,15},{10,... | collective-permute-start | bytes 442376 | tf_op jit(solution)/shard_map/ppermute | solution.py:42

commit v3 on v2

--- a/solution.py
+++ b/solution.py
@@ -80,6 +80,12 @@
     out_ref[:CHUNK, :] = latents_ref[...]
     for g in range(ROPE // ROPE_ROWS):
         out_ref[CHUNK:, g * LANES : (g + 1) * LANES] = turned_ref[g * ROPE_ROWS : (g + 1) * ROPE_ROWS, :]
+
+
+def final_kernel(mine_ref, other_ref, latent_ref, turned_ref):
+    total = mine_ref[...].astype(F32) + other_ref[...].astype(F32)
+    latent_ref[...] = total[:CHUNK]
+    turned_ref[...] = rope_rows(total[CHUNK:])
 
 
 def prep_kernel(own_ref, order_ref, query_ref, up_key_ref, out_grad_ref, up_value_ref, q_ref, gl_ref, bias_ref):
@@ -157,6 +163,19 @@
     return state, tops
 
 
+def turn_keys(k_refs, own, turned):
+    share = D_LATENT // CTX
+    for i, k_ref in enumerate(k_refs):
+        cols = slice(i * CHUNK, (i + 1) * CHUNK)
+        block = k_ref[:CHUNK, :].T
+        for r in range(CTX):
+            other = own ^ r
+            position = ((other & 1) << 3) | ((other >> 2) << 1) | ((other >> 1) & 1)
+            to = pl.ds(pl.multiple_of(position * share, share), share)
+            turned[to, cols] = block[r * share : (r + 1) * share, :]
+        turned[D_LATENT:, cols] = key_ropes(k_ref)
+
+
 def early_kernel(*refs):
     count = 2 * len(EARLY)
     k_refs = refs[:count]
@@ -176,8 +195,9 @@
 
 def scores_kernel(*refs):
     count = 2 * len(LATE)
-    k_refs = refs[:count]
-    q_ref, gl_ref, bias_ref, early_e, early_g, early_state, probs, grads, send_ref, keys, e_ref, g_ref = refs[count:]
+    own_ref, k_refs, early_refs = refs[0], refs[1 : count + 1], refs[count + 1 : CTX + 1]
+    q_ref, gl_ref, bias_ref, early_e, early_g, early_state = refs[CTX + 1 : CTX + 7]
+    probs, grads, send_ref, early_turned, turned, keys, e_ref, g_ref = refs[CTX + 7 :]
     step = pl.program_id(0)
 
     @pl.when(step == 0)
@@ -208,6 +228,8 @@
         rows = slice((BLOCKS // 2) * BLOCK, BLOCKS * BLOCK)
         both = [jnp.concatenate([ref[i, rows, :] for i in range(PAIRS)], axis=1) for ref in (probs, grads)]
         store_latents(send_ref, *latent_rows(*both, q_ref, gl_ref))
+        turn_keys(early_refs, own_ref[0], early_turned)
+        turn_keys(k_refs, own_ref[0], turned)
 
 
 def keep_kernel(probs_ref, grads_ref, q_ref, gl_ref, keep_ref):
@@ -216,45 +238,47 @@
     store_latents(keep_ref, *latent_rows(*both, q_ref, gl_ref))
 
 
-def weights_kernel(*refs):
-    own_ref = refs[0]
-    k_refs = refs[1 : CTX + 1]
-    probs_ref, grads_ref, query_ref, out_grad_ref, up_key_ref = refs[CTX + 1 : CTX + 6]
-    query_grad_ref, send_ref, keep_ref, kt_ref, w_ref = refs[CTX + 6 :]
+def diagonal(first, second):
+    zero = jnp.zeros_like(first)
+    return jnp.concatenate([jnp.concatenate([first, zero], axis=1), jnp.concatenate([zero, second], axis=1)], axis=0)
+
+
+def weights_kernel(
+    own_ref, early_ref, late_ref, probs_ref, grads_ref, query_ref, out_grad_ref, up_key_ref, query_grad_ref, send_ref, keep_ref, up_ref
+):
     step = pl.program_id(0)
+    share = D_LATENT // CTX
 
     @pl.when(step == 0)
     def _():
-        for i, k_ref in enumerate(k_refs):
-            cols = slice(i * CHUNK, (i + 1) * CHUNK)
-            kt_ref[:D_LATENT, cols] = k_ref[:CHUNK, :].T
-            kt_ref[D_LATENT:, cols] = key_ropes(k_ref)
-
-    out_t = dot(kt_ref[:D_LATENT, :], probs_ref[step], NN).astype(BF16)
-    abs_t = dot(kt_ref[...], grads_ref[step], NN) * SCALE
+        for position in range(CTX):
+            rows = pl.ds(pl.multiple_of((own_ref[0] ^ row_xor(position)) * share, share), share)
+            up_ref[position * share : (position + 1) * share, :] = up_key_ref[rows, :]
+
+    half = BLOCKS // 4 * BLOCK
+    turned = jnp.concatenate([ref[:, i * half : (i + 1) * half] for i in range(2) for ref in (early_ref, late_ref)], axis=1)
+    out_t = dot(turned[:D_LATENT, :], probs_ref[step], NN).astype(BF16)
+    abs_t = dot(turned, grads_ref[step], NN) * SCALE
     rope_t = abs_t[D_LATENT:, :]
     abs_t = abs_t[:D_LATENT, :].astype(BF16)
     queries = query_ref[:, pl.ds(pl.multiple_of(step * PAIR_COLS, PAIR_COLS), PAIR_COLS)]
     lanes = pl.ds(pl.multiple_of(step * 2 * NOPE, 2 * NOPE), 2 * NOPE)
     grad_out = out_grad_ref[:, lanes]
-    up_key = up_key_ref[:, lanes]
+    up_key = up_ref[:, lanes]
+    width = NOPE + ROPE
+    key_part = dot(abs_t, diagonal(queries[:, :NOPE], queries[:, width : width + NOPE]), NN).astype(BF16)
+    value_part = dot(out_t, diagonal(grad_out[:, :VDIM], grad_out[:, VDIM:]), NN).astype(BF16)
+    for position in range(CTX):
+        out = send_ref if position >= CTX // 2 else keep_ref
+        rows = slice(position * share, (position + 1) * share)
+        out[position % (CTX // 2), 0, :, lanes] = key_part[rows]
+        out[position % (CTX // 2), 1, :, lanes] = value_part[rows]
     pieces = []
     for h in range(2):
         cols = slice(h * NOPE, (h + 1) * NOPE)
-        first = h * (NOPE + ROPE)
-        nope = queries[:, first : first + NOPE]
-        w_ref[0, :, cols] = dot(abs_t[:, cols], nope, NN).astype(BF16)
-        w_ref[1, :, cols] = dot(out_t[:, cols], grad_out[:, cols], NN).astype(BF16)
         pieces.append(dot(abs_t[:, cols], up_key[:, cols], TN))
         pieces.append(rope_t[:, cols].T)
     query_grad_ref[...] = jnp.concatenate(pieces, axis=1).astype(BF16)
-    own = own_ref[0]
-    share = D_LATENT // CTX
-    for position in range(CTX):
-        rows = pl.ds(pl.multiple_of((own ^ row_xor(position)) * share, share), share)
-        out = send_ref if position >= CTX // 2 else keep_ref
-        out[position % (CTX // 2), 0, :, lanes] = w_ref[0, rows, :]
-        out[position % (CTX // 2), 1, :, lanes] = w_ref[1, rows, :]
 
 
 def spread_sum(parts):
@@ -285,7 +309,6 @@
     total = BLOCKS * BLOCK
     half = (CTX // 2) * PACKED
     pair_cols = 2 * (NOPE + ROPE)
-    rope_parts = ROPE // ROPE_ROWS
 
     keys = pl.pallas_call(
         pack_kernel,
@@ -352,12 +375,13 @@
         cost_estimate=cost(3_000_000_000, 10_000_000),
         name="early",
     )(*in_vmem(*early_chunks, query_all, grad_lat, bias))
-    probs, grads, latent_send = pl.pallas_call(
+    probs, grads, latent_send, early_turned, late_turned = pl.pallas_call(
         scores_kernel,
         grid=(PAIRS + 1,),
-        out_shape=(pair_shape, pair_shape, latent_shape),
-        in_specs=[vmem] * (len(late_chunks) + 6),
-        out_specs=(vmem,) * 3,
+        out_shape=(pair_shape, pair_shape, latent_shape)
+        + (pltpu.VMEM((WIDTH, early), BF16), pltpu.VMEM((WIDTH, late), BF16)),
+        in_specs=[smem] + [vmem] * (CTX + 6),
+        out_specs=(vmem,) * 5,
         scratch_shapes=[
             pltpu.VMEM((late, WIDTH), BF16),
             pltpu.VMEM((late, 2 * tok), BF16),
@@ -366,7 +390,7 @@
         compiler_params=pltpu.CompilerParams(vmem_limit_bytes=24 << 20),
         cost_estimate=cost(6_000_000_000, 14_000_000),
         name="scores",
-    )(*in_vmem(*late_chunks, query_all, grad_lat, bias, *early_parts))
+    )(own.reshape(1), *in_vmem(*late_chunks, *early_chunks, query_all, grad_lat, bias, *early_parts))
 
     latent_got = swap_ctx(latent_send, 1)
 
@@ -386,22 +410,13 @@
         weights_kernel,
         grid=(PAIRS,),
         out_shape=(jax.ShapeDtypeStruct(queries.shape, BF16), weight_shape, weight_shape),
-        in_specs=[smem]
-        + [vmem] * (CTX + 2)
-        + [
-            vmem,
-            vmem,
-            vmem,
-        ],
+        in_specs=[smem] + [vmem] * 7,
         out_specs=(pl.BlockSpec((tok, pair_cols), lambda i: (0, i)), vmem, vmem),
-        scratch_shapes=[
-            pltpu.VMEM((WIDTH, total), BF16),
-            pltpu.VMEM((2, D_LATENT, 2 * NOPE), BF16),
-        ],
+        scratch_shapes=[pltpu.VMEM((D_LATENT, heads * NOPE), BF16)],
         compiler_params=pltpu.CompilerParams(vmem_limit_bytes=24 << 20),
         cost_estimate=cost(5_000_000_000, 14_000_000),
         name="weights",
-    )(own.reshape(1), *in_vmem(*k_chunks, probs, grads, queries, out_grad, up_key_weight))
+    )(own.reshape(1), *in_vmem(early_turned, late_turned, probs, grads, queries, out_grad, up_key_weight))
 
     pieces = [
         [
@@ -424,11 +439,15 @@
     other = swap_head(mine, 2)
     mine = spread_sum([mine, other]).astype(BF16)
     other = swap_head(mine, 6)
-    latent_grad = spread_sum([mine[:tok], other[:tok]])
-    turned = [
-        spread_sum([part[tok:, g * LANES : (g + 1) * LANES] for part in (mine, other)]) for g in range(rope_parts)
-    ]
-    rope_grad = jnp.concatenate(turned, axis=0).T
+    latent_grad, rope_turned = pl.pallas_call(
+        final_kernel,
+        out_shape=(jax.ShapeDtypeStruct((tok, D_LATENT), F32), jax.ShapeDtypeStruct((ROPE, tok), F32)),
+        in_specs=[vmem] * 2,
+        out_specs=(vmem, vmem),
+        compiler_params=pltpu.CompilerParams(vmem_limit_bytes=4 << 20),
+        name="final",
+    )(*in_vmem(mine, other))
+    rope_grad = rope_turned.T
 
     weight_got = swap_ctx(weight_send, 1)
     pieces = [

time: 99.3 us -> 96.9 us (0.976)
  waiting for transfers between devices: 34.1 us -> 31.2 us
  starting transfers between devices: 33.1 us -> 34.6 us
  other arithmetic: 3.23 us -> 1.86 us
    ppermute x25, waiting for transfers between devices: 30.3 us -> 26.6 us  [swap_ctx(): return lax.ppermute(value, 'ctx', [(i, i ^ mask) for i in range(CTX)])]
    ppermute x1, starting transfers between devices: 0.79 us -> 4.12 us  [swap_both(): lax.ppermute(value, ('ctx', 'head'), [(i, i ^ mask) for i in range(CTX *...]
    ppermute x25, starting transfers between devices: 26.9 us -> 25.1 us  [swap_ctx(): return lax.ppermute(value, 'ctx', [(i, i ^ mask) for i in range(CTX)])]
    ppermute x3, waiting for transfers between devices: 0.65 us -> 1.96 us  [swap_head(): return lax.ppermute(value, 'head', [(i, i ^ mask) for i in range(HEAD)])]
    pallas_call x1, Pallas kernels: 8.77 us -> 7.68 us  [per_device(): pl.pallas_call(weights_kernel, grid=(PAIRS,), out_shape=(jax.ShapeDtypeSt...]
  transfers between devices with their start and end apart: 29 -> 29, of which waited for: 12 -> 15; matrix products, arithmetic and copies ran while one was open for 2% -> 2% of each run, Pallas kernels for 19% -> 19%
where the time goes in v3:
time: 96.9 us; the launch traced here: 96.7 us
  starting transfers between devices  34.6 us (36%)
  waiting for transfers between devices  31.2 us (32%)
  Pallas kernels  28.2 us (29%)
  other arithmetic  1.86 us (2%)
    ppermute x25, waiting for transfers between devices, swap_ctx(): return lax.ppermute(value, 'ctx', [(i, i ^ mask) for i in range(CTX)])  26.6 us
    ppermute x25, starting transfers between devices, swap_ctx(): return lax.ppermute(value, 'ctx', [(i, i ^ mask) for i in range(CTX)])  25.1 us
    pallas_call x1, Pallas kernels, per_device(): pl.pallas_call(scores_kernel, grid=(PAIRS + 1,), out_shape=(pair_shape, p...  8.41 us
    pallas_call x1, Pallas kernels, per_device(): pl.pallas_call(weights_kernel, grid=(PAIRS,), out_shape=(jax.ShapeDtypeSt...  7.68 us
    ppermute x3, starting transfers between devices, swap_head(): return lax.ppermute(value, 'head', [(i, i ^ mask) for i in range(HEAD)])  5.35 us
    pallas_call x1, Pallas kernels, per_device(): pl.pallas_call(early_kernel, grid=(PAIRS,), out_shape=(pltpu.VMEM((PAIRS,...  4.3 us
    ppermute x1, starting transfers between devices, swap_both(): lax.ppermute(value, ('ctx', 'head'), [(i, i ^ mask) for i in range(CTX *...  4.12 us
    pallas_call x1, Pallas kernels, per_device(): pl.pallas_call(prep_kernel, grid=(PAIRS,), out_shape=(jax.ShapeDtypeStruc...  3.27 us
  transfers between devices with their start and end apart: 29, of which 15 were waited for; matrix products, arithmetic and copies ran while one was open for 2% of the time, Pallas kernels for 19%

profile of v3, /device:TPU:0, one launch (start us, length us, event | category | flops | bytes accessed | tf_op | source)
XLA Modules:
  0.0 96.7 jit_solution(14016363323743113632)
XLA Ops:
  0.6 0.9 pack.1.refs_0_.refs_9_
  1.6 3.2 %collective-permute-start.10 = (bf16[144,512]{1,0:T(8,128)(2,1)S(1)}, bf16[144,512]{1,0:T(8,128)(2,1)S(1)}, u32[]{:S(2)}, u32[]{:S(2)}) collective-permute-start(bf16[144,512]{1,0:T(8,128)(2,1)S(1)} %pack.1.refs_0_.refs_9_), channel_id=1, source_target_pairs={{0,96},{8,104},{16,112},{24,120},{32,64},{40,72},{48,80},{56,88},{... | collective-permute-start | bytes 442376 | tf_op jit(solution)/shard_map/ppermute | solution.py:38
  4.8 0.6 collective-permute-start.9
  5.4 3.9 %collective-permute-start = (bf16[144,512]{1,0:T(8,128)(2,1)S(1)}, bf16[144,512]{1,0:T(8,128)(2,1)S(1)}, u32[]{:S(2)}, u32[]{:S(2)}) collective-permute-start(bf16[144,512]{1,0:T(8,128)(2,1)S(1)} %pack.1.refs_0_.refs_9_), channel_id=1, source_target_pairs={{0,16},{8,24},{16,0},{24,8},{32,48},{40,56},{48,32},{56,40},{64,80... | collective-permute-start | bytes 442376 | tf_op jit(solution)/shard_map/ppermute | solution.py:38
  9.3 0.5 collective-permute-start.8
  9.7 2.0 %collective-permute-done.10.refs_3_.refs_12_ = bf16[144,512]{1,0:T(8,128)(2,1)S(1)} collective-permute-done((bf16[144,512]{1,0:T(8,128)(2,1)S(1)}, bf16[144,512]{1,0:T(8,128)(2,1)S(1)}, u32[]{:S(2)}, u32[]{:S(2)}) %collective-permute-start.10) | collective-permute-done | bytes 147488 | tf_op jit(solution)/shard_map/ppermute | solution.py:38
  11.8 0.5 collective-permute-start.13
  12.3 0.3 collective-permute-done.refs_1_
  12.6 2.7 %collective-permute-start.3 = (bf16[144,512]{1,0:T(8,128)(2,1)S(1)}, bf16[144,512]{1,0:T(8,128)(2,1)S(1)}, u32[]{:S(2)}, u32[]{:S(2)}) collective-permute-start(bf16[144,512]{1,0:T(8,128)(2,1)S(1)} %collective-permute-done.refs_1_), channel_id=1, source_target_pairs={{0,96},{8,104},{16,112},{24,120},{32,64},{40,72},{48,80},{56,88},{... | collective-permute-start | bytes 442376 | tf_op jit(solution)/shard_map/ppermute | solution.py:38
  15.2 0.2 collective-permute-start.2
  15.5 1.1 %collective-permute-start.1 = (bf16[144,512]{1,0:T(8,128)(2,1)S(1)}, bf16[144,512]{1,0:T(8,128)(2,1)S(1)}, u32[]{:S(2)}, u32[]{:S(2)}) collective-permute-start(bf16[144,512]{1,0:T(8,128)(2,1)S(1)} %collective-permute-done.refs_1_), channel_id=1, source_target_pairs={{0,32},{8,40},{16,48},{24,56},{32,0},{40,8},{48,16},{56,24},{64,96... | collective-permute-start | bytes 442376 | tf_op jit(solution)/shard_map/ppermute | solution.py:38
  16.7 3.3 %prep.1 = (bf16[4,256,576]{2,1,0:T(8,128)(2,1)S(1)}, bf16[4,256,512]{2,1,0:T(8,128)(2,1)S(1)}, f32[2048,128]{1,0:T(8,128)S(1)}) custom-call(s32[1]{0:T(128)} %bitcast.own_ref.refs_0_, s32[32]{0:T(128)} %order_ref.1, bf16[128,1536]{1,0:T(8,128)(2,1)} %query_ref.3, bf16[512,1024]{1,0:T(8,128)(2,1)} %up_key_ref.3, bf16[128,1024]{1,0:T(8,128)(2,1)} %out_grad_ref.3, ...), custom_call_target="tpu_custom_call" | custom-call | flops 300000000 | bytes 10000000 | tf_op jit(solution)/shard_map/prep/pallas_call | solution.py:331
  19.9 0.6 collective-permute-start.4
  20.5 1.2 %collective-permute-done.3.refs_4_ = bf16[144,512]{1,0:T(8,128)(2,1)S(1)} collective-permute-done((bf16[144,512]{1,0:T(8,128)(2,1)S(1)}, bf16[144,512]{1,0:T(8,128)(2,1)S(1)}, u32[]{:S(2)}, u32[]{:S(2)}) %collective-permute-start.3) | collective-permute-done | bytes 147488 | tf_op jit(solution)/shard_map/ppermute | solution.py:38
  21.8 1.7 %collective-permute-done.2.refs_3_ = bf16[144,512]{1,0:T(8,128)(2,1)S(1)} collective-permute-done((bf16[144,512]{1,0:T(8,128)(2,1)S(1)}, bf16[144,512]{1,0:T(8,128)(2,1)S(1)}, u32[]{:S(2)}, u32[]{:S(2)}) %collective-permute-start.2) | collective-permute-done | bytes 147488 | tf_op jit(solution)/shard_map/ppermute | solution.py:38
  23.5 0.5 collective-permute-start.5
  24.0 4.3 %early.1 = (bf16[4,1024,256]{2,1,0:T(8,128)(2,1)S(1)}, f32[4,1024,256]{2,1,0:T(8,128)S(1)}, f32[4,8,256]{2,1,0:T(8,128)S(1)}) custom-call(bf16[144,512]{1,0:T(8,128)(2,1)S(1)} %pack.1.refs_0_.refs_9_, bf16[144,512]{1,0:T(8,128)(2,1)S(1)} %collective-permute-done.8.refs_1_.refs_10_, bf16[144,512]{1,0:T(8,128)(2,1)S(1)} %collective-permute-done.9.refs_2_.refs_11_, ...), custom_call_target="tpu_custom_call" | custom-call | flops 3000000000 | bytes 10000000 | tf_op jit(solution)/shard_map/early/pallas_call | solution.py:363
  28.4 8.4 %scores.1 = (bf16[4,2048,256]{2,1,0:T(8,128)(2,1)S(1)}, bf16[4,2048,256]{2,1,0:T(8,128)(2,1)S(1)}, bf16[1152,512]{1,0:T(8,128)(2,1)S(1)}, bf16[576,1024]{1,0:T(8,128)(2,1)S(1)}, bf16[576,1024]{1,0:T(8,128)(2,1)S(1)}) custom-call(s32[1]{0:T(128)} %bitcast.own_ref.refs_0_, bf16[144,512]{1,0:T(8,128)(2,1)S(1)} %collective-permute-done.refs_1_, ...), custom_call_target="tpu_custom_call" | custom-call | flops 6000000000 | bytes 14000000 | tf_op jit(solution)/shard_map/scores/pallas_call | solution.py:378
  36.8 0.1 collective-permute-start.15
  36.9 7.7 %weights.1 = (bf16[128,1536]{1,0:T(8,128)(2,1)}, bf16[8,2,32,1024]{3,2,1,0:T(8,128)(2,1)S(1)}, bf16[8,2,32,1024]{3,2,1,0:T(8,128)(2,1)S(1)}) custom-call(s32[1]{0:T(128)} %bitcast.own_ref.refs_0_, bf16[576,1024]{1,0:T(8,128)(2,1)S(1)} %get-tuple-element.27.early_ref, bf16[576,1024]{1,0:T(8,128)(2,1)S(1)} %get-tuple-element.28.late_ref, ...), custom_call_target="tpu_custom_call" | custom-call | flops 5000000000 | bytes 14000000 | tf_op jit(solution)/shard_map/weights/pallas_call | solution.py:409
  44.6 0.5 collective-permute-start.24
  45.1 2.9 %keep.1 = bf16[1152,512]{1,0:T(8,128)(2,1)S(1)} custom-call(bf16[4,2048,256]{2,1,0:T(8,128)(2,1)S(1)} %get-tuple-element.29.probs_ref, bf16[4,2048,256]{2,1,0:T(8,128)(2,1)S(1)} %get-tuple-element.30.grads_ref, bf16[4,256,576]{2,1,0:T(8,128)(2,1)S(1)} %get-tuple-element.21.refs_8_.refs_17_.q_ref, ...), custom_call_target="tpu_custom_call" | custom-call | flops 2300000000 | bytes 7000000 | tf_op jit(solution)/shard_map/keep/pallas_call | solution.py:397
  48.0 0.3 add_convert_fusion.14
  48.2 0.4 collective-permute-start.17
  48.7 2.0 %collective-permute-start.18 = (bf16[288,512]{1,0:T(8,128)(2,1)S(1)}, bf16[288,512]{1,0:T(8,128)(2,1)S(1)}, u32[]{:S(2)}, u32[]{:S(2)}) collective-permute-start(bf16[288,512]{1,0:T(8,128)(2,1)S(1)} %pad_maximum_fusion.2), channel_id=1, source_target_pairs={{0,96},{8,104},{16,112},{24,120},{32,64},{40,72},{48,80},{56,88},{... | collective-permute-start | bytes 884744 | tf_op jit(solution)/shard_map/ppermute | solution.py:38
  50.7 1.9 %collective-permute-start.16 = (bf16[288,512]{1,0:T(8,128)(2,1)S(1)}, bf16[288,512]{1,0:T(8,128)(2,1)S(1)}, u32[]{:S(2)}, u32[]{:S(2)}) collective-permute-start(bf16[288,512]{1,0:T(8,128)(2,1)S(1)} %pad_maximum_fusion), channel_id=1, source_target_pairs={{0,64},{8,72},{16,80},{24,88},{32,96},{40,104},{48,112},{56,120},{... | collective-permute-start | bytes 884744 | tf_op jit(solution)/shard_map/ppermute | solution.py:38
  52.6 5.6 %collective-permute-done.17 = bf16[288,512]{1,0:T(8,128)(2,1)S(1)} collective-permute-done((bf16[288,512]{1,0:T(8,128)(2,1)S(1)}, bf16[288,512]{1,0:T(8,128)(2,1)S(1)}, u32[]{:S(2)}, u32[]{:S(2)}) %collective-permute-start.17) | collective-permute-done | bytes 294944 | tf_op jit(solution)/shard_map/ppermute | solution.py:38
  58.2 5.6 %collective-permute-done.18 = bf16[288,512]{1,0:T(8,128)(2,1)S(1)} collective-permute-done((bf16[288,512]{1,0:T(8,128)(2,1)S(1)}, bf16[288,512]{1,0:T(8,128)(2,1)S(1)}, u32[]{:S(2)}, u32[]{:S(2)}) %collective-permute-start.18) | collective-permute-done | bytes 294944 | tf_op jit(solution)/shard_map/ppermute | solution.py:38
  63.8 1.8 %collective-permute-done.16 = bf16[288,512]{1,0:T(8,128)(2,1)S(1)} collective-permute-done((bf16[288,512]{1,0:T(8,128)(2,1)S(1)}, bf16[288,512]{1,0:T(8,128)(2,1)S(1)}, u32[]{:S(2)}, u32[]{:S(2)}) %collective-permute-start.16) | collective-permute-done | bytes 294944 | tf_op jit(solution)/shard_map/ppermute | solution.py:38
  65.6 0.2 add_convert_fusion.6
  65.8 4.1 %collective-permute-start.20 = (bf16[144,512]{1,0:T(8,128)(2,1)S(1)}, bf16[144,512]{1,0:T(8,128)(2,1)S(1)}, u32[]{:S(2)}, u32[]{:S(2)}) collective-permute-start(bf16[144,512]{1,0:T(8,128)(2,1)S(1)} %get-tuple-element.37), channel_id=1, source_target_pairs={{0,17},{1,16},{2,19},{3,18},{4,21},{5,20},{6,23},{7,22},{8,25},{9,... | collective-permute-start | bytes 442376 | tf_op jit(solution)/shard_map/ppermute | solution.py:47
  69.9 0.9 collective-permute-start.21
  70.9 0.4 add_convert_fusion.3
  71.3 2.0 %collective-permute-start.27 = (bf16[2,2,32,1024]{3,2,1,0:T(8,128)(2,1)S(1)}, bf16[2,2,32,1024]{3,2,1,0:T(8,128)(2,1)S(1)}, u32[]{:S(2)}, u32[]{:S(2)}) collective-permute-start(bf16[2,2,32,1024]{3,2,1,0:T(8,128)(2,1)S(1)} %get-tuple-element.46), channel_id=1, source_target_pairs={{0,96},{8,104},{16,112},{24,120},{32,64},{40,72},{48,80},{56,88},{... | collective-permute-start | bytes 786440 | tf_op jit(solution)/shard_map/ppermute | solution.py:38
  73.2 2.7 %collective-permute-done.20 = bf16[144,512]{1,0:T(8,128)(2,1)S(1)} collective-permute-done((bf16[144,512]{1,0:T(8,128)(2,1)S(1)}, bf16[144,512]{1,0:T(8,128)(2,1)S(1)}, u32[]{:S(2)}, u32[]{:S(2)}) %collective-permute-start.20) | collective-permute-done | bytes 147488 | tf_op jit(solution)/shard_map/ppermute | solution.py:47
  76.0 1.6 %collective-permute-start.25 = (bf16[2,2,32,1024]{3,2,1,0:T(8,128)(2,1)S(1)}, bf16[2,2,32,1024]{3,2,1,0:T(8,128)(2,1)S(1)}, u32[]{:S(2)}, u32[]{:S(2)}) collective-permute-start(bf16[2,2,32,1024]{3,2,1,0:T(8,128)(2,1)S(1)} %get-tuple-element.48), channel_id=1, source_target_pairs={{0,64},{8,72},{16,80},{24,88},{32,96},{40,104},{48,112},{56,120},{... | collective-permute-start | bytes 786440 | tf_op jit(solution)/shard_map/ppermute | solution.py:38
  77.6 0.6 collective-permute-done.19
  78.1 0.1 add_convert_fusion.5
  78.2 1.6 %collective-permute-start.22 = (bf16[144,512]{1,0:T(8,128)(2,1)S(1)}, bf16[144,512]{1,0:T(8,128)(2,1)S(1)}, u32[]{:S(2)}, u32[]{:S(2)}) collective-permute-start(bf16[144,512]{1,0:T(8,128)(2,1)S(1)} %add_convert_fusion.5), channel_id=1, source_target_pairs={{0,2},{1,3},{2,0},{3,1},{4,6},{5,7},{6,4},{7,5},{8,10},{9,11},{10,... | collective-permute-start | bytes 442376 | tf_op jit(solution)/shard_map/ppermute | solution.py:42
  79.8 0.3 collective-permute-done.27
  80.1 1.6 %collective-permute-done.26 = bf16[2,2,32,1024]{3,2,1,0:T(8,128)(2,1)S(1)} collective-permute-done((bf16[2,2,32,1024]{3,2,1,0:T(8,128)(2,1)S(1)}, bf16[2,2,32,1024]{3,2,1,0:T(8,128)(2,1)S(1)}, u32[]{:S(2)}, u32[]{:S(2)}) %collective-permute-start.26) | collective-permute-done | bytes 262176 | tf_op jit(solution)/shard_map/ppermute | solution.py:38
  81.7 4.9 %collective-permute-done.25 = bf16[2,2,32,1024]{3,2,1,0:T(8,128)(2,1)S(1)} collective-permute-done((bf16[2,2,32,1024]{3,2,1,0:T(8,128)(2,1)S(1)}, bf16[2,2,32,1024]{3,2,1,0:T(8,128)(2,1)S(1)}, u32[]{:S(2)}, u32[]{:S(2)}) %collective-permute-start.25) | collective-permute-done | bytes 262176 | tf_op jit(solution)/shard_map/ppermute | solution.py:38
  86.7 2.8 %collective-permute-start.28 = (bf16[2,32,1024]{2,1,0:T(8,128)(2,1)S(1)}, bf16[2,32,1024]{2,1,0:T(8,128)(2,1)S(1)}, u32[]{:S(2)}, u32[]{:S(2)}) collective-permute-start(bf16[2,32,1024]{2,1,0:T(8,128)(2,1)S(1)} %fusion), channel_id=1, source_target_pairs={{0,16},{8,24},{16,0},{24,8},{32,48},{40,56},{48,32},{56,40},{64,80... | collective-permute-start | bytes 393224 | tf_op jit(solution)/shard_map/ppermute | solution.py:38
  89.5 2.8 %collective-permute-start.23 = (bf16[144,512]{1,0:T(8,128)(2,1)S(1)}, bf16[144,512]{1,0:T(8,128)(2,1)S(1)}, u32[]{:S(2)}, u32[]{:S(2)}) collective-permute-start(bf16[144,512]{1,0:T(8,128)(2,1)S(1)} %add_convert_fusion.4.mine_ref), channel_id=1, source_target_pairs={{0,6},{1,7},{2,4},{3,5},{4,2},{5,3},{6,0},{7,1},{8,14},{9,15},{10,... | collective-permute-start | bytes 442376 | tf_op jit(solution)/shard_map/ppermute | solution.py:42
  92.4 0.9 collective-permute-done.28
  93.2 0.8 convert_add_fusion
  94.0 2.0 %collective-permute-done.23.other_ref = bf16[144,512]{1,0:T(8,128)(2,1)S(1)} collective-permute-done((bf16[144,512]{1,0:T(8,128)(2,1)S(1)}, bf16[144,512]{1,0:T(8,128)(2,1)S(1)}, u32[]{:S(2)}, u32[]{:S(2)}) %collective-permute-start.23) | collective-permute-done | bytes 147488 | tf_op jit(solution)/shard_map/ppermute | solution.py:42
  96.0 0.7 final.1
  (33 shorter events, 0.3 us)
Async XLA Ops:
  1.6 10.2 %collective-permute-start.10 = (bf16[144,512]{1,0:T(8,128)(2,1)S(1)}, bf16[144,512]{1,0:T(8,128)(2,1)S(1)}, u32[]{:S(2)}, u32[]{:S(2)}) collective-permute-start(bf16[144,512]{1,0:T(8,128)(2,1)S(1)} %pack.1.refs_0_.refs_9_), channel_id=1, source_target_pairs={{0,96},{8,104},{16,112},{24,120},{32,64},{40,72},{48,80},{56,88},{... | collective-permute-start | bytes 442376 | tf_op jit(solution)/shard_map/ppermute | solution.py:38
  4.8 7.0 %collective-permute-start.9 = (bf16[144,512]{1,0:T(8,128)(2,1)S(1)}, bf16[144,512]{1,0:T(8,128)(2,1)S(1)}, u32[]{:S(2)}, u32[]{:S(2)}) collective-permute-start(bf16[144,512]{1,0:T(8,128)(2,1)S(1)} %pack.1.refs_0_.refs_9_), channel_id=1, source_target_pairs={{0,64},{8,72},{16,80},{24,88},{32,96},{40,104},{48,112},{56,120},{... | collective-permute-start | bytes 442376 | tf_op jit(solution)/shard_map/ppermute | solution.py:38
  5.4 7.2 %collective-permute-start = (bf16[144,512]{1,0:T(8,128)(2,1)S(1)}, bf16[144,512]{1,0:T(8,128)(2,1)S(1)}, u32[]{:S(2)}, u32[]{:S(2)}) collective-permute-start(bf16[144,512]{1,0:T(8,128)(2,1)S(1)} %pack.1.refs_0_.refs_9_), channel_id=1, source_target_pairs={{0,16},{8,24},{16,0},{24,8},{32,48},{40,56},{48,32},{56,40},{64,80... | collective-permute-start | bytes 442376 | tf_op jit(solution)/shard_map/ppermute | solution.py:38
  9.3 6.0 %collective-permute-start.11 = (bf16[144,512]{1,0:T(8,128)(2,1)S(1)}, bf16[144,512]{1,0:T(8,128)(2,1)S(1)}, u32[]{:S(2)}, u32[]{:S(2)}) collective-permute-start(bf16[144,512]{1,0:T(8,128)(2,1)S(1)} %pack.1.refs_0_.refs_9_), channel_id=1, source_target_pairs={{0,8},{8,0},{16,24},{24,16},{32,40},{40,32},{48,56},{56,48},{64,72... | collective-permute-start | bytes 442376 | tf_op jit(solution)/shard_map/ppermute | solution.py:38
  9.3 6.3 %collective-permute-start.8 = (bf16[144,512]{1,0:T(8,128)(2,1)S(1)}, bf16[144,512]{1,0:T(8,128)(2,1)S(1)}, u32[]{:S(2)}, u32[]{:S(2)}) collective-permute-start(bf16[144,512]{1,0:T(8,128)(2,1)S(1)} %pack.1.refs_0_.refs_9_), channel_id=1, source_target_pairs={{0,32},{8,40},{16,48},{24,56},{32,0},{40,8},{48,16},{56,24},{64,96... | collective-permute-start | bytes 442376 | tf_op jit(solution)/shard_map/ppermute | solution.py:38
  11.8 4.9 %collective-permute-start.14 = (bf16[144,512]{1,0:T(8,128)(2,1)S(1)}, bf16[144,512]{1,0:T(8,128)(2,1)S(1)}, u32[]{:S(2)}, u32[]{:S(2)}) collective-permute-start(bf16[144,512]{1,0:T(8,128)(2,1)S(1)} %collective-permute-done.10.refs_3_.refs_12_), channel_id=1, source_target_pairs={{0,8},{8,0},{16,24},{24,16},{32,40},{40,32},{48,56},{56,48},{64,72... | collective-permute-start | bytes 442376 | tf_op jit(solution)/shard_map/ppermute | solution.py:38
  11.8 8.2 %collective-permute-start.13 = (bf16[144,512]{1,0:T(8,128)(2,1)S(1)}, bf16[144,512]{1,0:T(8,128)(2,1)S(1)}, u32[]{:S(2)}, u32[]{:S(2)}) collective-permute-start(bf16[144,512]{1,0:T(8,128)(2,1)S(1)} %collective-permute-done.9.refs_2_.refs_11_), channel_id=1, source_target_pairs={{0,8},{8,0},{16,24},{24,16},{32,40},{40,32},{48,56},{56,48},{64,72... | collective-permute-start | bytes 442376 | tf_op jit(solution)/shard_map/ppermute | solution.py:38
  12.6 9.2 %collective-permute-start.3 = (bf16[144,512]{1,0:T(8,128)(2,1)S(1)}, bf16[144,512]{1,0:T(8,128)(2,1)S(1)}, u32[]{:S(2)}, u32[]{:S(2)}) collective-permute-start(bf16[144,512]{1,0:T(8,128)(2,1)S(1)} %collective-permute-done.refs_1_), channel_id=1, source_target_pairs={{0,96},{8,104},{16,112},{24,120},{32,64},{40,72},{48,80},{56,88},{... | collective-permute-start | bytes 442376 | tf_op jit(solution)/shard_map/ppermute | solution.py:38
  15.2 8.2 %collective-permute-start.2 = (bf16[144,512]{1,0:T(8,128)(2,1)S(1)}, bf16[144,512]{1,0:T(8,128)(2,1)S(1)}, u32[]{:S(2)}, u32[]{:S(2)}) collective-permute-start(bf16[144,512]{1,0:T(8,128)(2,1)S(1)} %collective-permute-done.refs_1_), channel_id=1, source_target_pairs={{0,64},{8,72},{16,80},{24,88},{32,96},{40,104},{48,112},{56,120},{... | collective-permute-start | bytes 442376 | tf_op jit(solution)/shard_map/ppermute | solution.py:38
  15.5 7.9 %collective-permute-start.1 = (bf16[144,512]{1,0:T(8,128)(2,1)S(1)}, bf16[144,512]{1,0:T(8,128)(2,1)S(1)}, u32[]{:S(2)}, u32[]{:S(2)}) collective-permute-start(bf16[144,512]{1,0:T(8,128)(2,1)S(1)} %collective-permute-done.refs_1_), channel_id=1, source_target_pairs={{0,32},{8,40},{16,48},{24,56},{32,0},{40,8},{48,16},{56,24},{64,96... | collective-permute-start | bytes 442376 | tf_op jit(solution)/shard_map/ppermute | solution.py:38
  16.7 7.3 %collective-permute-start.12 = (bf16[144,512]{1,0:T(8,128)(2,1)S(1)}, bf16[144,512]{1,0:T(8,128)(2,1)S(1)}, u32[]{:S(2)}, u32[]{:S(2)}) collective-permute-start(bf16[144,512]{1,0:T(8,128)(2,1)S(1)} %collective-permute-done.8.refs_1_.refs_10_), channel_id=1, source_target_pairs={{0,8},{8,0},{16,24},{24,16},{32,40},{40,32},{48,56},{56,48},{64,72... | collective-permute-start | bytes 442376 | tf_op jit(solution)/shard_map/ppermute | solution.py:38
  19.9 8.3 %collective-permute-start.4 = (bf16[144,512]{1,0:T(8,128)(2,1)S(1)}, bf16[144,512]{1,0:T(8,128)(2,1)S(1)}, u32[]{:S(2)}, u32[]{:S(2)}) collective-permute-start(bf16[144,512]{1,0:T(8,128)(2,1)S(1)} %collective-permute-done.refs_1_), channel_id=1, source_target_pairs={{0,8},{8,0},{16,24},{24,16},{32,40},{40,32},{48,56},{56,48},{64,72... | collective-permute-start | bytes 442376 | tf_op jit(solution)/shard_map/ppermute | solution.py:38
  21.8 6.5 %collective-permute-start.7 = (bf16[144,512]{1,0:T(8,128)(2,1)S(1)}, bf16[144,512]{1,0:T(8,128)(2,1)S(1)}, u32[]{:S(2)}, u32[]{:S(2)}) collective-permute-start(bf16[144,512]{1,0:T(8,128)(2,1)S(1)} %collective-permute-done.3.refs_4_), channel_id=1, source_target_pairs={{0,8},{8,0},{16,24},{24,16},{32,40},{40,32},{48,56},{56,48},{64,72... | collective-permute-start | bytes 442376 | tf_op jit(solution)/shard_map/ppermute | solution.py:38
  23.5 4.8 %collective-permute-start.6 = (bf16[144,512]{1,0:T(8,128)(2,1)S(1)}, bf16[144,512]{1,0:T(8,128)(2,1)S(1)}, u32[]{:S(2)}, u32[]{:S(2)}) collective-permute-start(bf16[144,512]{1,0:T(8,128)(2,1)S(1)} %collective-permute-done.2.refs_3_), channel_id=1, source_target_pairs={{0,8},{8,0},{16,24},{24,16},{32,40},{40,32},{48,56},{56,48},{64,72... | collective-permute-start | bytes 442376 | tf_op jit(solution)/shard_map/ppermute | solution.py:38
  23.5 4.9 %collective-permute-start.5 = (bf16[144,512]{1,0:T(8,128)(2,1)S(1)}, bf16[144,512]{1,0:T(8,128)(2,1)S(1)}, u32[]{:S(2)}, u32[]{:S(2)}) collective-permute-start(bf16[144,512]{1,0:T(8,128)(2,1)S(1)} %collective-permute-done.1.refs_2_), channel_id=1, source_target_pairs={{0,8},{8,0},{16,24},{24,16},{32,40},{40,32},{48,56},{56,48},{64,72... | collective-permute-start | bytes 442376 | tf_op jit(solution)/shard_map/ppermute | solution.py:38
  28.3 8.6 %copy-start = (bf16[512,1024]{1,0:T(8,128)(2,1)S(1)}, bf16[512,1024]{1,0:T(8,128)(2,1)}, u32[]{:S(2)}) copy-start(bf16[512,1024]{1,0:T(8,128)(2,1)} %up_key_ref.3) | copy-start | bytes 3145732
  28.3 8.5 %copy-start.1 = (bf16[128,1536]{1,0:T(8,128)(2,1)S(1)}, bf16[128,1536]{1,0:T(8,128)(2,1)}, u32[]{:S(2)}) copy-start(bf16[128,1536]{1,0:T(8,128)(2,1)} %query_ref.3) | copy-start | bytes 1179652
  28.4 8.5 %copy-start.2 = (bf16[128,1024]{1,0:T(8,128)(2,1)S(1)}, bf16[128,1024]{1,0:T(8,128)(2,1)}, u32[]{:S(2)}) copy-start(bf16[128,1024]{1,0:T(8,128)(2,1)} %out_grad_ref.3) | copy-start | bytes 786436
  36.8 11.2 %collective-permute-start.15 = (bf16[1152,512]{1,0:T(8,128)(2,1)S(1)}, bf16[1152,512]{1,0:T(8,128)(2,1)S(1)}, u32[]{:S(2)}, u32[]{:S(2)}) collective-permute-start(bf16[1152,512]{1,0:T(8,128)(2,1)S(1)} %get-tuple-element.32), channel_id=1, source_target_pairs={{0,8},{8,0},{16,24},{24,16},{32,40},{40,32},{48,56},{56,48},{64,72... | collective-permute-start | bytes 3538952 | tf_op jit(solution)/shard_map/ppermute | solution.py:38
  44.6 26.3 %collective-permute-start.24 = (bf16[8,2,32,1024]{3,2,1,0:T(8,128)(2,1)S(1)}, bf16[8,2,32,1024]{3,2,1,0:T(8,128)(2,1)S(1)}, u32[]{:S(2)}, u32[]{:S(2)}) collective-permute-start(bf16[8,2,32,1024]{3,2,1,0:T(8,128)(2,1)S(1)} %get-tuple-element.36), channel_id=1, source_target_pairs={{0,8},{8,0},{16,24},{24,16},{32,40},{40,32},{48,56},{56,48},{64,72... | collective-permute-start | bytes 3145736 | tf_op jit(solution)/shard_map/ppermute | solution.py:38
  48.2 10.0 %collective-permute-start.17 = (bf16[288,512]{1,0:T(8,128)(2,1)S(1)}, bf16[288,512]{1,0:T(8,128)(2,1)S(1)}, u32[]{:S(2)}, u32[]{:S(2)}) collective-permute-start(bf16[288,512]{1,0:T(8,128)(2,1)S(1)} %pad_maximum_fusion.1), channel_id=1, source_target_pairs={{0,32},{8,40},{16,48},{24,56},{32,0},{40,8},{48,16},{56,24},{64,96... | collective-permute-start | bytes 884744 | tf_op jit(solution)/shard_map/ppermute | solution.py:38
  48.7 15.1 %collective-permute-start.18 = (bf16[288,512]{1,0:T(8,128)(2,1)S(1)}, bf16[288,512]{1,0:T(8,128)(2,1)S(1)}, u32[]{:S(2)}, u32[]{:S(2)}) collective-permute-start(bf16[288,512]{1,0:T(8,128)(2,1)S(1)} %pad_maximum_fusion.2), channel_id=1, source_target_pairs={{0,96},{8,104},{16,112},{24,120},{32,64},{40,72},{48,80},{56,88},{... | collective-permute-start | bytes 884744 | tf_op jit(solution)/shard_map/ppermute | solution.py:38
  50.7 14.9 %collective-permute-start.16 = (bf16[288,512]{1,0:T(8,128)(2,1)S(1)}, bf16[288,512]{1,0:T(8,128)(2,1)S(1)}, u32[]{:S(2)}, u32[]{:S(2)}) collective-permute-start(bf16[288,512]{1,0:T(8,128)(2,1)S(1)} %pad_maximum_fusion), channel_id=1, source_target_pairs={{0,64},{8,72},{16,80},{24,88},{32,96},{40,104},{48,112},{56,120},{... | collective-permute-start | bytes 884744 | tf_op jit(solution)/shard_map/ppermute | solution.py:38
  65.8 10.2 %collective-permute-start.20 = (bf16[144,512]{1,0:T(8,128)(2,1)S(1)}, bf16[144,512]{1,0:T(8,128)(2,1)S(1)}, u32[]{:S(2)}, u32[]{:S(2)}) collective-permute-start(bf16[144,512]{1,0:T(8,128)(2,1)S(1)} %get-tuple-element.37), channel_id=1, source_target_pairs={{0,17},{1,16},{2,19},{3,18},{4,21},{5,20},{6,23},{7,22},{8,25},{9,... | collective-permute-start | bytes 442376 | tf_op jit(solution)/shard_map/ppermute | solution.py:47
  69.9 8.2 %collective-permute-start.19 = (bf16[144,512]{1,0:T(8,128)(2,1)S(1)}, bf16[144,512]{1,0:T(8,128)(2,1)S(1)}, u32[]{:S(2)}, u32[]{:S(2)}) collective-permute-start(bf16[144,512]{1,0:T(8,128)(2,1)S(1)} %get-tuple-element.37), channel_id=1, source_target_pairs={{0,16},{8,24},{16,0},{24,8},{32,48},{40,56},{48,32},{56,40},{64,80... | collective-permute-start | bytes 442376 | tf_op jit(solution)/shard_map/ppermute | solution.py:38
  69.9 8.2 %collective-permute-start.21 = (bf16[144,512]{1,0:T(8,128)(2,1)S(1)}, bf16[144,512]{1,0:T(8,128)(2,1)S(1)}, u32[]{:S(2)}, u32[]{:S(2)}) collective-permute-start(bf16[144,512]{1,0:T(8,128)(2,1)S(1)} %get-tuple-element.38), channel_id=1, source_target_pairs={{0,1},{1,0},{2,3},{3,2},{4,5},{5,4},{6,7},{7,6},{8,9},{9,8},{10,11... | collective-permute-start | bytes 442376 | tf_op jit(solution)/shard_map/ppermute | solution.py:42
  71.3 8.8 %collective-permute-start.27 = (bf16[2,2,32,1024]{3,2,1,0:T(8,128)(2,1)S(1)}, bf16[2,2,32,1024]{3,2,1,0:T(8,128)(2,1)S(1)}, u32[]{:S(2)}, u32[]{:S(2)}) collective-permute-start(bf16[2,2,32,1024]{3,2,1,0:T(8,128)(2,1)S(1)} %get-tuple-element.46), channel_id=1, source_target_pairs={{0,96},{8,104},{16,112},{24,120},{32,64},{40,72},{48,80},{56,88},{... | collective-permute-start | bytes 786440 | tf_op jit(solution)/shard_map/ppermute | solution.py:38
  73.2 8.4 %collective-permute-start.26 = (bf16[2,2,32,1024]{3,2,1,0:T(8,128)(2,1)S(1)}, bf16[2,2,32,1024]{3,2,1,0:T(8,128)(2,1)S(1)}, u32[]{:S(2)}, u32[]{:S(2)}) collective-permute-start(bf16[2,2,32,1024]{3,2,1,0:T(8,128)(2,1)S(1)} %get-tuple-element.47), channel_id=1, source_target_pairs={{0,32},{8,40},{16,48},{24,56},{32,0},{40,8},{48,16},{56,24},{64,96... | collective-permute-start | bytes 786440 | tf_op jit(solution)/shard_map/ppermute | solution.py:38
  76.0 10.7 %collective-permute-start.25 = (bf16[2,2,32,1024]{3,2,1,0:T(8,128)(2,1)S(1)}, bf16[2,2,32,1024]{3,2,1,0:T(8,128)(2,1)S(1)}, u32[]{:S(2)}, u32[]{:S(2)}) collective-permute-start(bf16[2,2,32,1024]{3,2,1,0:T(8,128)(2,1)S(1)} %get-tuple-element.48), channel_id=1, source_target_pairs={{0,64},{8,72},{16,80},{24,88},{32,96},{40,104},{48,112},{56,120},{... | collective-permute-start | bytes 786440 | tf_op jit(solution)/shard_map/ppermute | solution.py:38
  78.2 11.3 %collective-permute-start.22 = (bf16[144,512]{1,0:T(8,128)(2,1)S(1)}, bf16[144,512]{1,0:T(8,128)(2,1)S(1)}, u32[]{:S(2)}, u32[]{:S(2)}) collective-permute-start(bf16[144,512]{1,0:T(8,128)(2,1)S(1)} %add_convert_fusion.5), channel_id=1, source_target_pairs={{0,2},{1,3},{2,0},{3,1},{4,6},{5,7},{6,4},{7,5},{8,10},{9,11},{10,... | collective-permute-start | bytes 442376 | tf_op jit(solution)/shard_map/ppermute | solution.py:42
  86.7 6.6 %collective-permute-start.28 = (bf16[2,32,1024]{2,1,0:T(8,128)(2,1)S(1)}, bf16[2,32,1024]{2,1,0:T(8,128)(2,1)S(1)}, u32[]{:S(2)}, u32[]{:S(2)}) collective-permute-start(bf16[2,32,1024]{2,1,0:T(8,128)(2,1)S(1)} %fusion), channel_id=1, source_target_pairs={{0,16},{8,24},{16,0},{24,8},{32,48},{40,56},{48,32},{56,40},{64,80... | collective-permute-start | bytes 393224 | tf_op jit(solution)/shard_map/ppermute | solution.py:38
  89.5 6.4 %collective-permute-start.23 = (bf16[144,512]{1,0:T(8,128)(2,1)S(1)}, bf16[144,512]{1,0:T(8,128)(2,1)S(1)}, u32[]{:S(2)}, u32[]{:S(2)}) collective-permute-start(bf16[144,512]{1,0:T(8,128)(2,1)S(1)} %add_convert_fusion.4.mine_ref), channel_id=1, source_target_pairs={{0,6},{1,7},{2,4},{3,5},{4,2},{5,3},{6,0},{7,1},{8,14},{9,15},{10,... | collective-permute-start | bytes 442376 | tf_op jit(solution)/shard_map/ppermute | solution.py:42

commit v4 on v3

--- a/solution.py
+++ b/solution.py
@@ -82,8 +82,9 @@
         out_ref[CHUNK:, g * LANES : (g + 1) * LANES] = turned_ref[g * ROPE_ROWS : (g + 1) * ROPE_ROWS, :]
 
 
-def final_kernel(mine_ref, other_ref, latent_ref, turned_ref):
-    total = mine_ref[...].astype(F32) + other_ref[...].astype(F32)
+def final_kernel(mine_ref, second_ref, first_ref, third_ref, latent_ref, turned_ref):
+    total = mine_ref[...].astype(F32) + second_ref[...].astype(F32)
+    total = total + (first_ref[...].astype(F32) + third_ref[...].astype(F32))
     latent_ref[...] = total[:CHUNK]
     turned_ref[...] = rope_rows(total[CHUNK:])
 
@@ -434,19 +435,18 @@
     first = swap_ctx(other, 2)
     second = swap_both(other, 2, 1)
     third = swap_head(mine, 1)
-    mine = spread_sum([mine, first, second, third])
-    mine = mine.astype(BF16)
-    other = swap_head(mine, 2)
-    mine = spread_sum([mine, other]).astype(BF16)
-    other = swap_head(mine, 6)
+    mine = (spread_sum([mine, third]) + spread_sum([first, second])).astype(BF16)
+    others = []
+    for mask in (4, 2, 6):
+        others.append(swap_head(mine, mask))
     latent_grad, rope_turned = pl.pallas_call(
         final_kernel,
         out_shape=(jax.ShapeDtypeStruct((tok, D_LATENT), F32), jax.ShapeDtypeStruct((ROPE, tok), F32)),
-        in_specs=[vmem] * 2,
+        in_specs=[vmem] * 4,
         out_specs=(vmem, vmem),
         compiler_params=pltpu.CompilerParams(vmem_limit_bytes=4 << 20),
         name="final",
-    )(*in_vmem(mine, other))
+    )(*in_vmem(mine, *others))
     rope_grad = rope_turned.T
 
     weight_got = swap_ctx(weight_send, 1)

time: 96.9 us -> 93.4 us (0.964)
  waiting for transfers between devices: 31.2 us -> 24.3 us
  starting transfers between devices: 34.6 us -> 37.3 us
    ppermute x25, waiting for transfers between devices: 26.6 us -> 19.2 us  [swap_ctx(): return lax.ppermute(value, 'ctx', [(i, i ^ mask) for i in range(CTX)])]
    ppermute x3 -> x4, waiting for transfers between devices: 1.96 us -> 5.14 us  [swap_head(): return lax.ppermute(value, 'head', [(i, i ^ mask) for i in range(HEAD)])]
    ppermute x1, waiting for transfers between devices: 2.71 us -> 0.01 us  [swap_both(): lax.ppermute(value, ('ctx', 'head'), [(i, i ^ mask) for i in range(CTX *...]
    ppermute x25, starting transfers between devices: 25.1 us -> 26.5 us  [swap_ctx(): return lax.ppermute(value, 'ctx', [(i, i ^ mask) for i in range(CTX)])]
    ppermute x3 -> x4, starting transfers between devices: 5.35 us -> 6.7 us  [swap_head(): return lax.ppermute(value, 'head', [(i, i ^ mask) for i in range(HEAD)])]
  transfers between devices with their start and end apart: 29 -> 30, of which waited for: 15 -> 11; matrix products, arithmetic and copies ran while one was open for 2% -> 2% of each run, Pallas kernels for 19% -> 20%
where the time goes in v4:
time: 93.4 us; the launch traced here: 92.5 us
  starting transfers between devices  37.3 us (40%)
  Pallas kernels  28.2 us (30%)
  waiting for transfers between devices  24.3 us (26%)
  other arithmetic  1.84 us (2%)
    ppermute x25, starting transfers between devices, swap_ctx(): return lax.ppermute(value, 'ctx', [(i, i ^ mask) for i in range(CTX)])  26.5 us
    ppermute x25, waiting for transfers between devices, swap_ctx(): return lax.ppermute(value, 'ctx', [(i, i ^ mask) for i in range(CTX)])  19.2 us
    pallas_call x1, Pallas kernels, per_device(): pl.pallas_call(scores_kernel, grid=(PAIRS + 1,), out_shape=(pair_shape, p...  8.41 us
    pallas_call x1, Pallas kernels, per_device(): pl.pallas_call(weights_kernel, grid=(PAIRS,), out_shape=(jax.ShapeDtypeSt...  7.68 us
    ppermute x4, starting transfers between devices, swap_head(): return lax.ppermute(value, 'head', [(i, i ^ mask) for i in range(HEAD)])  6.7 us
    ppermute x4, waiting for transfers between devices, swap_head(): return lax.ppermute(value, 'head', [(i, i ^ mask) for i in range(HEAD)])  5.14 us
    pallas_call x1, Pallas kernels, per_device(): pl.pallas_call(early_kernel, grid=(PAIRS,), out_shape=(pltpu.VMEM((PAIRS,...  4.3 us
    ppermute x1, starting transfers between devices, swap_both(): lax.ppermute(value, ('ctx', 'head'), [(i, i ^ mask) for i in range(CTX *...  4.11 us
  transfers between devices with their start and end apart: 30, of which 11 were waited for; matrix products, arithmetic and copies ran while one was open for 2% of the time, Pallas kernels for 20%

profile of v4, /device:TPU:0, one launch (start us, length us, event | category | flops | bytes accessed | tf_op | source)
XLA Modules:
  0.0 92.5 jit_solution(7258982370030350086)
XLA Ops:
  0.6 0.9 pack.1.refs_0_.refs_9_
  1.6 3.2 %collective-permute-start.10 = (bf16[144,512]{1,0:T(8,128)(2,1)S(1)}, bf16[144,512]{1,0:T(8,128)(2,1)S(1)}, u32[]{:S(2)}, u32[]{:S(2)}) collective-permute-start(bf16[144,512]{1,0:T(8,128)(2,1)S(1)} %pack.1.refs_0_.refs_9_), channel_id=1, source_target_pairs={{0,96},{8,104},{16,112},{24,120},{32,64},{40,72},{48,80},{56,88},{... | collective-permute-start | bytes 442376 | tf_op jit(solution)/shard_map/ppermute | solution.py:38
  4.8 0.6 collective-permute-start.9
  5.4 3.9 %collective-permute-start = (bf16[144,512]{1,0:T(8,128)(2,1)S(1)}, bf16[144,512]{1,0:T(8,128)(2,1)S(1)}, u32[]{:S(2)}, u32[]{:S(2)}) collective-permute-start(bf16[144,512]{1,0:T(8,128)(2,1)S(1)} %pack.1.refs_0_.refs_9_), channel_id=1, source_target_pairs={{0,16},{8,24},{16,0},{24,8},{32,48},{40,56},{48,32},{56,40},{64,80... | collective-permute-start | bytes 442376 | tf_op jit(solution)/shard_map/ppermute | solution.py:38
  9.3 0.5 collective-permute-start.8
  9.7 2.0 %collective-permute-done.10.refs_3_.refs_12_ = bf16[144,512]{1,0:T(8,128)(2,1)S(1)} collective-permute-done((bf16[144,512]{1,0:T(8,128)(2,1)S(1)}, bf16[144,512]{1,0:T(8,128)(2,1)S(1)}, u32[]{:S(2)}, u32[]{:S(2)}) %collective-permute-start.10) | collective-permute-done | bytes 147488 | tf_op jit(solution)/shard_map/ppermute | solution.py:38
  11.8 0.5 collective-permute-start.13
  12.3 0.3 collective-permute-done.refs_1_
  12.6 2.7 %collective-permute-start.3 = (bf16[144,512]{1,0:T(8,128)(2,1)S(1)}, bf16[144,512]{1,0:T(8,128)(2,1)S(1)}, u32[]{:S(2)}, u32[]{:S(2)}) collective-permute-start(bf16[144,512]{1,0:T(8,128)(2,1)S(1)} %collective-permute-done.refs_1_), channel_id=1, source_target_pairs={{0,96},{8,104},{16,112},{24,120},{32,64},{40,72},{48,80},{56,88},{... | collective-permute-start | bytes 442376 | tf_op jit(solution)/shard_map/ppermute | solution.py:38
  15.2 0.2 collective-permute-start.2
  15.5 0.1 collective-permute-done.8.refs_1_.refs_10_
  15.5 1.1 %collective-permute-start.1 = (bf16[144,512]{1,0:T(8,128)(2,1)S(1)}, bf16[144,512]{1,0:T(8,128)(2,1)S(1)}, u32[]{:S(2)}, u32[]{:S(2)}) collective-permute-start(bf16[144,512]{1,0:T(8,128)(2,1)S(1)} %collective-permute-done.refs_1_), channel_id=1, source_target_pairs={{0,32},{8,40},{16,48},{24,56},{32,0},{40,8},{48,16},{56,24},{64,96... | collective-permute-start | bytes 442376 | tf_op jit(solution)/shard_map/ppermute | solution.py:38
  16.7 3.3 %prep.1 = (bf16[4,256,576]{2,1,0:T(8,128)(2,1)S(1)}, bf16[4,256,512]{2,1,0:T(8,128)(2,1)S(1)}, f32[2048,128]{1,0:T(8,128)S(1)}) custom-call(s32[1]{0:T(128)} %bitcast.own_ref.refs_0_, s32[32]{0:T(128)} %order_ref.1, bf16[128,1536]{1,0:T(8,128)(2,1)} %query_ref.3, bf16[512,1024]{1,0:T(8,128)(2,1)} %up_key_ref.3, bf16[128,1024]{1,0:T(8,128)(2,1)} %out_grad_ref.3, ...), custom_call_target="tpu_custom_call" | custom-call | flops 300000000 | bytes 10000000 | tf_op jit(solution)/shard_map/prep/pallas_call | solution.py:332
  19.9 0.6 collective-permute-start.4
  20.5 1.2 %collective-permute-done.3.refs_4_ = bf16[144,512]{1,0:T(8,128)(2,1)S(1)} collective-permute-done((bf16[144,512]{1,0:T(8,128)(2,1)S(1)}, bf16[144,512]{1,0:T(8,128)(2,1)S(1)}, u32[]{:S(2)}, u32[]{:S(2)}) %collective-permute-start.3) | collective-permute-done | bytes 147488 | tf_op jit(solution)/shard_map/ppermute | solution.py:38
  21.8 1.7 %collective-permute-done.2.refs_3_ = bf16[144,512]{1,0:T(8,128)(2,1)S(1)} collective-permute-done((bf16[144,512]{1,0:T(8,128)(2,1)S(1)}, bf16[144,512]{1,0:T(8,128)(2,1)S(1)}, u32[]{:S(2)}, u32[]{:S(2)}) %collective-permute-start.2) | collective-permute-done | bytes 147488 | tf_op jit(solution)/shard_map/ppermute | solution.py:38
  23.5 0.5 collective-permute-start.5
  24.0 4.3 %early.1 = (bf16[4,1024,256]{2,1,0:T(8,128)(2,1)S(1)}, f32[4,1024,256]{2,1,0:T(8,128)S(1)}, f32[4,8,256]{2,1,0:T(8,128)S(1)}) custom-call(bf16[144,512]{1,0:T(8,128)(2,1)S(1)} %pack.1.refs_0_.refs_9_, bf16[144,512]{1,0:T(8,128)(2,1)S(1)} %collective-permute-done.8.refs_1_.refs_10_, bf16[144,512]{1,0:T(8,128)(2,1)S(1)} %collective-permute-done.9.refs_2_.refs_11_, ...), custom_call_target="tpu_custom_call" | custom-call | flops 3000000000 | bytes 10000000 | tf_op jit(solution)/shard_map/early/pallas_call | solution.py:364
  28.3 0.0 copy-start
  28.4 8.4 %scores.1 = (bf16[4,2048,256]{2,1,0:T(8,128)(2,1)S(1)}, bf16[4,2048,256]{2,1,0:T(8,128)(2,1)S(1)}, bf16[1152,512]{1,0:T(8,128)(2,1)S(1)}, bf16[576,1024]{1,0:T(8,128)(2,1)S(1)}, bf16[576,1024]{1,0:T(8,128)(2,1)S(1)}) custom-call(s32[1]{0:T(128)} %bitcast.own_ref.refs_0_, bf16[144,512]{1,0:T(8,128)(2,1)S(1)} %collective-permute-done.refs_1_, ...), custom_call_target="tpu_custom_call" | custom-call | flops 6000000000 | bytes 14000000 | tf_op jit(solution)/shard_map/scores/pallas_call | solution.py:379
  36.8 0.1 collective-permute-start.15
  36.9 7.7 %weights.1 = (bf16[128,1536]{1,0:T(8,128)(2,1)}, bf16[8,2,32,1024]{3,2,1,0:T(8,128)(2,1)S(1)}, bf16[8,2,32,1024]{3,2,1,0:T(8,128)(2,1)S(1)}) custom-call(s32[1]{0:T(128)} %bitcast.own_ref.refs_0_, bf16[576,1024]{1,0:T(8,128)(2,1)S(1)} %get-tuple-element.27.early_ref, bf16[576,1024]{1,0:T(8,128)(2,1)S(1)} %get-tuple-element.28.late_ref, ...), custom_call_target="tpu_custom_call" | custom-call | flops 5000000000 | bytes 14000000 | tf_op jit(solution)/shard_map/weights/pallas_call | solution.py:410
  44.6 0.5 collective-permute-start.25
  45.1 2.9 %keep.1 = bf16[1152,512]{1,0:T(8,128)(2,1)S(1)} custom-call(bf16[4,2048,256]{2,1,0:T(8,128)(2,1)S(1)} %get-tuple-element.29.probs_ref, bf16[4,2048,256]{2,1,0:T(8,128)(2,1)S(1)} %get-tuple-element.30.grads_ref, bf16[4,256,576]{2,1,0:T(8,128)(2,1)S(1)} %get-tuple-element.21.refs_8_.refs_17_.q_ref, ...), custom_call_target="tpu_custom_call" | custom-call | flops 2300000000 | bytes 7000000 | tf_op jit(solution)/shard_map/keep/pallas_call | solution.py:398
  48.0 0.3 add_convert_fusion.13
  48.2 0.4 collective-permute-start.17
  48.7 2.0 %collective-permute-start.18 = (bf16[288,512]{1,0:T(8,128)(2,1)S(1)}, bf16[288,512]{1,0:T(8,128)(2,1)S(1)}, u32[]{:S(2)}, u32[]{:S(2)}) collective-permute-start(bf16[288,512]{1,0:T(8,128)(2,1)S(1)} %pad_maximum_fusion.2), channel_id=1, source_target_pairs={{0,96},{8,104},{16,112},{24,120},{32,64},{40,72},{48,80},{56,88},{... | collective-permute-start | bytes 884744 | tf_op jit(solution)/shard_map/ppermute | solution.py:38
  50.7 1.9 %collective-permute-start.16 = (bf16[288,512]{1,0:T(8,128)(2,1)S(1)}, bf16[288,512]{1,0:T(8,128)(2,1)S(1)}, u32[]{:S(2)}, u32[]{:S(2)}) collective-permute-start(bf16[288,512]{1,0:T(8,128)(2,1)S(1)} %pad_maximum_fusion), channel_id=1, source_target_pairs={{0,64},{8,72},{16,80},{24,88},{32,96},{40,104},{48,112},{56,120},{... | collective-permute-start | bytes 884744 | tf_op jit(solution)/shard_map/ppermute | solution.py:38
  52.6 0.4 add_convert_fusion.3
  53.0 2.2 %collective-permute-start.28 = (bf16[2,2,32,1024]{3,2,1,0:T(8,128)(2,1)S(1)}, bf16[2,2,32,1024]{3,2,1,0:T(8,128)(2,1)S(1)}, u32[]{:S(2)}, u32[]{:S(2)}) collective-permute-start(bf16[2,2,32,1024]{3,2,1,0:T(8,128)(2,1)S(1)} %get-tuple-element.46), channel_id=1, source_target_pairs={{0,96},{8,104},{16,112},{24,120},{32,64},{40,72},{48,80},{56,88},{... | collective-permute-start | bytes 786440 | tf_op jit(solution)/shard_map/ppermute | solution.py:38
  55.3 3.0 %collective-permute-done.17 = bf16[288,512]{1,0:T(8,128)(2,1)S(1)} collective-permute-done((bf16[288,512]{1,0:T(8,128)(2,1)S(1)}, bf16[288,512]{1,0:T(8,128)(2,1)S(1)}, u32[]{:S(2)}, u32[]{:S(2)}) %collective-permute-start.17) | collective-permute-done | bytes 294944 | tf_op jit(solution)/shard_map/ppermute | solution.py:38
  58.2 1.7 %collective-permute-start.26 = (bf16[2,2,32,1024]{3,2,1,0:T(8,128)(2,1)S(1)}, bf16[2,2,32,1024]{3,2,1,0:T(8,128)(2,1)S(1)}, u32[]{:S(2)}, u32[]{:S(2)}) collective-permute-start(bf16[2,2,32,1024]{3,2,1,0:T(8,128)(2,1)S(1)} %get-tuple-element.48), channel_id=1, source_target_pairs={{0,64},{8,72},{16,80},{24,88},{32,96},{40,104},{48,112},{56,120},{... | collective-permute-start | bytes 786440 | tf_op jit(solution)/shard_map/ppermute | solution.py:38
  59.9 6.3 %collective-permute-done.18 = bf16[288,512]{1,0:T(8,128)(2,1)S(1)} collective-permute-done((bf16[288,512]{1,0:T(8,128)(2,1)S(1)}, bf16[288,512]{1,0:T(8,128)(2,1)S(1)}, u32[]{:S(2)}, u32[]{:S(2)}) %collective-permute-start.18) | collective-permute-done | bytes 294944 | tf_op jit(solution)/shard_map/ppermute | solution.py:38
  66.2 0.2 add_convert_fusion.7
  66.4 4.1 %collective-permute-start.21 = (bf16[144,512]{1,0:T(8,128)(2,1)S(1)}, bf16[144,512]{1,0:T(8,128)(2,1)S(1)}, u32[]{:S(2)}, u32[]{:S(2)}) collective-permute-start(bf16[144,512]{1,0:T(8,128)(2,1)S(1)} %get-tuple-element.38), channel_id=1, source_target_pairs={{0,17},{1,16},{2,19},{3,18},{4,21},{5,20},{6,23},{7,22},{8,25},{9,... | collective-permute-start | bytes 442376 | tf_op jit(solution)/shard_map/ppermute | solution.py:47
  70.5 4.6 %collective-permute-done.28 = bf16[2,2,32,1024]{3,2,1,0:T(8,128)(2,1)S(1)} collective-permute-done((bf16[2,2,32,1024]{3,2,1,0:T(8,128)(2,1)S(1)}, bf16[2,2,32,1024]{3,2,1,0:T(8,128)(2,1)S(1)}, u32[]{:S(2)}, u32[]{:S(2)}) %collective-permute-start.28) | collective-permute-done | bytes 262176 | tf_op jit(solution)/shard_map/ppermute | solution.py:38
  75.1 1.9 %collective-permute-start.19 = (bf16[144,512]{1,0:T(8,128)(2,1)S(1)}, bf16[144,512]{1,0:T(8,128)(2,1)S(1)}, u32[]{:S(2)}, u32[]{:S(2)}) collective-permute-start(bf16[144,512]{1,0:T(8,128)(2,1)S(1)} %get-tuple-element.37), channel_id=1, source_target_pairs={{0,1},{1,0},{2,3},{3,2},{4,5},{5,4},{6,7},{7,6},{8,9},{9,8},{10,11... | collective-permute-start | bytes 442376 | tf_op jit(solution)/shard_map/ppermute | solution.py:42
  77.0 0.1 fusion
  77.1 3.9 %collective-permute-start.29 = (bf16[2,32,1024]{2,1,0:T(8,128)(2,1)S(1)}, bf16[2,32,1024]{2,1,0:T(8,128)(2,1)S(1)}, u32[]{:S(2)}, u32[]{:S(2)}) collective-permute-start(bf16[2,32,1024]{2,1,0:T(8,128)(2,1)S(1)} %fusion), channel_id=1, source_target_pairs={{0,16},{8,24},{16,0},{24,8},{32,48},{40,56},{48,32},{56,40},{64,80... | collective-permute-start | bytes 393224 | tf_op jit(solution)/shard_map/ppermute | solution.py:38
  81.0 0.1 add_convert_fusion.4.mine_ref
  81.0 2.8 %collective-permute-start.24 = (bf16[144,512]{1,0:T(8,128)(2,1)S(1)}, bf16[144,512]{1,0:T(8,128)(2,1)S(1)}, u32[]{:S(2)}, u32[]{:S(2)}) collective-permute-start(bf16[144,512]{1,0:T(8,128)(2,1)S(1)} %add_convert_fusion.4.mine_ref), channel_id=1, source_target_pairs={{0,6},{1,7},{2,4},{3,5},{4,2},{5,3},{6,0},{7,1},{8,14},{9,15},{10,... | collective-permute-start | bytes 442376 | tf_op jit(solution)/shard_map/ppermute | solution.py:42
  83.9 0.2 collective-permute-start.23
  84.1 1.7 %collective-permute-start.22 = (bf16[144,512]{1,0:T(8,128)(2,1)S(1)}, bf16[144,512]{1,0:T(8,128)(2,1)S(1)}, u32[]{:S(2)}, u32[]{:S(2)}) collective-permute-start(bf16[144,512]{1,0:T(8,128)(2,1)S(1)} %add_convert_fusion.4.mine_ref), channel_id=1, source_target_pairs={{0,4},{1,5},{2,6},{3,7},{4,0},{5,1},{6,2},{7,3},{8,12},{9,13},{10,... | collective-permute-start | bytes 442376 | tf_op jit(solution)/shard_map/ppermute | solution.py:42
  85.8 0.8 convert_add_fusion
  86.6 1.7 %collective-permute-done.24.third_ref = bf16[144,512]{1,0:T(8,128)(2,1)S(1)} collective-permute-done((bf16[144,512]{1,0:T(8,128)(2,1)S(1)}, bf16[144,512]{1,0:T(8,128)(2,1)S(1)}, u32[]{:S(2)}, u32[]{:S(2)}) %collective-permute-start.24) | collective-permute-done | bytes 147488 | tf_op jit(solution)/shard_map/ppermute | solution.py:42
  88.3 2.0 %collective-permute-done.23.first_ref = bf16[144,512]{1,0:T(8,128)(2,1)S(1)} collective-permute-done((bf16[144,512]{1,0:T(8,128)(2,1)S(1)}, bf16[144,512]{1,0:T(8,128)(2,1)S(1)}, u32[]{:S(2)}, u32[]{:S(2)}) %collective-permute-start.23) | collective-permute-done | bytes 147488 | tf_op jit(solution)/shard_map/ppermute | solution.py:42
  90.2 1.5 %collective-permute-done.22.second_ref = bf16[144,512]{1,0:T(8,128)(2,1)S(1)} collective-permute-done((bf16[144,512]{1,0:T(8,128)(2,1)S(1)}, bf16[144,512]{1,0:T(8,128)(2,1)S(1)}, u32[]{:S(2)}, u32[]{:S(2)}) %collective-permute-start.22) | collective-permute-done | bytes 147488 | tf_op jit(solution)/shard_map/ppermute | solution.py:42
  91.8 0.8 final.1
  (34 shorter events, 0.1 us)
Async XLA Ops:
  1.6 10.2 %collective-permute-start.10 = (bf16[144,512]{1,0:T(8,128)(2,1)S(1)}, bf16[144,512]{1,0:T(8,128)(2,1)S(1)}, u32[]{:S(2)}, u32[]{:S(2)}) collective-permute-start(bf16[144,512]{1,0:T(8,128)(2,1)S(1)} %pack.1.refs_0_.refs_9_), channel_id=1, source_target_pairs={{0,96},{8,104},{16,112},{24,120},{32,64},{40,72},{48,80},{56,88},{... | collective-permute-start | bytes 442376 | tf_op jit(solution)/shard_map/ppermute | solution.py:38
  4.8 7.0 %collective-permute-start.9 = (bf16[144,512]{1,0:T(8,128)(2,1)S(1)}, bf16[144,512]{1,0:T(8,128)(2,1)S(1)}, u32[]{:S(2)}, u32[]{:S(2)}) collective-permute-start(bf16[144,512]{1,0:T(8,128)(2,1)S(1)} %pack.1.refs_0_.refs_9_), channel_id=1, source_target_pairs={{0,64},{8,72},{16,80},{24,88},{32,96},{40,104},{48,112},{56,120},{... | collective-permute-start | bytes 442376 | tf_op jit(solution)/shard_map/ppermute | solution.py:38
  5.4 7.2 %collective-permute-start = (bf16[144,512]{1,0:T(8,128)(2,1)S(1)}, bf16[144,512]{1,0:T(8,128)(2,1)S(1)}, u32[]{:S(2)}, u32[]{:S(2)}) collective-permute-start(bf16[144,512]{1,0:T(8,128)(2,1)S(1)} %pack.1.refs_0_.refs_9_), channel_id=1, source_target_pairs={{0,16},{8,24},{16,0},{24,8},{32,48},{40,56},{48,32},{56,40},{64,80... | collective-permute-start | bytes 442376 | tf_op jit(solution)/shard_map/ppermute | solution.py:38
  9.3 6.0 %collective-permute-start.11 = (bf16[144,512]{1,0:T(8,128)(2,1)S(1)}, bf16[144,512]{1,0:T(8,128)(2,1)S(1)}, u32[]{:S(2)}, u32[]{:S(2)}) collective-permute-start(bf16[144,512]{1,0:T(8,128)(2,1)S(1)} %pack.1.refs_0_.refs_9_), channel_id=1, source_target_pairs={{0,8},{8,0},{16,24},{24,16},{32,40},{40,32},{48,56},{56,48},{64,72... | collective-permute-start | bytes 442376 | tf_op jit(solution)/shard_map/ppermute | solution.py:38
  9.3 6.3 %collective-permute-start.8 = (bf16[144,512]{1,0:T(8,128)(2,1)S(1)}, bf16[144,512]{1,0:T(8,128)(2,1)S(1)}, u32[]{:S(2)}, u32[]{:S(2)}) collective-permute-start(bf16[144,512]{1,0:T(8,128)(2,1)S(1)} %pack.1.refs_0_.refs_9_), channel_id=1, source_target_pairs={{0,32},{8,40},{16,48},{24,56},{32,0},{40,8},{48,16},{56,24},{64,96... | collective-permute-start | bytes 442376 | tf_op jit(solution)/shard_map/ppermute | solution.py:38
  11.8 4.9 %collective-permute-start.14 = (bf16[144,512]{1,0:T(8,128)(2,1)S(1)}, bf16[144,512]{1,0:T(8,128)(2,1)S(1)}, u32[]{:S(2)}, u32[]{:S(2)}) collective-permute-start(bf16[144,512]{1,0:T(8,128)(2,1)S(1)} %collective-permute-done.10.refs_3_.refs_12_), channel_id=1, source_target_pairs={{0,8},{8,0},{16,24},{24,16},{32,40},{40,32},{48,56},{56,48},{64,72... | collective-permute-start | bytes 442376 | tf_op jit(solution)/shard_map/ppermute | solution.py:38
  11.8 8.2 %collective-permute-start.13 = (bf16[144,512]{1,0:T(8,128)(2,1)S(1)}, bf16[144,512]{1,0:T(8,128)(2,1)S(1)}, u32[]{:S(2)}, u32[]{:S(2)}) collective-permute-start(bf16[144,512]{1,0:T(8,128)(2,1)S(1)} %collective-permute-done.9.refs_2_.refs_11_), channel_id=1, source_target_pairs={{0,8},{8,0},{16,24},{24,16},{32,40},{40,32},{48,56},{56,48},{64,72... | collective-permute-start | bytes 442376 | tf_op jit(solution)/shard_map/ppermute | solution.py:38
  12.6 9.2 %collective-permute-start.3 = (bf16[144,512]{1,0:T(8,128)(2,1)S(1)}, bf16[144,512]{1,0:T(8,128)(2,1)S(1)}, u32[]{:S(2)}, u32[]{:S(2)}) collective-permute-start(bf16[144,512]{1,0:T(8,128)(2,1)S(1)} %collective-permute-done.refs_1_), channel_id=1, source_target_pairs={{0,96},{8,104},{16,112},{24,120},{32,64},{40,72},{48,80},{56,88},{... | collective-permute-start | bytes 442376 | tf_op jit(solution)/shard_map/ppermute | solution.py:38
  15.2 8.2 %collective-permute-start.2 = (bf16[144,512]{1,0:T(8,128)(2,1)S(1)}, bf16[144,512]{1,0:T(8,128)(2,1)S(1)}, u32[]{:S(2)}, u32[]{:S(2)}) collective-permute-start(bf16[144,512]{1,0:T(8,128)(2,1)S(1)} %collective-permute-done.refs_1_), channel_id=1, source_target_pairs={{0,64},{8,72},{16,80},{24,88},{32,96},{40,104},{48,112},{56,120},{... | collective-permute-start | bytes 442376 | tf_op jit(solution)/shard_map/ppermute | solution.py:38
  15.5 7.9 %collective-permute-start.1 = (bf16[144,512]{1,0:T(8,128)(2,1)S(1)}, bf16[144,512]{1,0:T(8,128)(2,1)S(1)}, u32[]{:S(2)}, u32[]{:S(2)}) collective-permute-start(bf16[144,512]{1,0:T(8,128)(2,1)S(1)} %collective-permute-done.refs_1_), channel_id=1, source_target_pairs={{0,32},{8,40},{16,48},{24,56},{32,0},{40,8},{48,16},{56,24},{64,96... | collective-permute-start | bytes 442376 | tf_op jit(solution)/shard_map/ppermute | solution.py:38
  16.7 7.3 %collective-permute-start.12 = (bf16[144,512]{1,0:T(8,128)(2,1)S(1)}, bf16[144,512]{1,0:T(8,128)(2,1)S(1)}, u32[]{:S(2)}, u32[]{:S(2)}) collective-permute-start(bf16[144,512]{1,0:T(8,128)(2,1)S(1)} %collective-permute-done.8.refs_1_.refs_10_), channel_id=1, source_target_pairs={{0,8},{8,0},{16,24},{24,16},{32,40},{40,32},{48,56},{56,48},{64,72... | collective-permute-start | bytes 442376 | tf_op jit(solution)/shard_map/ppermute | solution.py:38
  19.9 8.3 %collective-permute-start.4 = (bf16[144,512]{1,0:T(8,128)(2,1)S(1)}, bf16[144,512]{1,0:T(8,128)(2,1)S(1)}, u32[]{:S(2)}, u32[]{:S(2)}) collective-permute-start(bf16[144,512]{1,0:T(8,128)(2,1)S(1)} %collective-permute-done.refs_1_), channel_id=1, source_target_pairs={{0,8},{8,0},{16,24},{24,16},{32,40},{40,32},{48,56},{56,48},{64,72... | collective-permute-start | bytes 442376 | tf_op jit(solution)/shard_map/ppermute | solution.py:38
  21.8 6.5 %collective-permute-start.7 = (bf16[144,512]{1,0:T(8,128)(2,1)S(1)}, bf16[144,512]{1,0:T(8,128)(2,1)S(1)}, u32[]{:S(2)}, u32[]{:S(2)}) collective-permute-start(bf16[144,512]{1,0:T(8,128)(2,1)S(1)} %collective-permute-done.3.refs_4_), channel_id=1, source_target_pairs={{0,8},{8,0},{16,24},{24,16},{32,40},{40,32},{48,56},{56,48},{64,72... | collective-permute-start | bytes 442376 | tf_op jit(solution)/shard_map/ppermute | solution.py:38
  23.5 4.8 %collective-permute-start.6 = (bf16[144,512]{1,0:T(8,128)(2,1)S(1)}, bf16[144,512]{1,0:T(8,128)(2,1)S(1)}, u32[]{:S(2)}, u32[]{:S(2)}) collective-permute-start(bf16[144,512]{1,0:T(8,128)(2,1)S(1)} %collective-permute-done.2.refs_3_), channel_id=1, source_target_pairs={{0,8},{8,0},{16,24},{24,16},{32,40},{40,32},{48,56},{56,48},{64,72... | collective-permute-start | bytes 442376 | tf_op jit(solution)/shard_map/ppermute | solution.py:38
  23.5 4.9 %collective-permute-start.5 = (bf16[144,512]{1,0:T(8,128)(2,1)S(1)}, bf16[144,512]{1,0:T(8,128)(2,1)S(1)}, u32[]{:S(2)}, u32[]{:S(2)}) collective-permute-start(bf16[144,512]{1,0:T(8,128)(2,1)S(1)} %collective-permute-done.1.refs_2_), channel_id=1, source_target_pairs={{0,8},{8,0},{16,24},{24,16},{32,40},{40,32},{48,56},{56,48},{64,72... | collective-permute-start | bytes 442376 | tf_op jit(solution)/shard_map/ppermute | solution.py:38
  28.3 8.6 %copy-start = (bf16[512,1024]{1,0:T(8,128)(2,1)S(1)}, bf16[512,1024]{1,0:T(8,128)(2,1)}, u32[]{:S(2)}) copy-start(bf16[512,1024]{1,0:T(8,128)(2,1)} %up_key_ref.3) | copy-start | bytes 3145732
  28.3 8.5 %copy-start.1 = (bf16[128,1536]{1,0:T(8,128)(2,1)S(1)}, bf16[128,1536]{1,0:T(8,128)(2,1)}, u32[]{:S(2)}) copy-start(bf16[128,1536]{1,0:T(8,128)(2,1)} %query_ref.3) | copy-start | bytes 1179652
  28.4 8.5 %copy-start.2 = (bf16[128,1024]{1,0:T(8,128)(2,1)S(1)}, bf16[128,1024]{1,0:T(8,128)(2,1)}, u32[]{:S(2)}) copy-start(bf16[128,1024]{1,0:T(8,128)(2,1)} %out_grad_ref.3) | copy-start | bytes 786436
  36.8 11.2 %collective-permute-start.15 = (bf16[1152,512]{1,0:T(8,128)(2,1)S(1)}, bf16[1152,512]{1,0:T(8,128)(2,1)S(1)}, u32[]{:S(2)}, u32[]{:S(2)}) collective-permute-start(bf16[1152,512]{1,0:T(8,128)(2,1)S(1)} %get-tuple-element.32), channel_id=1, source_target_pairs={{0,8},{8,0},{16,24},{24,16},{32,40},{40,32},{48,56},{56,48},{64,72... | collective-permute-start | bytes 3538952 | tf_op jit(solution)/shard_map/ppermute | solution.py:38
  44.6 8.0 %collective-permute-start.25 = (bf16[8,2,32,1024]{3,2,1,0:T(8,128)(2,1)S(1)}, bf16[8,2,32,1024]{3,2,1,0:T(8,128)(2,1)S(1)}, u32[]{:S(2)}, u32[]{:S(2)}) collective-permute-start(bf16[8,2,32,1024]{3,2,1,0:T(8,128)(2,1)S(1)} %get-tuple-element.36), channel_id=1, source_target_pairs={{0,8},{8,0},{16,24},{24,16},{32,40},{40,32},{48,56},{56,48},{64,72... | collective-permute-start | bytes 3145736 | tf_op jit(solution)/shard_map/ppermute | solution.py:38
  48.2 10.0 %collective-permute-start.17 = (bf16[288,512]{1,0:T(8,128)(2,1)S(1)}, bf16[288,512]{1,0:T(8,128)(2,1)S(1)}, u32[]{:S(2)}, u32[]{:S(2)}) collective-permute-start(bf16[288,512]{1,0:T(8,128)(2,1)S(1)} %pad_maximum_fusion.1), channel_id=1, source_target_pairs={{0,32},{8,40},{16,48},{24,56},{32,0},{40,8},{48,16},{56,24},{64,96... | collective-permute-start | bytes 884744 | tf_op jit(solution)/shard_map/ppermute | solution.py:38
  48.7 17.5 %collective-permute-start.18 = (bf16[288,512]{1,0:T(8,128)(2,1)S(1)}, bf16[288,512]{1,0:T(8,128)(2,1)S(1)}, u32[]{:S(2)}, u32[]{:S(2)}) collective-permute-start(bf16[288,512]{1,0:T(8,128)(2,1)S(1)} %pad_maximum_fusion.2), channel_id=1, source_target_pairs={{0,96},{8,104},{16,112},{24,120},{32,64},{40,72},{48,80},{56,88},{... | collective-permute-start | bytes 884744 | tf_op jit(solution)/shard_map/ppermute | solution.py:38
  50.7 15.5 %collective-permute-start.16 = (bf16[288,512]{1,0:T(8,128)(2,1)S(1)}, bf16[288,512]{1,0:T(8,128)(2,1)S(1)}, u32[]{:S(2)}, u32[]{:S(2)}) collective-permute-start(bf16[288,512]{1,0:T(8,128)(2,1)S(1)} %pad_maximum_fusion), channel_id=1, source_target_pairs={{0,64},{8,72},{16,80},{24,88},{32,96},{40,104},{48,112},{56,120},{... | collective-permute-start | bytes 884744 | tf_op jit(solution)/shard_map/ppermute | solution.py:38
  53.0 22.0 %collective-permute-start.28 = (bf16[2,2,32,1024]{3,2,1,0:T(8,128)(2,1)S(1)}, bf16[2,2,32,1024]{3,2,1,0:T(8,128)(2,1)S(1)}, u32[]{:S(2)}, u32[]{:S(2)}) collective-permute-start(bf16[2,2,32,1024]{3,2,1,0:T(8,128)(2,1)S(1)} %get-tuple-element.46), channel_id=1, source_target_pairs={{0,96},{8,104},{16,112},{24,120},{32,64},{40,72},{48,80},{56,88},{... | collective-permute-start | bytes 786440 | tf_op jit(solution)/shard_map/ppermute | solution.py:38
  55.2 21.7 %collective-permute-start.27 = (bf16[2,2,32,1024]{3,2,1,0:T(8,128)(2,1)S(1)}, bf16[2,2,32,1024]{3,2,1,0:T(8,128)(2,1)S(1)}, u32[]{:S(2)}, u32[]{:S(2)}) collective-permute-start(bf16[2,2,32,1024]{3,2,1,0:T(8,128)(2,1)S(1)} %get-tuple-element.47), channel_id=1, source_target_pairs={{0,32},{8,40},{16,48},{24,56},{32,0},{40,8},{48,16},{56,24},{64,96... | collective-permute-start | bytes 786440 | tf_op jit(solution)/shard_map/ppermute | solution.py:38
  58.2 18.8 %collective-permute-start.26 = (bf16[2,2,32,1024]{3,2,1,0:T(8,128)(2,1)S(1)}, bf16[2,2,32,1024]{3,2,1,0:T(8,128)(2,1)S(1)}, u32[]{:S(2)}, u32[]{:S(2)}) collective-permute-start(bf16[2,2,32,1024]{3,2,1,0:T(8,128)(2,1)S(1)} %get-tuple-element.48), channel_id=1, source_target_pairs={{0,64},{8,72},{16,80},{24,88},{32,96},{40,104},{48,112},{56,120},{... | collective-permute-start | bytes 786440 | tf_op jit(solution)/shard_map/ppermute | solution.py:38
  66.4 14.6 %collective-permute-start.21 = (bf16[144,512]{1,0:T(8,128)(2,1)S(1)}, bf16[144,512]{1,0:T(8,128)(2,1)S(1)}, u32[]{:S(2)}, u32[]{:S(2)}) collective-permute-start(bf16[144,512]{1,0:T(8,128)(2,1)S(1)} %get-tuple-element.38), channel_id=1, source_target_pairs={{0,17},{1,16},{2,19},{3,18},{4,21},{5,20},{6,23},{7,22},{8,25},{9,... | collective-permute-start | bytes 442376 | tf_op jit(solution)/shard_map/ppermute | solution.py:47
  70.5 10.5 %collective-permute-start.20 = (bf16[144,512]{1,0:T(8,128)(2,1)S(1)}, bf16[144,512]{1,0:T(8,128)(2,1)S(1)}, u32[]{:S(2)}, u32[]{:S(2)}) collective-permute-start(bf16[144,512]{1,0:T(8,128)(2,1)S(1)} %get-tuple-element.38), channel_id=1, source_target_pairs={{0,16},{8,24},{16,0},{24,8},{32,48},{40,56},{48,32},{56,40},{64,80... | collective-permute-start | bytes 442376 | tf_op jit(solution)/shard_map/ppermute | solution.py:38
  75.1 5.9 %collective-permute-start.19 = (bf16[144,512]{1,0:T(8,128)(2,1)S(1)}, bf16[144,512]{1,0:T(8,128)(2,1)S(1)}, u32[]{:S(2)}, u32[]{:S(2)}) collective-permute-start(bf16[144,512]{1,0:T(8,128)(2,1)S(1)} %get-tuple-element.37), channel_id=1, source_target_pairs={{0,1},{1,0},{2,3},{3,2},{4,5},{5,4},{6,7},{7,6},{8,9},{9,8},{10,11... | collective-permute-start | bytes 442376 | tf_op jit(solution)/shard_map/ppermute | solution.py:42
  77.1 8.8 %collective-permute-start.29 = (bf16[2,32,1024]{2,1,0:T(8,128)(2,1)S(1)}, bf16[2,32,1024]{2,1,0:T(8,128)(2,1)S(1)}, u32[]{:S(2)}, u32[]{:S(2)}) collective-permute-start(bf16[2,32,1024]{2,1,0:T(8,128)(2,1)S(1)} %fusion), channel_id=1, source_target_pairs={{0,16},{8,24},{16,0},{24,8},{32,48},{40,56},{48,32},{56,40},{64,80... | collective-permute-start | bytes 393224 | tf_op jit(solution)/shard_map/ppermute | solution.py:38
  81.0 7.2 %collective-permute-start.24 = (bf16[144,512]{1,0:T(8,128)(2,1)S(1)}, bf16[144,512]{1,0:T(8,128)(2,1)S(1)}, u32[]{:S(2)}, u32[]{:S(2)}) collective-permute-start(bf16[144,512]{1,0:T(8,128)(2,1)S(1)} %add_convert_fusion.4.mine_ref), channel_id=1, source_target_pairs={{0,6},{1,7},{2,4},{3,5},{4,2},{5,3},{6,0},{7,1},{8,14},{9,15},{10,... | collective-permute-start | bytes 442376 | tf_op jit(solution)/shard_map/ppermute | solution.py:42
  83.9 6.4 %collective-permute-start.23 = (bf16[144,512]{1,0:T(8,128)(2,1)S(1)}, bf16[144,512]{1,0:T(8,128)(2,1)S(1)}, u32[]{:S(2)}, u32[]{:S(2)}) collective-permute-start(bf16[144,512]{1,0:T(8,128)(2,1)S(1)} %add_convert_fusion.4.mine_ref), channel_id=1, source_target_pairs={{0,2},{1,3},{2,0},{3,1},{4,6},{5,7},{6,4},{7,5},{8,10},{9,11},{10,... | collective-permute-start | bytes 442376 | tf_op jit(solution)/shard_map/ppermute | solution.py:42
  84.1 7.6 %collective-permute-start.22 = (bf16[144,512]{1,0:T(8,128)(2,1)S(1)}, bf16[144,512]{1,0:T(8,128)(2,1)S(1)}, u32[]{:S(2)}, u32[]{:S(2)}) collective-permute-start(bf16[144,512]{1,0:T(8,128)(2,1)S(1)} %add_convert_fusion.4.mine_ref), channel_id=1, source_target_pairs={{0,4},{1,5},{2,6},{3,7},{4,0},{5,1},{6,2},{7,3},{8,12},{9,13},{10,... | collective-permute-start | bytes 442376 | tf_op jit(solution)/shard_map/ppermute | solution.py:42
